TPU v7x, 32 devices: a whole 2x2x4 slice. The times are simulated.
32 devices in a mesh: dom: 8 (over z, y), col: 4 (over x, core).
Axes of the slice: x: 2, y: 2, z: 4, core: 2. Of those that a mesh axis runs over, the one named last changes fastest.
Arguments:
- right_side: float32 [3, 64, 32768], P(None, 'col', 'dom'), may hold values from -90 to 90, as said below
- stiffness: float32 [64, 32768], P(None, 'dom'), may hold values from -1 to 9, as said below
- contact: float32 [64, 32768], P(None, 'dom'), may hold values from -1 to 60, as said below
- pair_local: int32 [512], P('dom'), may hold values from 0 to 63
- pair_partner: int32 [512], P('dom'), may hold values from 0 to 71, as said below
- pair_count: int32 [8], P('dom'), may hold values from 16 to 64, as said below
- objective_weight: float32 [3, 32768], P(None, 'dom'), may hold values from -20 to 20
Outputs:
- solution_field: float32 [3, 64, 32768], P(None, 'col', 'dom')
- residual: float32 [3, 64, 32768], P(None, 'col', 'dom')
- param_step: float32 [64], P('col')
Inputs may be any that keep to these rules, and one draw needn't show every extreme that they name: `right_side`: varies from node to node. `stiffness`: every patch's block is symmetric and diagonally dominant with a positive diagonal. `contact`: every slot's block is symmetric and diagonally dominant with a nonnegative diagonal. `pair_partner`: A value below 64 names another patch of the slot's own partition; a value 64 + q names patch q of the next partition, with q below 8; slots of the last partition name only their own partition. `pair_count`: some partition has all 64 slots live.
All inputs are finite; a program needn't handle non-finite values.
Results may differ from a plain program's by a relative error of at most 0.0003.
Values sent between devices are 32-bit elements; how exact they have to be, the bound alone decides.
No kernel may reach another device: no remote copies, remote signals or barrier semaphores. Data moves between devices by JAX's collectives and lax.ppermute only.
A program may use at most 64 MiB of HBM per device.

v0:
```python
import jax
import jax.numpy as jnp
from jax import lax
from jax.sharding import PartitionSpec as P

PN = 64
NB = 8
COLS = 64
ITERS = 2


def shifted(value, axis, by):
    count = lax.axis_size(axis)
    pairs = [(i, i + by) for i in range(count) if 0 <= i + by < count]
    return lax.ppermute(value, axis, pairs)


def column_sums(left, right):
    return jnp.sum(left * right, axis=(0, 2))


def shards(right_side, stiffness, contact, pair_local, pair_partner, pair_count, objective_weight):
    components, columns, node_count = right_side.shape
    patches = node_count // PN
    pair_total = pair_local.shape[0]
    row_count = components * columns
    stiff_blocks = stiffness.reshape(PN, patches, PN)
    pair_blocks = contact.reshape(PN, pair_total, PN)
    live_mask = (jnp.arange(pair_total, dtype=jnp.int32) < pair_count[0]).astype(jnp.float32)
    joined_width = patches + NB
    slot_ids = jnp.arange(joined_width, dtype=jnp.int32)
    incidence = (pair_local[:, None] == slot_ids[None, :]).astype(jnp.float32) - (
        pair_partner[:, None] == slot_ids[None, :]
    ).astype(jnp.float32)

    def squares(vector):
        return lax.psum(column_sums(vector, vector), "dom")

    solution_field = jnp.zeros_like(right_side)
    residual = right_side
    direction = right_side
    norm_now = squares(residual)
    for iteration in range(ITERS):
        field_rows = direction.reshape(row_count, patches, PN)
        far_side = shifted(direction[:, :, : NB * PN], "dom", -1)
        far_rows = far_side.reshape(row_count, NB, PN)
        joined = jnp.concatenate([field_rows, far_rows], axis=1)
        gap_rows = (
            jnp.take(field_rows, pair_local, axis=1) - jnp.take(joined, pair_partner, axis=1)
        ) * live_mask[None, :, None]
        forces = jnp.einsum("cki,ikj->ckj", gap_rows, pair_blocks, precision=lax.Precision.HIGHEST)
        elastic = jnp.einsum(
            "cpi,ipj->cpj", field_rows, stiff_blocks, precision=lax.Precision.HIGHEST
        )
        spread = jnp.einsum("ckj,kw->cwj", forces, incidence, precision=lax.Precision.HIGHEST)
        own_spread = spread[:, :patches]
        received = shifted(spread[:, patches:].reshape(components, columns, NB * PN), "dom", 1)
        applied = (elastic + own_spread).reshape(components, columns, node_count)
        applied = applied.at[:, :, : NB * PN].add(received)
        step_size = norm_now / lax.psum(column_sums(direction, applied), "dom")
        solution_field = solution_field + step_size[None, :, None] * direction
        residual = residual - step_size[None, :, None] * applied
        norm_next = squares(residual)
        direction = residual + (norm_next / norm_now)[None, :, None] * direction
        norm_now = norm_next
    partial_gradient = jnp.sum(objective_weight[:, None, :] * solution_field, axis=(0, 2))
    gradient = lax.psum(partial_gradient, "dom")
    square_total = lax.psum(jnp.sum(gradient * gradient), "col")
    param_step = gradient / jnp.sqrt(square_total / COLS + 1e-06)
    return (solution_field, residual, param_step)


def solution(mesh):
    placed = (
        P(None, "col", "dom"),
        P(None, "dom"),
        P(None, "dom"),
        P("dom"),
        P("dom"),
        P("dom"),
        P(None, "dom"),
    )
    return jax.shard_map(
        shards,
        mesh=mesh,
        in_specs=placed,
        out_specs=(P(None, "col", "dom"), P(None, "col", "dom"), P("col")),
        check_vma=False,
    )
```

profile of v0, /device:TPU:0, one launch (start us, length us, event | category | flops | bytes accessed | tf_op | source)
XLA Modules:
  0.0 180.9 jit_solution(2643704245959054977)
XLA Ops:
  2.9 1.8 reshape.118
  4.7 2.1 %copy.25 = f32[48,64,64]{2,0,1:T(8,128)} copy(f32[48,64,64]{2,1,0:T(8,128)S(1)} %reshape.118) | data formatting | bytes 1572864 | tf_op jit(solution)/shard_map/reshape | solution.py:44
  6.8 2.1 %reshape.120 = f32[64,64,64]{2,1,0:T(8,128)} reshape(f32[64,4096]{1,0:T(8,128)S(1)} %copy-done.7) | data formatting | bytes 2097152 | tf_op jit(solution)/shard_map/reshape | solution.py:28
  9.6 2.0 %reshape.117 = f32[64,64,64]{2,1,0:T(8,128)S(1)} reshape(f32[64,4096]{1,0:T(8,128)} %param.16) | data formatting | bytes 2097152 | tf_op jit(solution)/shard_map/reshape | solution.py:27
  11.6 4.1 %gather_fusion = f32[64,48,64]{2,1,0:T(8,128)} fusion(f32[48,64,64]{2,0,1:T(8,128)} %copy.25, s32[1024]{0:T(1024)S(1)} %pad_clamp_fusion.1), kind=kCustom, calls=%fused_computation.clone | custom fusion | bytes 1573120 | tf_op jit(solution)/shard_map/jit(_take)/gather | solution.py:49
  15.8 2.8 %pad_maximum_fusion = f32[48,72,64]{2,0,1:T(8,128)} fusion(f32[48,8,64]{2,0,1:T(8,128)S(1)} %copy.28, f32[48,64,64]{2,0,1:T(8,128)} %copy.25), kind=kLoop, calls=%fused_computation.12 | loop fusion | flops 221184 | bytes 1769472 | tf_op jit(solution)/shard_map/concatenate | solution.py:47
  18.6 3.3 %gather_fusion.1 = f32[64,48,64]{2,1,0:T(8,128)} fusion(f32[48,72,64]{2,0,1:T(8,128)} %pad_maximum_fusion, s32[1024]{0:T(1024)S(1)} %pad_clamp_fusion), kind=kCustom, calls=%fused_computation.1.clone | custom fusion | bytes 1573120 | tf_op jit(solution)/shard_map/jit(_take)/gather | solution.py:49
  21.8 7.0 %fusion.18 = f32[48,64,64]{2,0,1:T(8,128)} fusion(f32[64,64,64]{2,1,0:T(8,128)} %reshape.120, f32[64,48,64]{2,1,0:T(8,128)} %gather_fusion.1, f32[64,48,64]{2,1,0:T(8,128)} %gather_fusion, f32[64]{0:T(128)S(1)} %compare_convert_fusion, pred[64]{0:T(512)(128)(4,1)S(1)} %get-tuple-element.36, pred[64]{0:T(512)(128)(4,1)S(1)} %get-tuple-element.37), kind=kOutput, calls=%fused_computation.26 | convolution fusion | flops 151781376 | bytes 3408256 | tf_op jit(solution)/shard_map/cki,ikj->ckj/dot_general | solution.py:51
  28.9 3.2 %copy.30 = f32[48,64,64]{1,2,0:T(8,128)} copy(f32[48,64,64]{2,0,1:T(8,128)} %fusion.18) | data formatting | bytes 1572864 | tf_op jit(solution)/shard_map/cki,ikj->ckj/transpose | solution.py:51
  32.1 4.0 %fusion.43 = f32[72,3072]{0,1} fusion(f32[64,3072]{0,1:T(8,128)} %bitcast.54, s32[64]{0:T(128)S(1)} %copy-done.9, s32[64]{0:T(128)S(1)} %copy-done.10), kind=kOutput, calls=%fused_computation.52 | convolution fusion | flops 169892352 | bytes 1671680
  36.1 2.7 %copy.31 = f32[72,48,64]{2,1,0:T(8,128)} copy(f32[72,48,64]{0,2,1:T(8,128)} %bitcast.55) | data formatting | bytes 1769472 | tf_op jit(solution)/shard_map/ckj,kw->cwj/dot_general | solution.py:55
  40.0 5.7 %collective-permute-start.1 = (f32[3,16,512]{2,1,0:T(8,128)S(1)}, f32[3,16,512]{2,1,0:T(8,128)S(1)}, u32[]{:S(2)}, u32[]{:S(2)}) collective-permute-start(f32[3,16,512]{2,1,0:T(8,128)S(1)} %reshape.122), channel_id=1, source_target_pairs={{0,4},{4,8},{8,12},{12,16},{16,20},{20,24},{24,28},{1,5},{5,9},{9,... | collective-permute-start | bytes 294920 | tf_op jit(solution)/shard_map/ppermute | solution.py:15
  45.7 6.0 %slice_add_fusion.1 = f32[48,64,64]{2,0,1:T(8,128)S(1)} fusion(f32[48,72,64]{2,0,1:T(8,128)} %bitcast.53, f32[64,64,64]{2,1,0:T(8,128)S(1)} %reshape.117, f32[48,64,64]{2,1,0:T(8,128)} %copy-done.2), kind=kOutput, calls=%fused_computation.15 | convolution fusion | flops 151191552 | bytes 3407872 | tf_op jit(solution)/shard_map/cpi,ipj->cpj/dot_general | solution.py:52
  53.6 20.3 %all-reduce = (f32[16]{0:T(128)S(1)}, f32[16]{0:T(128)S(1)}) all-reduce(f32[16]{0:T(128)S(1)} %get-tuple-element.30, f32[16]{0:T(128)S(1)} %get-tuple-element.29), channel_id=1, replica_groups=mesh['dom'=8,'col'=4] {'dom'}, use_global_device_ids=true, to_apply=%region_1.0 | all-reduce | flops 32 | bytes 256 | tf_op jit(solution)/shard_map/psum | solution.py:37
  74.2 17.1 %psum.44 = f32[16]{0:T(128)S(1)} all-reduce(f32[16]{0:T(128)S(1)} %multiply_reduce_fusion.2), channel_id=1, replica_groups=mesh['dom'=8,'col'=4] {'dom'}, use_global_device_ids=true, to_apply=%region_5.8 | all-reduce | flops 16 | bytes 128 | tf_op jit(solution)/shard_map/psum | solution.py:37
  91.5 1.5 collective-permute-start.2
  93.1 1.8 reshape.123
  94.9 2.3 %copy.34 = f32[48,64,64]{2,0,1:T(8,128)S(1)} copy(f32[48,64,64]{2,1,0:T(8,128)} %reshape.123) | data formatting | bytes 1572864 | tf_op jit(solution)/shard_map/reshape | solution.py:44
  97.2 1.8 %gather_fusion.2 = f32[64,48,64]{2,1,0:T(8,128)} fusion(f32[48,64,64]{2,0,1:T(8,128)S(1)} %copy.34, s32[1024]{0:T(1024)S(1)} %pad_clamp_fusion.1), kind=kCustom, calls=%fused_computation.2.clone | custom fusion | bytes 1573120 | tf_op jit(solution)/shard_map/jit(_take)/gather | solution.py:49
  100.5 3.5 %gather_fusion.3 = f32[64,48,64]{2,1,0:T(8,128)} fusion(f32[48,72,64]{2,0,1:T(8,128)} %pad_maximum_fusion.1, s32[1024]{0:T(1024)S(1)} %pad_clamp_fusion), kind=kCustom, calls=%fused_computation.3.clone | custom fusion | bytes 1573120 | tf_op jit(solution)/shard_map/jit(_take)/gather | solution.py:49
  104.0 6.6 %fusion.23 = f32[48,64,64]{2,0,1:T(8,128)} fusion(f32[64,64,64]{2,1,0:T(8,128)} %reshape.120, f32[64,48,64]{2,1,0:T(8,128)} %gather_fusion.3, f32[64,48,64]{2,1,0:T(8,128)S(1)} %copy-done.6, f32[64]{0:T(128)S(1)} %compare_convert_fusion, pred[64]{0:T(512)(128)(4,1)S(1)} %get-tuple-element.36, pred[64]{0:T(512)(128)(4,1)S(1)} %get-tuple-element.37), kind=kOutput, calls=%fused_computation.27 | convolution fusion | flops 151781376 | bytes 3408256 | tf_op jit(solution)/shard_map/cki,ikj->ckj/dot_general | solution.py:51
  110.5 2.0 %copy.40 = f32[48,64,64]{1,2,0:T(8,128)S(1)} copy(f32[48,64,64]{2,0,1:T(8,128)} %fusion.23) | data formatting | bytes 1572864 | tf_op jit(solution)/shard_map/cki,ikj->ckj/transpose | solution.py:51
  112.5 2.6 %fusion.42 = f32[72,3072]{0,1} fusion(f32[64,3072]{0,1:T(8,128)S(1)} %bitcast.56, s32[64]{0:T(128)S(1)} %copy-done.9, s32[64]{0:T(128)S(1)} %copy-done.10), kind=kOutput, calls=%fused_computation.51 | convolution fusion | flops 169892352 | bytes 1671680
  115.1 2.9 %copy.41 = f32[72,48,64]{2,1,0:T(8,128)} copy(f32[72,48,64]{0,2,1:T(8,128)} %bitcast.57) | data formatting | bytes 1769472 | tf_op jit(solution)/shard_map/ckj,kw->cwj/dot_general | solution.py:55
  119.1 4.9 %collective-permute-start.3 = (f32[3,16,512]{2,1,0:T(8,128)S(1)}, f32[3,16,512]{2,1,0:T(8,128)S(1)}, u32[]{:S(2)}, u32[]{:S(2)}) collective-permute-start(f32[3,16,512]{2,1,0:T(8,128)S(1)} %reshape.126), channel_id=1, source_target_pairs={{0,4},{4,8},{8,12},{12,16},{16,20},{20,24},{24,28},{1,5},{5,9},{9,... | collective-permute-start | bytes 294920 | tf_op jit(solution)/shard_map/ppermute | solution.py:15
  124.0 6.2 %slice_add_fusion = f32[48,64,64]{2,0,1:T(8,128)S(1)} fusion(f32[48,72,64]{2,0,1:T(8,128)} %bitcast.51, f32[64,64,64]{2,1,0:T(8,128)} %copy-done.1, f32[48,64,64]{2,1,0:T(8,128)S(1)} %copy-done.3), kind=kOutput, calls=%fused_computation.14 | convolution fusion | flops 151191552 | bytes 3407872 | tf_op jit(solution)/shard_map/cpi,ipj->cpj/dot_general | solution.py:52
  130.2 1.6 copy.42
  131.8 2.0 %reshape.125 = f32[3,16,4096]{2,1,0:T(8,128)S(1)} reshape(f32[48,64,64]{2,1,0:T(8,128)} %copy.42) | data formatting | bytes 1572864 | tf_op jit(solution)/shard_map/reshape | solution.py:58
  134.1 20.0 %psum.45 = f32[16]{0:T(128)S(1)} all-reduce(f32[16]{0:T(128)S(1)} %multiply_reduce_fusion.1), channel_id=1, replica_groups=mesh['dom'=8,'col'=4] {'dom'}, use_global_device_ids=true, to_apply=%region_7.10 | all-reduce | flops 16 | bytes 128 | tf_op jit(solution)/shard_map/psum | solution.py:60
  154.2 1.6 multiply_reduce_fusion
  155.7 17.1 %psum.46 = f32[16]{0:T(128)S(1)} all-reduce(f32[16]{0:T(128)S(1)} %get-tuple-element.33), channel_id=1, replica_groups=mesh['dom'=8,'col'=4] {'dom'}, use_global_device_ids=true, to_apply=%region_9.12 | all-reduce | flops 16 | bytes 128 | tf_op jit(solution)/shard_map/psum | solution.py:67
  173.5 6.3 %psum.47 = f32[]{:T(128)} all-reduce(f32[]{:T(128)} %multiply_reduce_fusion.5), channel_id=1, replica_groups=mesh['dom'=8,'col'=4] {'col'}, use_global_device_ids=true, to_apply=%region_11.14 | all-reduce | flops 1 | bytes 8 | tf_op jit(solution)/shard_map/psum | solution.py:68
  (59 shorter events, 9.9 us)
Async XLA Ops:
  0.6 4.0 %copy-start.9 = (s32[64]{0:T(128)S(1)}, s32[64]{0:T(128)}, u32[]{:S(2)}) copy-start(s32[64]{0:T(128)} %param.19) | copy-start | bytes 772
  0.6 4.0 %copy-start.10 = (s32[64]{0:T(128)S(1)}, s32[64]{0:T(128)}, u32[]{:S(2)}) copy-start(s32[64]{0:T(128)} %param.18) | copy-start | bytes 772
  1.6 14.1 %collective-permute-start = (f32[3,16,512]{2,1,0:T(8,128)S(1)}, f32[3,16,512]{2,1,0:T(8,128)S(1)}, u32[]{:S(2)}, u32[]{:S(2)}) collective-permute-start(f32[3,16,512]{2,1,0:T(8,128)S(1)} %slice.66), channel_id=1, source_target_pairs={{4,0},{8,4},{12,8},{16,12},{20,16},{24,20},{28,24},{5,1},{9,5},{13... | collective-permute-start | bytes 294920 | tf_op jit(solution)/shard_map/ppermute | solution.py:15
  4.6 2.1 %copy-start.2 = (f32[48,64,64]{2,1,0:T(8,128)}, f32[48,64,64]{2,1,0:T(8,128)S(1)}, u32[]{:S(2)}) copy-start(f32[48,64,64]{2,1,0:T(8,128)S(1)} %reshape.118) | copy-start | bytes 2359300
  4.7 2.1 %copy-start.7 = (f32[64,4096]{1,0:T(8,128)S(1)}, f32[64,4096]{1,0:T(8,128)}, u32[]{:S(2)}) copy-start(f32[64,4096]{1,0:T(8,128)} %param.17) | copy-start | bytes 3145732
  11.6 34.1 %copy-start.1 = (f32[64,64,64]{2,1,0:T(8,128)}, f32[64,64,64]{2,1,0:T(8,128)S(1)}, u32[]{:S(2)}) copy-start(f32[64,64,64]{2,1,0:T(8,128)S(1)} %reshape.117) | copy-start | bytes 3145732
  40.0 12.7 %collective-permute-start.1 = (f32[3,16,512]{2,1,0:T(8,128)S(1)}, f32[3,16,512]{2,1,0:T(8,128)S(1)}, u32[]{:S(2)}, u32[]{:S(2)}) collective-permute-start(f32[3,16,512]{2,1,0:T(8,128)S(1)} %reshape.122), channel_id=1, source_target_pairs={{0,4},{4,8},{8,12},{12,16},{16,20},{20,24},{24,28},{1,5},{5,9},{9,... | collective-permute-start | bytes 294920 | tf_op jit(solution)/shard_map/ppermute | solution.py:15
  52.2 1.1 copy-start
  91.5 1.6 copy-start.4
  91.5 7.5 %collective-permute-start.2 = (f32[3,16,512]{2,1,0:T(8,128)S(1)}, f32[3,16,512]{2,1,0:T(8,128)S(1)}, u32[]{:S(2)}, u32[]{:S(2)}) collective-permute-start(f32[3,16,512]{2,1,0:T(8,128)S(1)} %slice.85), channel_id=1, source_target_pairs={{4,0},{8,4},{12,8},{16,12},{20,16},{24,20},{28,24},{5,1},{9,5},{13... | collective-permute-start | bytes 294920 | tf_op jit(solution)/shard_map/ppermute | solution.py:15
  100.5 3.5 %copy-start.6 = (f32[64,48,64]{2,1,0:T(8,128)S(1)}, f32[64,48,64]{2,1,0:T(8,128)}, u32[]{:S(2)}) copy-start(f32[64,48,64]{2,1,0:T(8,128)} %gather_fusion.2) | copy-start | bytes 2359300
  115.1 8.9 %copy-start.3 = (f32[48,64,64]{2,1,0:T(8,128)S(1)}, f32[48,64,64]{2,1,0:T(8,128)}, u32[]{:S(2)}) copy-start(f32[48,64,64]{2,1,0:T(8,128)} %reshape.123) | copy-start | bytes 2359300
  119.1 14.7 %collective-permute-start.3 = (f32[3,16,512]{2,1,0:T(8,128)S(1)}, f32[3,16,512]{2,1,0:T(8,128)S(1)}, u32[]{:S(2)}, u32[]{:S(2)}) collective-permute-start(f32[3,16,512]{2,1,0:T(8,128)S(1)} %reshape.126), channel_id=1, source_target_pairs={{0,4},{4,8},{8,12},{12,16},{16,20},{20,24},{24,28},{1,5},{5,9},{9,... | collective-permute-start | bytes 294920 | tf_op jit(solution)/shard_map/ppermute | solution.py:15
  131.8 2.0 %copy-start.5 = (f32[3,16,4096]{2,1,0:T(8,128)S(1)}, f32[3,16,4096]{2,1,0:T(8,128)}, u32[]{:S(2)}) copy-start(f32[3,16,4096]{2,1,0:T(8,128)} %copy-done.4) | copy-start | bytes 2359300
  131.8 22.3 %copy-start.8 = (f32[3,4096]{1,0:T(4,128)S(1)}, f32[3,4096]{1,0:T(4,128)}, u32[]{:S(2)}) copy-start(f32[3,4096]{1,0:T(4,128)} %param.21) | copy-start | bytes 147460
where the time goes:
time: 182 us; the launch traced here: 181 us
  blocking collectives  80.8 us (44%)
  local copies, waits for them, and re-layouts  44.2 us (24%)
  matrix products  32.3 us (18%)
  starting transfers between devices  13.4 us (7%)
  other arithmetic  7.92 us (4%)
  between operations  2.3 us (1%)
    psum x2, blocking collectives, squares(): return lax.psum(column_sums(vector, vector), 'dom')  37.4 us
    psum x1, blocking collectives, shards(): step_size = norm_now / lax.psum(column_sums(direction, applied), 'dom')  20 us
    psum x1, blocking collectives, shards(): gradient = lax.psum(partial_gradient, 'dom')  17.1 us
    dot_general x2, matrix products, shards(): jnp.einsum('cki,ikj->ckj', gap_rows, pair_blocks, precision=lax.Precision...  13.6 us
    ppermute x4, starting transfers between devices, shifted(): return lax.ppermute(value, axis, pairs)  13.4 us
    dot_general x2, matrix products, shards(): jnp.einsum('cpi,ipj->cpj', field_rows, stiff_blocks, precision=lax.Precis...  12.1 us
    reshape x4, local copies, waits for them, and re-layouts, shards(): field_rows = direction.reshape(row_count, patches, PN)  7.94 us
    gather x2, local copies, waits for them, and re-layouts, shards(): jnp.take(joined, pair_partner, axis=1)  6.76 us
  transfers between devices with their start and end apart: 4, of which 0 were waited for; matrix products, arithmetic and copies ran while one was open for 19% of the time, Pallas kernels for 0%

commit v1 on v0

v1 whole, which is shorter than its diff:
```python
import functools

import jax
import jax.numpy as jnp
from jax import lax
from jax.experimental import pallas as pl
from jax.experimental.pallas import tpu as pltpu
from jax.sharding import PartitionSpec as P

PN = 64
NB = 8
LANES = 128
MOMENT_LANES = 256
VMEM = pl.BlockSpec(memory_space=pltpu.VMEM)
SMEM = pl.BlockSpec(memory_space=pltpu.SMEM)


def shifted(value, axis, by):
    count = lax.axis_size(axis)
    pairs = [(i, i + by) for i in range(count) if 0 <= i + by < count]
    return lax.ppermute(value, axis, pairs)


def left_half(shape):
    return lax.broadcasted_iota(jnp.int32, shape, len(shape) - 1) < PN


def split(value):
    high = value.astype(jnp.bfloat16)
    low = (value - high.astype(jnp.float32)).astype(jnp.bfloat16)
    return high, low


def tile(ref, index):
    return ref[:, index * LANES : (index + 1) * LANES]


def pair_product(rows, blocks):
    mask = left_half((PN, LANES)).astype(jnp.bfloat16)
    other = (1 - left_half((PN, LANES)).astype(jnp.int32)).astype(jnp.bfloat16)
    block_high, block_low = split(blocks)
    right_high = jnp.concatenate([block_high * mask, block_high * other], axis=0)
    right_low = jnp.concatenate([block_low * mask, block_low * other], axis=0)
    row_high, row_low = split(rows)
    dot = functools.partial(jnp.dot, preferred_element_type=jnp.float32)
    return dot(row_high, right_high) + (dot(row_low, right_high) + dot(row_high, right_low))


def fill_twins(field_tile, twin_ref, patch):
    swapped = pltpu.roll(field_tile, PN, 1)
    left = left_half(field_tile.shape)
    twin_ref[patch] = jnp.where(left, field_tile, swapped)
    twin_ref[patch + 1] = jnp.where(left, swapped, field_tile)


def elastic(field_tile, blocks, total_ref, patch):
    product = pair_product(field_tile, blocks)
    left = left_half(product.shape)
    total_ref[patch] = jnp.where(left, product, 0.0)
    total_ref[patch + 1] = jnp.where(left, 0.0, product)


def contacts(twin_ref, contact_ref, local_ref, partner_ref, count_ref, total_ref):
    rows = twin_ref.shape[1]
    left = left_half((rows, LANES))
    live_count = count_ref[0]
    for step in range(contact_ref.shape[1] // LANES):
        slot = 2 * step
        first_a, first_b = local_ref[slot], partner_ref[slot]
        second_a, second_b = local_ref[slot + 1], partner_ref[slot + 1]
        first_live = jnp.where(slot < live_count, 1.0, 0.0)
        second_live = jnp.where(slot + 1 < live_count, 1.0, 0.0)
        first_gap = (twin_ref[first_a] - twin_ref[first_b]) * first_live
        second_gap = (twin_ref[second_a] - twin_ref[second_b]) * second_live
        force = pair_product(jnp.where(left, first_gap, second_gap), tile(contact_ref, step))
        first_force = jnp.where(left, force, 0.0)
        second_force = jnp.where(left, 0.0, force)
        total_ref[first_a] = total_ref[first_a] + first_force
        total_ref[first_b] = total_ref[first_b] - first_force
        total_ref[second_a] = total_ref[second_a] + second_force
        total_ref[second_b] = total_ref[second_b] - second_force


def folded(total_ref, patch):
    first, second = total_ref[patch], total_ref[patch + 1]
    first = first + pltpu.roll(first, PN, 1)
    second = second + pltpu.roll(second, PN, 1)
    return jnp.where(left_half(first.shape), first, second)


def clear(total_ref, start, stop):
    zero = jnp.zeros(total_ref.shape[1:], jnp.float32)
    for patch in range(start, stop):
        total_ref[patch] = zero


def first_kernel(
    local_ref, partner_ref, count_ref, field_ref, halo_ref, stiff_ref, contact_ref,
    image_ref, lead_ref, spread_ref, twin_ref, total_ref,
):
    patches = field_ref.shape[1] // PN
    for index in range(patches // 2):
        field_tile = tile(field_ref, index)
        fill_twins(field_tile, twin_ref, 2 * index)
        elastic(field_tile, tile(stiff_ref, index), total_ref, 2 * index)
    for index in range(NB // 2):
        fill_twins(tile(halo_ref, index), twin_ref, patches + 2 * index)
    clear(total_ref, patches, patches + NB)
    contacts(twin_ref, contact_ref, local_ref, partner_ref, count_ref, total_ref)
    for index in range(patches // 2):
        value = folded(total_ref, 2 * index)
        image_ref[:, index * LANES : (index + 1) * LANES] = value
        if index < NB // 2:
            lead_ref[:, index * LANES : (index + 1) * LANES] = value
    for index in range(NB // 2):
        spread_ref[:, index * LANES : (index + 1) * LANES] = folded(total_ref, patches + 2 * index)


def by_column(product, columns):
    total = product[:columns]
    for part in range(1, product.shape[0] // columns):
        total = total + product[part * columns : (part + 1) * columns]
    return total


def second_kernel(
    local_ref, partner_ref, count_ref, field_ref, halo_ref, image_ref, spread_ref, received_ref, far_ref,
    stiff_ref, contact_ref, weight_ref,
    twice_ref, moment_ref, far_spread_ref, twin_ref, total_ref, *, columns,
):
    rows = field_ref.shape[0]
    patches = field_ref.shape[1] // PN
    tiles = patches // 2
    lead = NB // 2
    across = jnp.zeros((columns, LANES), jnp.float32)
    square = jnp.zeros((columns, LANES), jnp.float32)
    for index in range(tiles):
        image_tile = tile(image_ref, index)
        if index < lead:
            image_tile = image_tile + tile(received_ref, index)
        fill_twins(image_tile, twin_ref, 2 * index)
        elastic(image_tile, tile(stiff_ref, index), total_ref, 2 * index)
        across = across + by_column(tile(field_ref, index) * image_tile, columns)
        square = square + by_column(image_tile * image_tile, columns)
    across = jnp.sum(across, axis=1, keepdims=True)
    square = jnp.sum(square, axis=1, keepdims=True)
    trial = jnp.where(square > 0.0, across / jnp.where(square > 0.0, square, 1.0), 0.0)
    trial = jnp.broadcast_to(trial, (columns, LANES))
    trial_rows = jnp.concatenate([trial] * (rows // columns), axis=0)
    for index in range(lead):
        far_tile = tile(far_ref, index) + tile(spread_ref, index)
        fill_twins(far_tile, twin_ref, patches + 2 * index)
    clear(total_ref, patches, patches + NB)
    contacts(twin_ref, contact_ref, local_ref, partner_ref, count_ref, total_ref)
    sums = [jnp.zeros((columns, LANES), jnp.float32) for _ in range(12)]

    def add(place, product):
        sums[place] = sums[place] + by_column(product, columns)

    for index in range(tiles):
        field_tile = tile(field_ref, index)
        image_tile = tile(image_ref, index)
        if index < lead:
            image_tile = image_tile + tile(received_ref, index)
        twice_tile = folded(total_ref, 2 * index)
        twice_ref[:, index * LANES : (index + 1) * LANES] = twice_tile
        rest = field_tile - trial_rows * image_tile
        image_rest = image_tile - trial_rows * twice_tile
        weight_tile = jnp.concatenate(
            [
                jnp.broadcast_to(weight_ref[part : part + 1, index * LANES : (index + 1) * LANES], (columns, LANES))
                for part in range(rows // columns)
            ],
            axis=0,
        )
        add(0, field_tile * field_tile)
        add(1, field_tile * image_tile)
        add(2, rest * rest)
        add(3, rest * image_tile)
        add(4, image_tile * image_tile)
        add(5, rest * image_rest)
        add(6, rest * twice_tile + image_tile * image_rest)
        add(7, image_tile * twice_tile)
        add(10, weight_tile * field_tile)
        add(11, weight_tile * image_tile)
    for index in range(lead):
        far_spread = folded(total_ref, patches + 2 * index)
        far_spread_ref[:, index * LANES : (index + 1) * LANES] = far_spread
        far_tile = tile(far_ref, index) + tile(spread_ref, index)
        add(8, (tile(halo_ref, index) - trial_rows * far_tile) * far_spread)
        add(9, far_tile * far_spread)
    lane = lax.broadcasted_iota(jnp.int32, (columns, LANES), 1)
    table = jnp.where(lane == 12, trial, 0.0)
    for place in range(12):
        table = jnp.where(lane == place, jnp.sum(sums[place], axis=1, keepdims=True), table)
    table = jnp.concatenate([table, jnp.zeros((LANES - columns, LANES), jnp.float32)], axis=0)
    flipped = jnp.transpose(table)
    for half in range(2):
        part = flipped[half * 8 : half * 8 + 8]
        row = pltpu.roll(part, 0, 1, stride=columns, stride_axis=0)
        row = jnp.sum(row, axis=0, keepdims=True)
        moment_ref[:, half * LANES : (half + 1) * LANES] = jnp.broadcast_to(row, (moment_ref.shape[0], LANES))


def last_kernel(
    place_ref, moment_ref, field_ref, image_ref, received_ref, twice_ref, far_received_ref,
    solution_ref, residual_ref, step_ref, *, columns, groups,
):
    rows = field_ref.shape[0]
    devices = moment_ref.shape[0]

    def moment(place):
        half = place // 8
        value = moment_ref[:, half * LANES : (half + 1) * LANES]
        shift = (LANES - columns * (place % 8)) % LANES
        if shift:
            value = pltpu.roll(value, shift, 1)
        return value.reshape(devices // 8, 8, LANES)

    def total(value):
        value = jnp.sum(value, axis=0)
        width = groups
        while width < 8:
            value = value + pltpu.roll(value, width, 0)
            width *= 2
        return value

    norm = total(moment(0))
    bend = total(moment(1))
    first_step = norm / bend
    change = first_step[None] - moment(12)
    square = moment(4)
    mixed = moment(3)
    norm_next = total(moment(2) - 2.0 * change * mixed + change * change * square)
    drift = total(mixed - change * square)
    curve = total(
        moment(5) - change * moment(6) + change * change * moment(7)
        - first_step[None] * (moment(8) - change * moment(9))
    )
    ratio = norm_next / norm
    bend_next = curve + 2.0 * ratio * drift + ratio * ratio * bend
    second_step = norm_next / bend_next
    on_field = first_step + second_step * (1.0 + ratio)
    on_image = -second_step * first_step
    gradient = on_field * total(moment(10)) + on_image * total(moment(11))
    lane = lax.broadcasted_iota(jnp.int32, (8, LANES), 1)
    row = lax.broadcasted_iota(jnp.int32, (8, LANES), 0)
    counted = jnp.where((lane < columns) & (row < groups), gradient * gradient, 0.0)
    square_total = jnp.sum(jnp.sum(counted, axis=1, keepdims=True), axis=0, keepdims=True)
    scaled = gradient / jnp.sqrt(square_total / (columns * groups) + 1e-06)
    mine = row == place_ref[0]

    def own(value):
        return jnp.sum(jnp.where(mine, value, 0.0), axis=0, keepdims=True)

    step_ref[...] = own(scaled)[:, :columns]
    pair = jnp.concatenate([own(on_field), own(on_image), jnp.zeros((LANES - 2, LANES), jnp.float32)], axis=0)
    flipped = jnp.transpose(pair)[:columns]
    field_rows = jnp.concatenate([jnp.broadcast_to(flipped[:, 0:1], (columns, LANES))] * (rows // columns), axis=0)
    image_rows = jnp.concatenate([jnp.broadcast_to(flipped[:, 1:2], (columns, LANES))] * (rows // columns), axis=0)
    for index in range(field_ref.shape[1] // LANES):
        field_tile = tile(field_ref, index)
        image_tile = tile(image_ref, index)
        twice_tile = tile(twice_ref, index)
        if index < NB // 2:
            image_tile = image_tile + tile(received_ref, index)
            twice_tile = twice_tile + tile(far_received_ref, index)
        where = slice(index * LANES, (index + 1) * LANES)
        solution_ref[:, where] = field_rows * field_tile + image_rows * image_tile
        residual_ref[:, where] = field_tile - field_rows * image_tile - image_rows * twice_tile


def shards(right_side, stiffness, contact, pair_local, pair_partner, pair_count, objective_weight):
    components, columns, nodes = right_side.shape
    rows = components * columns
    patches = nodes // PN
    groups = lax.axis_size("col")
    devices = lax.axis_size("dom") * groups
    f32 = jnp.float32
    field = right_side.reshape(rows, nodes)
    width = NB * PN
    halo = shifted(right_side[:, :, :width], "dom", -1).reshape(rows, width)
    params = pltpu.CompilerParams(vmem_limit_bytes=48 * 1024 * 1024)
    scratch = [pltpu.VMEM((patches + NB, rows, LANES), f32)] * 2
    wide = jax.ShapeDtypeStruct((rows, nodes), f32)
    narrow = jax.ShapeDtypeStruct((rows, width), f32)
    image, lead, spread = pl.pallas_call(
        first_kernel,
        out_shape=(wide, narrow, narrow),
        in_specs=[SMEM] * 3 + [VMEM] * 4,
        out_specs=(VMEM,) * 3,
        scratch_shapes=scratch,
        compiler_params=params,
        name="first",
    )(pair_local, pair_partner, pair_count, field, halo, stiffness, contact)
    far = shifted(lead, "dom", -1)
    received = shifted(spread, "dom", 1)
    twice, moments, far_spread = pl.pallas_call(
        functools.partial(second_kernel, columns=columns),
        out_shape=(wide, jax.ShapeDtypeStruct((devices, MOMENT_LANES), f32), narrow),
        in_specs=[SMEM] * 3 + [VMEM] * 9,
        out_specs=(VMEM,) * 3,
        scratch_shapes=scratch,
        compiler_params=params,
        name="second",
    )(
        pair_local, pair_partner, pair_count, field, halo, image, spread, received, far,
        stiffness, contact, objective_weight,
    )
    far_received = shifted(far_spread, "dom", 1)
    gathered = lax.all_to_all(moments, ("dom", "col"), 0, 0, tiled=True)
    place = lax.axis_index("col").astype(jnp.int32).reshape(1)
    solution_field, residual, step = pl.pallas_call(
        functools.partial(last_kernel, columns=columns, groups=groups),
        out_shape=(wide, wide, jax.ShapeDtypeStruct((1, columns), f32)),
        in_specs=[SMEM] + [VMEM] * 6,
        out_specs=(VMEM,) * 3,
        compiler_params=params,
        name="last",
    )(place, gathered, field, image, received, twice, far_received)
    return (
        solution_field.reshape(right_side.shape),
        residual.reshape(right_side.shape),
        step.reshape(columns),
    )


def solution(mesh):
    placed = (
        P(None, "col", "dom"),
        P(None, "dom"),
        P(None, "dom"),
        P("dom"),
        P("dom"),
        P("dom"),
        P(None, "dom"),
    )
    return jax.shard_map(
        shards,
        mesh=mesh,
        in_specs=placed,
        out_specs=(P(None, "col", "dom"), P(None, "col", "dom"), P("col")),
        check_vma=False,
    )
```

time: 182 us -> 50.2 us (0.28)
  blocking collectives: 80.8 us -> 0 us
  local copies, waits for them, and re-layouts: 44.2 us -> 5.81 us
  matrix products: 32.3 us -> 0 us
  waiting for transfers between devices: 0.01 us -> 15.2 us
  Pallas kernels: 0 us -> 8.19 us
  other arithmetic: 7.92 us -> 0 us
  starting transfers between devices: 13.4 us -> 19.3 us
    psum x5 -> x0, blocking collectives: 80.8 us -> none  [the longest x2 37.4 us: squares(): return lax.psum(column_sums(vector, vector), 'dom')]
    dot_general x4 -> x0, matrix products: 25.7 us -> none  [the longest x2 13.6 us: shards(): jnp.einsum('cki,ikj->ckj', gap_rows, pair_blocks, precision=lax.Precision...]
    reshape x14 -> x0, local copies, waits for them, and re-layouts: 15 us -> none  [the longest x4 7.94 us: shards(): field_rows = direction.reshape(row_count, patches, PN)]
    gather x4 -> x0, local copies, waits for them, and re-layouts: 12.6 us -> none  [the longest x2 6.76 us: shards(): jnp.take(joined, pair_partner, axis=1)]
    pallas_call x0 -> x3, Pallas kernels: none -> 8.19 us  [the longest x1 3.55 us: shards(): pl.pallas_call(functools.partial(second_kernel, columns=columns), out_sha...]
    ppermute x4, waiting for transfers between devices: 0.01 us -> 7.91 us  [shifted(): return lax.ppermute(value, axis, pairs)]
    all_to_all x0 -> x1, waiting for transfers between devices: none -> 7.25 us  [shards(): gathered = lax.all_to_all(moments, ('dom', 'col'), 0, 0, tiled=True)]
    all_to_all x0 -> x1, starting transfers between devices: none -> 6.62 us  [shards(): gathered = lax.all_to_all(moments, ('dom', 'col'), 0, 0, tiled=True)]
  transfers between devices with their start and end apart: 4 -> 5, of which waited for: 0 -> 4; matrix products, arithmetic and copies ran while one was open for 19% -> 1% of each run, Pallas kernels for 0% -> 0%
where the time goes in v1:
time: 50.2 us; the launch traced here: 49.8 us
  starting transfers between devices  19.3 us (38%)
  waiting for transfers between devices  15.2 us (30%)
  Pallas kernels  8.19 us (16%)
  local copies, waits for them, and re-layouts  5.81 us (12%)
  between operations  1.34 us (3%)
    ppermute x4, starting transfers between devices, shifted(): return lax.ppermute(value, axis, pairs)  12.6 us
    ppermute x4, waiting for transfers between devices, shifted(): return lax.ppermute(value, axis, pairs)  7.91 us
    all_to_all x1, waiting for transfers between devices, shards(): gathered = lax.all_to_all(moments, ('dom', 'col'), 0, 0, tiled=True)  7.25 us
    all_to_all x1, starting transfers between devices, shards(): gathered = lax.all_to_all(moments, ('dom', 'col'), 0, 0, tiled=True)  6.62 us
    unnamed x15, local copies, waits for them, and re-layouts  4.26 us
    pallas_call x1, Pallas kernels, shards(): pl.pallas_call(functools.partial(second_kernel, columns=columns), out_sha...  3.55 us
    pallas_call x1, Pallas kernels, shards(): pl.pallas_call(first_kernel, out_shape=(wide, narrow, narrow), in_specs=[...  2.91 us
    pallas_call x1, Pallas kernels, shards(): pl.pallas_call(functools.partial(last_kernel, columns=columns, groups=gro...  1.73 us
  transfers between devices with their start and end apart: 5, of which 4 were waited for; matrix products, arithmetic and copies ran while one was open for 1% of the time, Pallas kernels for 0%

profile of v1, /device:TPU:0, one launch (start us, length us, event | category | flops | bytes accessed | tf_op | source)
XLA Modules:
  0.0 49.8 jit_solution(6935122139567991866)
XLA Ops:
  0.6 0.9 %slice.3 = f32[3,16,512]{2,1,0:T(8,128)S(1)} slice(f32[3,16,4096]{2,1,0:T(8,128)} %param.7), slice={[0:3], [0:16], [0:512]} | slice | bytes 196608 | tf_op jit(solution)/shard_map/slice | solution.py:282
  1.5 1.3 %collective-permute-start = (f32[3,16,512]{2,1,0:T(8,128)S(1)}, f32[3,16,512]{2,1,0:T(8,128)S(1)}, u32[]{:S(2)}, u32[]{:S(2)}) collective-permute-start(f32[3,16,512]{2,1,0:T(8,128)S(1)} %slice.3), channel_id=1, source_target_pairs={{4,0},{8,4},{12,8},{16,12},{20,16},{24,20},{28,24},{5,1},{9,5},{13... | collective-permute-start | bytes 294920 | tf_op jit(solution)/shard_map/ppermute | solution.py:21
  3.5 5.7 %collective-permute-done = f32[3,16,512]{2,1,0:T(8,128)S(1)} collective-permute-done((f32[3,16,512]{2,1,0:T(8,128)S(1)}, f32[3,16,512]{2,1,0:T(8,128)S(1)}, u32[]{:S(2)}, u32[]{:S(2)}) %collective-permute-start) | collective-permute-done | bytes 98336 | tf_op jit(solution)/shard_map/ppermute | solution.py:21
  9.2 0.0 copy-start.5
  9.2 0.0 copy-start.6
  9.2 0.7 %copy-done.5 = s32[64]{0:T(128)S(1)} copy-done((s32[64]{0:T(128)S(1)}, s32[64]{0:T(128)}, u32[]{:S(2)}) %copy-start.5) | copy-done | bytes 280
  9.8 0.0 copy-done.6
  9.9 0.0 copy-start
  9.9 1.1 %copy-done = f32[3,16,4096]{2,1,0:T(8,128)S(1)} copy-done((f32[3,16,4096]{2,1,0:T(8,128)S(1)}, f32[3,16,4096]{2,1,0:T(8,128)}, u32[]{:S(2)}) %copy-start) | copy-done | bytes 786456
  11.0 0.0 copy-start.2
  11.0 1.2 %copy-done.2 = f32[64,4096]{1,0:T(8,128)S(1)} copy-done((f32[64,4096]{1,0:T(8,128)S(1)}, f32[64,4096]{1,0:T(8,128)}, u32[]{:S(2)}) %copy-start.2) | copy-done | bytes 1048600
  12.2 0.0 copy-start.3
  12.2 1.2 %copy-done.3 = f32[64,4096]{1,0:T(8,128)S(1)} copy-done((f32[64,4096]{1,0:T(8,128)S(1)}, f32[64,4096]{1,0:T(8,128)}, u32[]{:S(2)}) %copy-start.3) | copy-done | bytes 1048600
  13.4 0.0 copy-start.4
  13.4 2.9 %first.1 = (f32[48,4096]{1,0:T(8,128)S(1)}, f32[48,512]{1,0:T(8,128)S(1)}, f32[48,512]{1,0:T(8,128)S(1)}) custom-call(s32[64]{0:T(128)S(1)} %copy-done.5, s32[64]{0:T(128)S(1)} %copy-done.6, s32[1]{0:T(128)S(6)} %copy.14.count_ref, f32[48,4096]{1,0:T(8,128)S(1)} %bitcast.10, f32[48,512]{1,0:T(8,128)S(1)} %bitcast.13, f32[64,4096]{1,0:T(8,128)S(1)} %copy-done.2, ...), custom_call_target="tpu_custom_call" | custom-call | tf_op jit(solution)/shard_map/first/pallas_call | solution.py:287
  16.4 1.3 %collective-permute-start.2 = (f32[48,512]{1,0:T(8,128)S(1)}, f32[48,512]{1,0:T(8,128)S(1)}, u32[]{:S(2)}, u32[]{:S(2)}) collective-permute-start(f32[48,512]{1,0:T(8,128)S(1)} %get-tuple-element.14), channel_id=1, source_target_pairs={{4,0},{8,4},{12,8},{16,12},{20,16},{24,20},{28,24},{5,1},{9,5},{13... | collective-permute-start | bytes 294920 | tf_op jit(solution)/shard_map/ppermute | solution.py:21
  17.7 5.2 %collective-permute-start.1 = (f32[48,512]{1,0:T(8,128)S(1)}, f32[48,512]{1,0:T(8,128)S(1)}, u32[]{:S(2)}, u32[]{:S(2)}) collective-permute-start(f32[48,512]{1,0:T(8,128)S(1)} %get-tuple-element.13.spread_ref), channel_id=1, source_target_pairs={{0,4},{4,8},{8,12},{12,16},{16,20},{20,24},{24,28},{1,5},{5,9},{9,... | collective-permute-start | bytes 294920 | tf_op jit(solution)/shard_map/ppermute | solution.py:21
  22.9 0.7 %collective-permute-done.2.far_ref = f32[48,512]{1,0:T(8,128)S(1)} collective-permute-done((f32[48,512]{1,0:T(8,128)S(1)}, f32[48,512]{1,0:T(8,128)S(1)}, u32[]{:S(2)}, u32[]{:S(2)}) %collective-permute-start.2) | collective-permute-done | bytes 98336 | tf_op jit(solution)/shard_map/ppermute | solution.py:21
  23.6 1.5 %collective-permute-done.1.received_ref = f32[48,512]{1,0:T(8,128)S(1)} collective-permute-done((f32[48,512]{1,0:T(8,128)S(1)}, f32[48,512]{1,0:T(8,128)S(1)}, u32[]{:S(2)}, u32[]{:S(2)}) %collective-permute-start.1) | collective-permute-done | bytes 98336 | tf_op jit(solution)/shard_map/ppermute | solution.py:21
  25.1 0.0 copy-done.4
  25.1 0.0 copy-start.1
  25.1 3.6 %second.1 = (f32[48,4096]{1,0:T(8,128)S(1)}, f32[32,256]{1,0:T(8,128)S(1)}, f32[48,512]{1,0:T(8,128)S(1)}) custom-call(s32[64]{0:T(128)S(1)} %copy-done.5, s32[64]{0:T(128)S(1)} %copy-done.6, s32[1]{0:T(128)S(6)} %copy.14.count_ref, f32[48,4096]{1,0:T(8,128)S(1)} %bitcast.11, f32[48,512]{1,0:T(8,128)S(1)} %bitcast.14, ...), custom_call_target="tpu_custom_call" | custom-call | tf_op jit(solution)/shard_map/second/pallas_call | solution.py:298
  28.7 4.8 %collective-permute-start.3 = (f32[48,512]{1,0:T(8,128)S(1)}, f32[48,512]{1,0:T(8,128)S(1)}, u32[]{:S(2)}, u32[]{:S(2)}) collective-permute-start(f32[48,512]{1,0:T(8,128)S(1)} %get-tuple-element.17), channel_id=1, source_target_pairs={{0,4},{4,8},{8,12},{12,16},{16,20},{20,24},{24,28},{1,5},{5,9},{9,... | collective-permute-start | bytes 294920 | tf_op jit(solution)/shard_map/ppermute | solution.py:21
  33.5 0.6 %copy.10 = f32[32,1,256]{2,1,0:T(1,128)} copy(f32[32,1,256]{2,0,1:T(8,128)S(1)} %bitcast.16) | data formatting | bytes 65536 | tf_op jit(solution)/shard_map/all_to_all | solution.py:311
  34.1 6.6 %all-to-all-start = ((f32[32,1,256]{2,1,0:T(1,128)}), f32[32,1,256]{2,1,0:T(1,128)S(1)}, u32[]{:S(2)}, u32[]{:S(2)}) async-start(f32[32,1,256]{2,1,0:T(1,128)} %copy.10), calls=%async_computation | async-start | bytes 65536 | tf_op jit(solution)/shard_map/all_to_all | solution.py:311
  40.8 7.2 %all-to-all-done = f32[32,1,256]{2,1,0:T(1,128)S(1)} async-done(((f32[32,1,256]{2,1,0:T(1,128)}), f32[32,1,256]{2,1,0:T(1,128)S(1)}, u32[]{:S(2)}, u32[]{:S(2)}) %all-to-all-start) | async-done | bytes 32800 | tf_op jit(solution)/shard_map/all_to_all | solution.py:311
  48.0 0.0 collective-permute-done.3.far_received_ref
  48.0 0.0 copy-done.1
  48.0 1.7 %last.1 = (f32[48,4096]{1,0:T(8,128)}, f32[48,4096]{1,0:T(8,128)}, f32[1,16]{1,0:T(1,128)}) custom-call(s32[1]{0:T(128)} %bitcast.place_ref, f32[32,256]{1,0:T(8,128)S(1)} %bitcast.15, f32[48,4096]{1,0:T(8,128)S(1)} %bitcast.12, f32[48,4096]{1,0:T(8,128)S(1)} %get-tuple-element.12.image_ref, f32[48,512]{1,0:T(8,128)S(1)} %collective-permute-done.1.received_ref, ...), custom_call_target="tpu_custom_call" | custom-call | tf_op jit(solution)/shard_map/last/pallas_call | solution.py:313
  (1 shorter events, 0.0 us)
Async XLA Ops:
  1.5 7.6 %collective-permute-start = (f32[3,16,512]{2,1,0:T(8,128)S(1)}, f32[3,16,512]{2,1,0:T(8,128)S(1)}, u32[]{:S(2)}, u32[]{:S(2)}) collective-permute-start(f32[3,16,512]{2,1,0:T(8,128)S(1)} %slice.3), channel_id=1, source_target_pairs={{4,0},{8,4},{12,8},{16,12},{20,16},{24,20},{28,24},{5,1},{9,5},{13... | collective-permute-start | bytes 294920 | tf_op jit(solution)/shard_map/ppermute | solution.py:21
  9.2 0.7 %copy-start.5 = (s32[64]{0:T(128)S(1)}, s32[64]{0:T(128)}, u32[]{:S(2)}) copy-start(s32[64]{0:T(128)} %local_ref.3) | copy-start | bytes 772
  9.2 0.7 %copy-start.6 = (s32[64]{0:T(128)S(1)}, s32[64]{0:T(128)}, u32[]{:S(2)}) copy-start(s32[64]{0:T(128)} %partner_ref.3) | copy-start | bytes 772
  9.9 1.1 %copy-start = (f32[3,16,4096]{2,1,0:T(8,128)S(1)}, f32[3,16,4096]{2,1,0:T(8,128)}, u32[]{:S(2)}) copy-start(f32[3,16,4096]{2,1,0:T(8,128)} %param.7) | copy-start | bytes 2359300
  11.0 1.2 %copy-start.2 = (f32[64,4096]{1,0:T(8,128)S(1)}, f32[64,4096]{1,0:T(8,128)}, u32[]{:S(2)}) copy-start(f32[64,4096]{1,0:T(8,128)} %stiff_ref.3) | copy-start | bytes 3145732
  12.2 1.2 %copy-start.3 = (f32[64,4096]{1,0:T(8,128)S(1)}, f32[64,4096]{1,0:T(8,128)}, u32[]{:S(2)}) copy-start(f32[64,4096]{1,0:T(8,128)} %contact_ref.3) | copy-start | bytes 3145732
  13.4 11.7 %copy-start.4 = (f32[3,4096]{1,0:T(4,128)S(1)}, f32[3,4096]{1,0:T(4,128)}, u32[]{:S(2)}) copy-start(f32[3,4096]{1,0:T(4,128)} %weight_ref.1) | copy-start | bytes 147460
  16.4 7.2 %collective-permute-start.2 = (f32[48,512]{1,0:T(8,128)S(1)}, f32[48,512]{1,0:T(8,128)S(1)}, u32[]{:S(2)}, u32[]{:S(2)}) collective-permute-start(f32[48,512]{1,0:T(8,128)S(1)} %get-tuple-element.14), channel_id=1, source_target_pairs={{4,0},{8,4},{12,8},{16,12},{20,16},{24,20},{28,24},{5,1},{9,5},{13... | collective-permute-start | bytes 294920 | tf_op jit(solution)/shard_map/ppermute | solution.py:21
  17.7 7.4 %collective-permute-start.1 = (f32[48,512]{1,0:T(8,128)S(1)}, f32[48,512]{1,0:T(8,128)S(1)}, u32[]{:S(2)}, u32[]{:S(2)}) collective-permute-start(f32[48,512]{1,0:T(8,128)S(1)} %get-tuple-element.13.spread_ref), channel_id=1, source_target_pairs={{0,4},{4,8},{8,12},{12,16},{16,20},{20,24},{24,28},{1,5},{5,9},{9,... | collective-permute-start | bytes 294920 | tf_op jit(solution)/shard_map/ppermute | solution.py:21
  25.1 22.9 %copy-start.1 = (f32[3,16,4096]{2,1,0:T(8,128)S(1)}, f32[3,16,4096]{2,1,0:T(8,128)}, u32[]{:S(2)}) copy-start(f32[3,16,4096]{2,1,0:T(8,128)} %param.7) | copy-start | bytes 2359300
  28.7 19.4 %collective-permute-start.3 = (f32[48,512]{1,0:T(8,128)S(1)}, f32[48,512]{1,0:T(8,128)S(1)}, u32[]{:S(2)}, u32[]{:S(2)}) collective-permute-start(f32[48,512]{1,0:T(8,128)S(1)} %get-tuple-element.17), channel_id=1, source_target_pairs={{0,4},{4,8},{8,12},{12,16},{16,20},{20,24},{24,28},{1,5},{5,9},{9,... | collective-permute-start | bytes 294920 | tf_op jit(solution)/shard_map/ppermute | solution.py:21
  34.1 13.9 %all-to-all-start = ((f32[32,1,256]{2,1,0:T(1,128)}), f32[32,1,256]{2,1,0:T(1,128)S(1)}, u32[]{:S(2)}, u32[]{:S(2)}) async-start(f32[32,1,256]{2,1,0:T(1,128)} %copy.10), calls=%async_computation | async-start | bytes 65536 | tf_op jit(solution)/shard_map/all_to_all | solution.py:311

commit v2 on v1

v2 whole, which is shorter than its diff:
```python
import functools

import jax
import jax.numpy as jnp
from jax import lax
from jax.experimental import pallas as pl
from jax.experimental.pallas import tpu as pltpu
from jax.sharding import PartitionSpec as P

PN = 64
NB = 8
LANES = 128
MOMENT_LANES = 256
VMEM = pl.BlockSpec(memory_space=pltpu.VMEM)
SMEM = pl.BlockSpec(memory_space=pltpu.SMEM)
HBM = pl.BlockSpec(memory_space=pltpu.HBM)
SUMS = 12


def shifted(value, axis, by):
    count = lax.axis_size(axis)
    pairs = [(i, i + by) for i in range(count) if 0 <= i + by < count]
    return lax.ppermute(value, axis, pairs)


def swapped(value, axis, odd):
    count = lax.axis_size(axis)
    pairs = []
    for low in range(1 if odd else 0, count, 2):
        high = (low + 1) % count
        pairs += [(low, high), (high, low)]
    return lax.ppermute(value, axis, pairs)


def left_half(shape):
    return lax.broadcasted_iota(jnp.int32, shape, len(shape) - 1) < PN


def split(value):
    high = value.astype(jnp.bfloat16)
    low = (value - high.astype(jnp.float32)).astype(jnp.bfloat16)
    return high, low


def tile(ref, index):
    return ref[:, index * LANES : (index + 1) * LANES]


def put(ref, index, value):
    ref[:, index * LANES : (index + 1) * LANES] = value


def block_diagonal(high, low):
    mask = left_half((PN, LANES)).astype(jnp.bfloat16)
    other = (1 - left_half((PN, LANES)).astype(jnp.int32)).astype(jnp.bfloat16)
    return (
        jnp.concatenate([high * mask, high * other], axis=0),
        jnp.concatenate([low * mask, low * other], axis=0),
    )


def pair_product(rows, high, low):
    right_high, right_low = block_diagonal(high, low)
    row_high, row_low = split(rows)
    dot = functools.partial(jnp.dot, preferred_element_type=jnp.float32)
    return dot(row_high, right_high) + (dot(row_low, right_high) + dot(row_high, right_low))


def fill_twins(field_tile, twin_ref, patch):
    swapped = pltpu.roll(field_tile, PN, 1)
    left = left_half(field_tile.shape)
    twin_ref[patch] = jnp.where(left, field_tile, swapped)
    twin_ref[patch + 1] = jnp.where(left, swapped, field_tile)


def contacts(twin_ref, high_ref, low_ref, local_ref, partner_ref, count_ref, total_ref):
    rows = twin_ref.shape[1]
    left = left_half((rows, LANES))
    live_count = count_ref[0]
    for step in range(high_ref.shape[1] // LANES):
        slot = 2 * step
        first_a, first_b = local_ref[slot], partner_ref[slot]
        second_a, second_b = local_ref[slot + 1], partner_ref[slot + 1]
        first_live = jnp.where(slot < live_count, 1.0, 0.0)
        second_live = jnp.where(slot + 1 < live_count, 1.0, 0.0)
        first_gap = (twin_ref[first_a] - twin_ref[first_b]) * first_live
        second_gap = (twin_ref[second_a] - twin_ref[second_b]) * second_live
        force = pair_product(
            jnp.where(left, first_gap, second_gap), tile(high_ref, step), tile(low_ref, step)
        )
        first_force = jnp.where(left, force, 0.0)
        second_force = jnp.where(left, 0.0, force)
        total_ref[first_a] = total_ref[first_a] + first_force
        total_ref[first_b] = total_ref[first_b] - first_force
        total_ref[second_a] = total_ref[second_a] + second_force
        total_ref[second_b] = total_ref[second_b] - second_force


def folded(total_ref, patch):
    first, second = total_ref[patch], total_ref[patch + 1]
    first = first + pltpu.roll(first, PN, 1)
    second = second + pltpu.roll(second, PN, 1)
    return jnp.where(left_half(first.shape), first, second)


def clear(total_ref):
    zero = jnp.zeros(total_ref.shape[1:], jnp.float32)
    for patch in range(total_ref.shape[0]):
        total_ref[patch] = zero


def prepare_kernel(
    field_hbm, stiff_hbm, contact_hbm,
    field_ref, elastic_ref, stiff_high_ref, stiff_low_ref, contact_high_ref, contact_low_ref,
    stiff_ref, contact_ref, sems,
):
    patches = field_ref.shape[1] // PN
    copies = [
        pltpu.make_async_copy(field_hbm, field_ref, sems.at[0]),
        pltpu.make_async_copy(stiff_hbm, stiff_ref, sems.at[1]),
        pltpu.make_async_copy(contact_hbm, contact_ref, sems.at[2]),
    ]
    for copy in copies:
        copy.start()
    copies[0].wait()
    copies[1].wait()
    for index in range(patches // 2):
        field_tile = tile(field_ref, index)
        high, low = split(tile(stiff_ref, index))
        put(stiff_high_ref, index, high)
        put(stiff_low_ref, index, low)
        put(elastic_ref, index, pair_product(field_tile, high, low))
    copies[2].wait()
    for index in range(contact_ref.shape[1] // LANES):
        high, low = split(tile(contact_ref, index))
        put(contact_high_ref, index, high)
        put(contact_low_ref, index, low)


def couple_kernel(
    local_ref, partner_ref, count_ref, chain_ref, field_ref, elastic_ref, halo_ref, high_ref, low_ref,
    image_ref, spread_ref, even_ref, odd_ref, twin_ref, total_ref,
):
    patches = image_ref.shape[1] // PN
    lead = NB // 2
    clear(total_ref)
    for index in range(patches // 2):
        fill_twins(tile(field_ref, index), twin_ref, 2 * index)
    for index in range(lead):
        fill_twins(tile(halo_ref, index), twin_ref, patches + 2 * index)
    contacts(twin_ref, high_ref, low_ref, local_ref, partner_ref, count_ref, total_ref)
    even = chain_ref[0] % 2 == 0
    for index in range(patches // 2):
        value = tile(elastic_ref, index) + folded(total_ref, 2 * index)
        put(image_ref, index, value)
        if index < lead:
            spread = folded(total_ref, patches + 2 * index)
            put(spread_ref, index, spread)
            put(even_ref, index, jnp.where(even, spread, value))
            put(odd_ref, index, jnp.where(even, value, spread))


def by_column(product, columns):
    total = product[:columns]
    for part in range(1, product.shape[0] // columns):
        total = total + product[part * columns : (part + 1) * columns]
    return total


class Sums:
    def __init__(self, columns):
        self.columns = columns
        self.values = {}

    def add(self, place, product):
        product = by_column(product, self.columns)
        self.values[place] = self.values[place] + product if place in self.values else product

    def load(self, ref):
        for place in range(SUMS):
            self.values[place] = ref[place * self.columns : (place + 1) * self.columns]

    def store(self, ref):
        for place in range(SUMS):
            zero = jnp.zeros((self.columns, LANES), jnp.float32)
            ref[place * self.columns : (place + 1) * self.columns] = self.values.get(place, zero)


def weights_of(weight_ref, index, rows):
    parts = weight_ref.shape[0]
    return jnp.concatenate(
        [
            jnp.broadcast_to(weight_ref[part : part + 1, index * LANES : (index + 1) * LANES], (rows // parts, LANES))
            for part in range(parts)
        ],
        axis=0,
    )


def lift_kernel(
    field_ref, image_ref, stiff_high_ref, stiff_low_ref, weight_ref,
    elastic_ref, sums_ref, trial_ref, *, columns,
):
    rows = field_ref.shape[0]
    patches = field_ref.shape[1] // PN
    lead = NB // 2
    sums = Sums(columns)
    for index in range(patches // 2):
        field_tile = tile(field_ref, index)
        weight_tile = weights_of(weight_ref, index, rows)
        sums.add(0, field_tile * field_tile)
        sums.add(10, weight_tile * field_tile)
        if index < lead:
            continue
        image_tile = tile(image_ref, index)
        product = pair_product(image_tile, tile(stiff_high_ref, index), tile(stiff_low_ref, index))
        put(elastic_ref, index - lead, product)
        sums.add(1, field_tile * image_tile)
        sums.add(4, image_tile * image_tile)
        sums.add(11, weight_tile * image_tile)
    across = jnp.sum(sums.values[1], axis=1, keepdims=True)
    square = jnp.sum(sums.values[4], axis=1, keepdims=True)
    some = square > 0.0
    trial = jnp.where(some, across / jnp.where(some, square, 1.0), 0.0)
    trial = jnp.broadcast_to(trial, (columns, LANES))
    trial_ref[...] = trial
    trial_rows = jnp.concatenate([trial] * (rows // columns), axis=0)
    for index in range(lead, patches // 2):
        image_tile = tile(image_ref, index)
        rest = tile(field_ref, index) - trial_rows * image_tile
        sums.add(2, rest * rest)
        sums.add(3, rest * image_tile)
    sums.store(sums_ref)


def second_kernel(
    local_ref, partner_ref, count_ref, chain_ref, field_ref, halo_ref, image_ref, spread_ref, even_ref, odd_ref,
    stiff_high_ref, stiff_low_ref, contact_high_ref, contact_low_ref, weight_ref, sums_ref, trial_ref, elastic_ref,
    twice_ref, lead_ref, moment_ref, far_spread_ref, twin_ref, total_ref, *, columns,
):
    rows = field_ref.shape[0]
    patches = field_ref.shape[1] // PN
    lead = NB // 2
    place, last = chain_ref[0], chain_ref[1] - 1
    even = place % 2 == 0
    trial = trial_ref[...]
    trial_rows = jnp.concatenate([trial] * (rows // columns), axis=0)
    sums = Sums(columns)
    sums.load(sums_ref)
    far_tiles = []
    products = []
    clear(total_ref)
    for index in range(lead, patches // 2):
        fill_twins(tile(image_ref, index), twin_ref, 2 * index)
    for index in range(lead):
        first, second = tile(even_ref, index), tile(odd_ref, index)
        received = jnp.where(place > 0, jnp.where(even, second, first), 0.0)
        far_tile = jnp.where(place < last, jnp.where(even, first, second) + tile(spread_ref, index), 0.0)
        far_tiles.append(far_tile)
        fill_twins(far_tile, twin_ref, patches + 2 * index)
        field_tile = tile(field_ref, index)
        image_tile = tile(image_ref, index) + received
        put(lead_ref, index, image_tile)
        fill_twins(image_tile, twin_ref, 2 * index)
        products.append(pair_product(image_tile, tile(stiff_high_ref, index), tile(stiff_low_ref, index)))
        rest = field_tile - trial_rows * image_tile
        sums.add(1, field_tile * image_tile)
        sums.add(2, rest * rest)
        sums.add(3, rest * image_tile)
        sums.add(4, image_tile * image_tile)
        sums.add(11, weights_of(weight_ref, index, rows) * image_tile)
    contacts(twin_ref, contact_high_ref, contact_low_ref, local_ref, partner_ref, count_ref, total_ref)
    for index in range(patches // 2):
        image_tile = tile(lead_ref if index < lead else image_ref, index)
        product = products[index] if index < lead else tile(elastic_ref, index - lead)
        twice_tile = product + folded(total_ref, 2 * index)
        put(twice_ref, index, twice_tile)
        rest = tile(field_ref, index) - trial_rows * image_tile
        image_rest = image_tile - trial_rows * twice_tile
        sums.add(5, rest * image_rest)
        sums.add(6, rest * twice_tile + image_tile * image_rest)
        sums.add(7, image_tile * twice_tile)
    for index in range(lead):
        far_spread = folded(total_ref, patches + 2 * index)
        put(far_spread_ref, index, far_spread)
        sums.add(8, (tile(halo_ref, index) - trial_rows * far_tiles[index]) * far_spread)
        sums.add(9, far_tiles[index] * far_spread)
    lane = lax.broadcasted_iota(jnp.int32, (columns, LANES), 1)
    table = jnp.where(lane == SUMS, trial, 0.0)
    for number in range(SUMS):
        table = jnp.where(lane == number, jnp.sum(sums.values[number], axis=1, keepdims=True), table)
    table = jnp.concatenate([table, jnp.zeros((LANES - columns, LANES), jnp.float32)], axis=0)
    flipped = jnp.transpose(table)
    for half in range(2):
        row = pltpu.roll(flipped[half * 8 : half * 8 + 8], 0, 1, stride=columns, stride_axis=0)
        row = jnp.sum(row, axis=0, keepdims=True)
        moment_ref[:, :, half * LANES : (half + 1) * LANES] = jnp.broadcast_to(
            row[None], (moment_ref.shape[0], 1, LANES)
        )


def relay_kernel(value_ref, out_ref):
    out_ref[...] = value_ref[...]


def last_kernel(
    place_ref, moment_ref, field_ref, image_ref, lead_ref, twice_ref, far_received_ref,
    solution_ref, residual_ref, step_ref, *, columns, groups,
):
    rows = field_ref.shape[0]
    devices = moment_ref.shape[0]

    def moment(place):
        half = place // 8
        value = moment_ref[:, half * LANES : (half + 1) * LANES]
        shift = (LANES - columns * (place % 8)) % LANES
        if shift:
            value = pltpu.roll(value, shift, 1)
        return value.reshape(devices // 8, 8, LANES)

    def total(value):
        value = jnp.sum(value, axis=0)
        width = groups
        while width < 8:
            value = value + pltpu.roll(value, width, 0)
            width *= 2
        return value

    norm = total(moment(0))
    bend = total(moment(1))
    first_step = norm / bend
    change = first_step[None] - moment(12)
    square = moment(4)
    mixed = moment(3)
    norm_next = total(moment(2) - 2.0 * change * mixed + change * change * square)
    drift = total(mixed - change * square)
    curve = total(
        moment(5) - change * moment(6) + change * change * moment(7)
        - first_step[None] * (moment(8) - change * moment(9))
    )
    ratio = norm_next / norm
    bend_next = curve + 2.0 * ratio * drift + ratio * ratio * bend
    second_step = norm_next / bend_next
    on_field = first_step + second_step * (1.0 + ratio)
    on_image = -second_step * first_step
    gradient = on_field * total(moment(10)) + on_image * total(moment(11))
    lane = lax.broadcasted_iota(jnp.int32, (8, LANES), 1)
    row = lax.broadcasted_iota(jnp.int32, (8, LANES), 0)
    counted = jnp.where((lane < columns) & (row < groups), gradient * gradient, 0.0)
    square_total = jnp.sum(jnp.sum(counted, axis=1, keepdims=True), axis=0, keepdims=True)
    scaled = gradient / jnp.sqrt(square_total / (columns * groups) + 1e-06)
    mine = row == place_ref[0]

    def own(value):
        return jnp.sum(jnp.where(mine, value, 0.0), axis=0, keepdims=True)

    step_ref[...] = own(scaled)[:, :columns]
    pair = jnp.concatenate([own(on_field), own(on_image), jnp.zeros((LANES - 2, LANES), jnp.float32)], axis=0)
    flipped = jnp.transpose(pair)[:columns]
    field_rows = jnp.concatenate([jnp.broadcast_to(flipped[:, 0:1], (columns, LANES))] * (rows // columns), axis=0)
    image_rows = jnp.concatenate([jnp.broadcast_to(flipped[:, 1:2], (columns, LANES))] * (rows // columns), axis=0)
    for index in range(field_ref.shape[1] // LANES):
        field_tile = tile(field_ref, index)
        image_tile = tile(lead_ref if index < NB // 2 else image_ref, index)
        twice_tile = tile(twice_ref, index)
        if index < NB // 2:
            twice_tile = twice_tile + tile(far_received_ref, index)
        where = slice(index * LANES, (index + 1) * LANES)
        solution_ref[:, where] = field_rows * field_tile + image_rows * image_tile
        residual_ref[:, where] = field_tile - field_rows * image_tile - image_rows * twice_tile


def shards(right_side, stiffness, contact, pair_local, pair_partner, pair_count, objective_weight):
    components, columns, nodes = right_side.shape
    rows = components * columns
    patches = nodes // PN
    groups = lax.axis_size("col")
    chain_length = lax.axis_size("dom")
    devices = chain_length * groups
    f32 = jnp.float32
    width = NB * PN
    call = functools.partial(
        pl.pallas_call, compiler_params=pltpu.CompilerParams(vmem_limit_bytes=16 * 1024 * 1024)
    )
    shape = jax.ShapeDtypeStruct
    wide = shape((rows, nodes), f32)
    narrow = shape((rows, width), f32)
    scratch = [pltpu.VMEM((patches + NB, rows, LANES), f32)] * 2
    parts = [shape(block.shape, jnp.bfloat16) for block in (stiffness, stiffness, contact, contact)]

    field_hbm = right_side.reshape(rows, nodes)
    halo = shifted(right_side[:, :, :width], "dom", -1).reshape(rows, width)
    chain = jnp.stack([lax.axis_index("dom").astype(jnp.int32), jnp.int32(chain_length)])
    tables = (pair_local, pair_partner, pair_count, chain)
    field, elastic, stiff_high, stiff_low, contact_high, contact_low = call(
        prepare_kernel,
        out_shape=(wide, wide, *parts),
        in_specs=[HBM] * 3,
        out_specs=(VMEM,) * 6,
        scratch_shapes=[
            pltpu.VMEM(stiffness.shape, f32),
            pltpu.VMEM(contact.shape, f32),
            pltpu.SemaphoreType.DMA((3,)),
        ],
        name="prepare",
    )(*(pltpu.with_memory_space_constraint(value, pltpu.HBM) for value in (field_hbm, stiffness, contact)))
    image, spread, even, odd = call(
        couple_kernel,
        out_shape=(wide, narrow, narrow, narrow),
        in_specs=[SMEM] * 4 + [VMEM] * 5,
        out_specs=(VMEM,) * 4,
        scratch_shapes=scratch,
        name="couple",
    )(*tables, field, elastic, halo, contact_high, contact_low)
    even = swapped(even, "dom", False)
    odd = swapped(odd, "dom", True)
    elastic, sums, trial = call(
        functools.partial(lift_kernel, columns=columns),
        out_shape=(
            shape((rows, nodes - width), f32),
            shape((SUMS * columns, LANES), f32),
            shape((columns, LANES), f32),
        ),
        in_specs=[VMEM] * 5,
        out_specs=(VMEM,) * 3,
        name="lift",
    )(field, image, stiff_high, stiff_low, objective_weight)
    twice, lead, moments, far_spread = call(
        functools.partial(second_kernel, columns=columns),
        out_shape=(wide, narrow, shape((devices, 1, MOMENT_LANES), f32), narrow),
        in_specs=[SMEM] * 4 + [VMEM] * 14,
        out_specs=(VMEM,) * 4,
        scratch_shapes=scratch,
        name="second",
    )(
        *tables, field, halo, image, spread, even, odd, stiff_high, stiff_low, contact_high, contact_low,
        objective_weight, sums, trial, elastic,
    )
    gathered = lax.all_to_all(moments, ("dom", "col"), 0, 0, tiled=True).reshape(devices, MOMENT_LANES)
    far_spread = call(relay_kernel, out_shape=narrow, in_specs=[VMEM], out_specs=VMEM, name="relay")(far_spread)
    far_received = shifted(far_spread, "dom", 1)
    place = lax.axis_index("col").astype(jnp.int32).reshape(1)
    solution_field, residual, step = call(
        functools.partial(last_kernel, columns=columns, groups=groups),
        out_shape=(wide, wide, shape((1, columns), f32)),
        in_specs=[SMEM] + [VMEM] * 6,
        out_specs=(VMEM,) * 3,
        name="last",
    )(place, gathered, field, image, lead, twice, far_received)
    return (
        solution_field.reshape(right_side.shape),
        residual.reshape(right_side.shape),
        step.reshape(columns),
    )


def solution(mesh):
    placed = (
        P(None, "col", "dom"),
        P(None, "dom"),
        P(None, "dom"),
        P("dom"),
        P("dom"),
        P("dom"),
        P(None, "dom"),
    )
    return jax.shard_map(
        shards,
        mesh=mesh,
        in_specs=placed,
        out_specs=(P(None, "col", "dom"), P(None, "col", "dom"), P("col")),
        check_vma=False,
    )
```

time: 50.2 us -> 41.9 us (0.83)
  starting transfers between devices: 19.3 us -> 13.5 us
  local copies, waits for them, and re-layouts: 5.81 us -> 1.58 us
  Pallas kernels: 8.19 us -> 11.4 us
  waiting for transfers between devices: 15.2 us -> 13.8 us
    ppermute x4 -> x2, starting transfers between devices: 12.6 us -> 2.58 us  [shifted(): return lax.ppermute(value, axis, pairs)]
    ppermute x0 -> x2, starting transfers between devices: none -> 5.62 us  [swapped(): return lax.ppermute(value, axis, pairs)]
    ppermute x4 -> x2, waiting for transfers between devices: 7.91 us -> 2.98 us  [shifted(): return lax.ppermute(value, axis, pairs)]
    unnamed x15 -> x7, local copies, waits for them, and re-layouts: 4.26 us -> 0.68 us
    ppermute x0 -> x2, waiting for transfers between devices: none -> 3.52 us  [swapped(): return lax.ppermute(value, axis, pairs)]
    pallas_call x3 -> x6, Pallas kernels: 8.19 us -> 11.4 us  [the longest x1 3.49 us: shards(): call(functools.partial(second_kernel, columns=columns), out_shape=(wide,...]
    all_to_all x1, starting transfers between devices: 6.62 us -> 5.31 us  [shards(): lax.all_to_all(moments, ('dom', 'col'), 0, 0, tiled=True)]
    all_to_all x1 -> x0, local copies, waits for them, and re-layouts: 0.65 us -> none  [shards(): gathered = lax.all_to_all(moments, ('dom', 'col'), 0, 0, tiled=True)]
  transfers between devices with their start and end apart: 5 -> 5, of which waited for: 4 -> 3; matrix products, arithmetic and copies ran while one was open for 1% -> 0% of each run, Pallas kernels for 0% -> 9%
where the time goes in v2:
time: 41.9 us; the launch traced here: 41.6 us
  waiting for transfers between devices  13.8 us (33%)
  starting transfers between devices  13.5 us (32%)
  Pallas kernels  11.4 us (27%)
  local copies, waits for them, and re-layouts  1.58 us (4%)
  between operations  1.35 us (3%)
    all_to_all x1, waiting for transfers between devices, shards(): lax.all_to_all(moments, ('dom', 'col'), 0, 0, tiled=True)  7.25 us
    ppermute x2, starting transfers between devices, swapped(): return lax.ppermute(value, axis, pairs)  5.62 us
    all_to_all x1, starting transfers between devices, shards(): lax.all_to_all(moments, ('dom', 'col'), 0, 0, tiled=True)  5.31 us
    ppermute x2, waiting for transfers between devices, swapped(): return lax.ppermute(value, axis, pairs)  3.52 us
    pallas_call x1, Pallas kernels, shards(): call(functools.partial(second_kernel, columns=columns), out_shape=(wide,...  3.49 us
    ppermute x2, waiting for transfers between devices, shifted(): return lax.ppermute(value, axis, pairs)  2.98 us
    pallas_call x1, Pallas kernels, shards(): call(prepare_kernel, out_shape=(wide, wide, *parts), in_specs=[HBM] * 3,...  2.65 us
    ppermute x2, starting transfers between devices, shifted(): return lax.ppermute(value, axis, pairs)  2.58 us
  transfers between devices with their start and end apart: 5, of which 3 were waited for; matrix products, arithmetic and copies ran while one was open for 0% of the time, Pallas kernels for 9%

profile of v2, /device:TPU:0, one launch (start us, length us, event | category | flops | bytes accessed | tf_op | source)
XLA Modules:
  0.0 41.6 jit_solution(6847456241807123709)
XLA Ops:
  0.6 0.9 %slice.3 = f32[3,16,512]{2,1,0:T(8,128)S(1)} slice(f32[3,16,4096]{2,1,0:T(8,128)} %param.7), slice={[0:3], [0:16], [0:512]} | slice | bytes 196608 | tf_op jit(solution)/shard_map/slice | solution.py:392
  1.5 1.3 %collective-permute-start = (f32[3,16,512]{2,1,0:T(8,128)S(1)}, f32[3,16,512]{2,1,0:T(8,128)S(1)}, u32[]{:S(2)}, u32[]{:S(2)}) collective-permute-start(f32[3,16,512]{2,1,0:T(8,128)S(1)} %slice.3), channel_id=1, source_target_pairs={{4,0},{8,4},{12,8},{16,12},{20,16},{24,20},{28,24},{5,1},{9,5},{13... | collective-permute-start | bytes 294920 | tf_op jit(solution)/shard_map/ppermute | solution.py:23
  3.5 2.7 %prepare.1 = (f32[48,4096]{1,0:T(8,128)S(1)}, f32[48,4096]{1,0:T(8,128)S(1)}, bf16[64,4096]{1,0:T(8,128)(2,1)S(1)}, bf16[64,4096]{1,0:T(8,128)(2,1)S(1)}, bf16[6...) custom-call(f32[48,4096]{1,0:T(8,128)} %bitcast.13, f32[64,4096]{1,0:T(8,128)} %stiff_hbm.1, f32[64,4096]{1,0:T(8,128)} %contact_hbm.1), custom_call_target="tpu_custom_call" | custom-call | tf_op jit(solution)/shard_map/prepare/pallas_call | solution.py:395
  6.1 0.1 pad_add_fusion.chain_ref
  6.2 3.0 %collective-permute-done = f32[3,16,512]{2,1,0:T(8,128)S(1)} collective-permute-done((f32[3,16,512]{2,1,0:T(8,128)S(1)}, f32[3,16,512]{2,1,0:T(8,128)S(1)}, u32[]{:S(2)}, u32[]{:S(2)}) %collective-permute-start) | collective-permute-done | bytes 98336 | tf_op jit(solution)/shard_map/ppermute | solution.py:23
  9.2 0.0 copy-start.1
  9.2 0.0 copy-start.2
  9.2 0.7 %copy-done.1 = s32[64]{0:T(128)S(1)} copy-done((s32[64]{0:T(128)S(1)}, s32[64]{0:T(128)}, u32[]{:S(2)}) %copy-start.1) | copy-done | bytes 280
  9.8 0.0 copy-done.2
  9.9 0.0 copy-start
  9.9 2.6 %couple.1 = (f32[48,4096]{1,0:T(8,128)S(1)}, f32[48,512]{1,0:T(8,128)S(1)}, f32[48,512]{1,0:T(8,128)S(1)}, f32[48,512]{1,0:T(8,128)S(1)}) custom-call(s32[64]{0:T(128)S(1)} %copy-done.1, s32[64]{0:T(128)S(1)} %copy-done.2, s32[1]{0:T(128)S(6)} %copy.14.count_ref, s32[2]{0:T(128)S(1)} %pad_add_fusion.chain_ref, f32[48,4096]{1,0:T(8,128)S(1)} %get-tuple-element.23.field_ref, ...), custom_call_target="tpu_custom_call" | custom-call | tf_op jit(solution)/shard_map/couple/pallas_call | solution.py:407
  12.4 2.8 %collective-permute-start.1 = (f32[48,512]{1,0:T(8,128)S(1)}, f32[48,512]{1,0:T(8,128)S(1)}, u32[]{:S(2)}, u32[]{:S(2)}) collective-permute-start(f32[48,512]{1,0:T(8,128)S(1)} %get-tuple-element.29), channel_id=1, source_target_pairs={{0,4},{4,0},{8,12},{12,8},{16,20},{20,16},{24,28},{28,24},{1,5},{5... | collective-permute-start | bytes 294920 | tf_op jit(solution)/shard_map/ppermute | solution.py:32
  15.2 2.8 %collective-permute-start.2 = (f32[48,512]{1,0:T(8,128)S(1)}, f32[48,512]{1,0:T(8,128)S(1)}, u32[]{:S(2)}, u32[]{:S(2)}) collective-permute-start(f32[48,512]{1,0:T(8,128)S(1)} %get-tuple-element.30), channel_id=1, source_target_pairs={{4,8},{8,4},{12,16},{16,12},{20,24},{24,20},{28,0},{0,28},{5,9},{9... | collective-permute-start | bytes 294920 | tf_op jit(solution)/shard_map/ppermute | solution.py:32
  18.1 0.0 copy-done
  18.1 0.9 %lift.1 = (f32[48,3584]{1,0:T(8,128)S(1)}, f32[192,128]{1,0:T(8,128)S(1)}, f32[16,128]{1,0:T(8,128)S(1)}) custom-call(f32[48,4096]{1,0:T(8,128)S(1)} %get-tuple-element.23.field_ref, f32[48,4096]{1,0:T(8,128)S(1)} %get-tuple-element.27.image_ref, bf16[64,4096]{1,0:T(8,128)(2,1)S(1)} %get-tuple-element.31.stiff_high_ref, ...), custom_call_target="tpu_custom_call" | custom-call | tf_op jit(solution)/shard_map/lift/pallas_call | solution.py:417
  19.0 0.0 collective-permute-done.1.even_ref
  19.0 3.5 %collective-permute-done.2.odd_ref = f32[48,512]{1,0:T(8,128)S(1)} collective-permute-done((f32[48,512]{1,0:T(8,128)S(1)}, f32[48,512]{1,0:T(8,128)S(1)}, u32[]{:S(2)}, u32[]{:S(2)}) %collective-permute-start.2) | collective-permute-done | bytes 98336 | tf_op jit(solution)/shard_map/ppermute | solution.py:32
  22.5 3.5 %second.1 = (f32[48,4096]{1,0:T(8,128)S(1)}, f32[48,512]{1,0:T(8,128)S(1)}, f32[32,1,256]{2,1,0:T(1,128)}, f32[48,512]{1,0:T(8,128)S(1)}) custom-call(s32[64]{0:T(128)S(1)} %copy-done.1, s32[64]{0:T(128)S(1)} %copy-done.2, s32[1]{0:T(128)S(6)} %copy.14.count_ref, s32[2]{0:T(128)S(1)} %pad_add_fusion.chain_ref, f32[48,4096]{1,0:T(8,128)S(1)} %get-tuple-element.23.field_ref, ...), custom_call_target="tpu_custom_call" | custom-call | tf_op jit(solution)/shard_map/second/pallas_call | solution.py:428
  26.0 1.3 %collective-permute-start.3 = (f32[48,512]{1,0:T(8,128)S(1)}, f32[48,512]{1,0:T(8,128)S(1)}, u32[]{:S(2)}, u32[]{:S(2)}) collective-permute-start(f32[48,512]{1,0:T(8,128)S(1)} %relay.1), channel_id=1, source_target_pairs={{0,4},{4,8},{8,12},{12,16},{16,20},{20,24},{24,28},{1,5},{5,9},{9,... | collective-permute-start | bytes 294920 | tf_op jit(solution)/shard_map/ppermute | solution.py:23
  27.3 5.3 %all-to-all-start = ((f32[32,1,256]{2,1,0:T(1,128)}), f32[32,1,256]{2,1,0:T(1,128)S(1)}, u32[]{:S(2)}, u32[]{:S(2)}) async-start(f32[32,1,256]{2,1,0:T(1,128)} %get-tuple-element.36), calls=%async_computation | async-start | bytes 65536 | tf_op jit(solution)/shard_map/all_to_all | solution.py:439
  32.7 7.2 %all-to-all-done = f32[32,1,256]{2,1,0:T(1,128)S(1)} async-done(((f32[32,1,256]{2,1,0:T(1,128)}), f32[32,1,256]{2,1,0:T(1,128)S(1)}, u32[]{:S(2)}, u32[]{:S(2)}) %all-to-all-start) | async-done | bytes 32800 | tf_op jit(solution)/shard_map/all_to_all | solution.py:439
  39.9 0.0 collective-permute-done.3.far_received_ref
  39.9 1.7 %last.1 = (f32[48,4096]{1,0:T(8,128)}, f32[48,4096]{1,0:T(8,128)}, f32[1,16]{1,0:T(1,128)}) custom-call(s32[1]{0:T(128)} %bitcast.place_ref, f32[32,256]{1,0:T(8,128)S(1)} %bitcast.12, f32[48,4096]{1,0:T(8,128)S(1)} %get-tuple-element.23.field_ref, f32[48,4096]{1,0:T(8,128)S(1)} %get-tuple-element.27.image_ref, f32[48,512]{1,0:T(8,128)S(1)} %get-tuple-element.37.lead_ref, ...), custom_call_target="tpu_custom_call" | custom-call | tf_op jit(solution)/shard_map/last/pallas_call | solution.py:443
  (2 shorter events, 0.0 us)
Async XLA Ops:
  1.5 7.6 %collective-permute-start = (f32[3,16,512]{2,1,0:T(8,128)S(1)}, f32[3,16,512]{2,1,0:T(8,128)S(1)}, u32[]{:S(2)}, u32[]{:S(2)}) collective-permute-start(f32[3,16,512]{2,1,0:T(8,128)S(1)} %slice.3), channel_id=1, source_target_pairs={{4,0},{8,4},{12,8},{16,12},{20,16},{24,20},{28,24},{5,1},{9,5},{13... | collective-permute-start | bytes 294920 | tf_op jit(solution)/shard_map/ppermute | solution.py:23
  9.2 0.7 %copy-start.1 = (s32[64]{0:T(128)S(1)}, s32[64]{0:T(128)}, u32[]{:S(2)}) copy-start(s32[64]{0:T(128)} %local_ref.3) | copy-start | bytes 772
  9.2 0.7 %copy-start.2 = (s32[64]{0:T(128)S(1)}, s32[64]{0:T(128)}, u32[]{:S(2)}) copy-start(s32[64]{0:T(128)} %partner_ref.3) | copy-start | bytes 772
  9.9 8.2 %copy-start = (f32[3,4096]{1,0:T(4,128)S(1)}, f32[3,4096]{1,0:T(4,128)}, u32[]{:S(2)}) copy-start(f32[3,4096]{1,0:T(4,128)} %weight_ref.3) | copy-start | bytes 147460
  12.4 6.6 %collective-permute-start.1 = (f32[48,512]{1,0:T(8,128)S(1)}, f32[48,512]{1,0:T(8,128)S(1)}, u32[]{:S(2)}, u32[]{:S(2)}) collective-permute-start(f32[48,512]{1,0:T(8,128)S(1)} %get-tuple-element.29), channel_id=1, source_target_pairs={{0,4},{4,0},{8,12},{12,8},{16,20},{20,16},{24,28},{28,24},{1,5},{5... | collective-permute-start | bytes 294920 | tf_op jit(solution)/shard_map/ppermute | solution.py:32
  15.2 7.3 %collective-permute-start.2 = (f32[48,512]{1,0:T(8,128)S(1)}, f32[48,512]{1,0:T(8,128)S(1)}, u32[]{:S(2)}, u32[]{:S(2)}) collective-permute-start(f32[48,512]{1,0:T(8,128)S(1)} %get-tuple-element.30), channel_id=1, source_target_pairs={{4,8},{8,4},{12,16},{16,12},{20,24},{24,20},{28,0},{0,28},{5,9},{9... | collective-permute-start | bytes 294920 | tf_op jit(solution)/shard_map/ppermute | solution.py:32
  26.0 13.9 %collective-permute-start.3 = (f32[48,512]{1,0:T(8,128)S(1)}, f32[48,512]{1,0:T(8,128)S(1)}, u32[]{:S(2)}, u32[]{:S(2)}) collective-permute-start(f32[48,512]{1,0:T(8,128)S(1)} %relay.1), channel_id=1, source_target_pairs={{0,4},{4,8},{8,12},{12,16},{16,20},{20,24},{24,28},{1,5},{5,9},{9,... | collective-permute-start | bytes 294920 | tf_op jit(solution)/shard_map/ppermute | solution.py:23
  27.3 12.6 %all-to-all-start = ((f32[32,1,256]{2,1,0:T(1,128)}), f32[32,1,256]{2,1,0:T(1,128)S(1)}, u32[]{:S(2)}, u32[]{:S(2)}) async-start(f32[32,1,256]{2,1,0:T(1,128)} %get-tuple-element.36), calls=%async_computation | async-start | bytes 65536 | tf_op jit(solution)/shard_map/all_to_all | solution.py:439

commit v3 on v2

--- a/solution.py
+++ b/solution.py
@@ -12,9 +12,10 @@
 LANES = 128
 MOMENT_LANES = 256
 VMEM = pl.BlockSpec(memory_space=pltpu.VMEM)
+HBM = pl.BlockSpec(memory_space=pltpu.HBM)
 SMEM = pl.BlockSpec(memory_space=pltpu.SMEM)
-HBM = pl.BlockSpec(memory_space=pltpu.HBM)
 SUMS = 12
+CHUNKS = 4
 
 
 def shifted(value, axis, by):
@@ -48,6 +49,29 @@
 
 def put(ref, index, value):
     ref[:, index * LANES : (index + 1) * LANES] = value
+
+
+def fetch(sources, targets, sems):
+    copies = [
+        pltpu.make_async_copy(source, target, sems.at[place])
+        for place, (source, target) in enumerate(zip(sources, targets))
+    ]
+    for copy in copies:
+        copy.start()
+    return copies
+
+
+def chunked(sources, targets, sems, chunk):
+    copies = []
+    for start in range(0, targets[0].shape[1], chunk):
+        lanes = pl.ds(start, chunk)
+        group = []
+        for source, target in zip(sources, targets):
+            group.append(
+                pltpu.make_async_copy(source.at[:, lanes], target.at[:, lanes], sems.at[len(copies) * len(targets) + len(group)])
+            )
+        copies.append(group)
+    return copies
 
 
 def block_diagonal(high, low):
@@ -110,37 +134,44 @@
 
 
 def prepare_kernel(
-    field_hbm, stiff_hbm, contact_hbm,
+    field_hbm, stiff_hbm, contact_hbm, local_hbm, partner_hbm,
     field_ref, elastic_ref, stiff_high_ref, stiff_low_ref, contact_high_ref, contact_low_ref,
-    stiff_ref, contact_ref, sems,
+    local_ref, partner_ref,
+    stiff_ref, contact_ref, sems, contact_sems, table_sems,
 ):
-    patches = field_ref.shape[1] // PN
-    copies = [
-        pltpu.make_async_copy(field_hbm, field_ref, sems.at[0]),
-        pltpu.make_async_copy(stiff_hbm, stiff_ref, sems.at[1]),
-        pltpu.make_async_copy(contact_hbm, contact_ref, sems.at[2]),
-    ]
-    for copy in copies:
-        copy.start()
-    copies[0].wait()
-    copies[1].wait()
-    for index in range(patches // 2):
-        field_tile = tile(field_ref, index)
-        high, low = split(tile(stiff_ref, index))
-        put(stiff_high_ref, index, high)
-        put(stiff_low_ref, index, low)
-        put(elastic_ref, index, pair_product(field_tile, high, low))
-    copies[2].wait()
-    for index in range(contact_ref.shape[1] // LANES):
-        high, low = split(tile(contact_ref, index))
-        put(contact_high_ref, index, high)
-        put(contact_low_ref, index, low)
+    chunk = stiff_ref.shape[1] // CHUNKS
+    tiles = chunk // LANES
+    copies = chunked((field_hbm, stiff_hbm), (field_ref, stiff_ref), sems, chunk)
+    contact_copies = chunked((contact_hbm,), (contact_ref,), contact_sems, chunk)
+    for group in copies + contact_copies:
+        for copy in group:
+            copy.start()
+    tables = fetch((local_hbm, partner_hbm), (local_ref, partner_ref), table_sems)
+    for place, group in enumerate(copies):
+        for copy in group:
+            copy.wait()
+        for index in range(place * tiles, (place + 1) * tiles):
+            high, low = split(tile(stiff_ref, index))
+            put(stiff_high_ref, index, high)
+            put(stiff_low_ref, index, low)
+            put(elastic_ref, index, pair_product(tile(field_ref, index), high, low))
+    for place, group in enumerate(contact_copies):
+        for copy in group:
+            copy.wait()
+        for index in range(place * tiles, (place + 1) * tiles):
+            high, low = split(tile(contact_ref, index))
+            put(contact_high_ref, index, high)
+            put(contact_low_ref, index, low)
+    for copy in tables:
+        copy.wait()
 
 
 def couple_kernel(
-    local_ref, partner_ref, count_ref, chain_ref, field_ref, elastic_ref, halo_ref, high_ref, low_ref,
-    image_ref, spread_ref, even_ref, odd_ref, twin_ref, total_ref,
+    count_ref, local_vmem, partner_vmem, field_ref, elastic_ref, halo_ref, high_ref, low_ref,
+    image_ref, spread_ref, even_ref, odd_ref,
+    local_ref, partner_ref, sems, twin_ref, total_ref,
 ):
+    tables = fetch((local_vmem, partner_vmem), (local_ref, partner_ref), sems)
     patches = image_ref.shape[1] // PN
     lead = NB // 2
     clear(total_ref)
@@ -148,8 +179,10 @@
         fill_twins(tile(field_ref, index), twin_ref, 2 * index)
     for index in range(lead):
         fill_twins(tile(halo_ref, index), twin_ref, patches + 2 * index)
+    for copy in tables:
+        copy.wait()
     contacts(twin_ref, high_ref, low_ref, local_ref, partner_ref, count_ref, total_ref)
-    even = chain_ref[0] % 2 == 0
+    even = lax.axis_index("dom") % 2 == 0
     for index in range(patches // 2):
         value = tile(elastic_ref, index) + folded(total_ref, 2 * index)
         put(image_ref, index, value)
@@ -234,14 +267,16 @@
 
 
 def second_kernel(
-    local_ref, partner_ref, count_ref, chain_ref, field_ref, halo_ref, image_ref, spread_ref, even_ref, odd_ref,
+    count_ref, local_vmem, partner_vmem, field_ref, halo_ref, image_ref, spread_ref, even_ref, odd_ref,
     stiff_high_ref, stiff_low_ref, contact_high_ref, contact_low_ref, weight_ref, sums_ref, trial_ref, elastic_ref,
-    twice_ref, lead_ref, moment_ref, far_spread_ref, twin_ref, total_ref, *, columns,
+    twice_ref, lead_ref, moment_ref, far_spread_ref,
+    local_ref, partner_ref, sems, twin_ref, total_ref, *, columns,
 ):
+    tables = fetch((local_vmem, partner_vmem), (local_ref, partner_ref), sems)
     rows = field_ref.shape[0]
     patches = field_ref.shape[1] // PN
     lead = NB // 2
-    place, last = chain_ref[0], chain_ref[1] - 1
+    place, last = lax.axis_index("dom"), lax.axis_size("dom") - 1
     even = place % 2 == 0
     trial = trial_ref[...]
     trial_rows = jnp.concatenate([trial] * (rows // columns), axis=0)
@@ -269,6 +304,8 @@
         sums.add(3, rest * image_tile)
         sums.add(4, image_tile * image_tile)
         sums.add(11, weights_of(weight_ref, index, rows) * image_tile)
+    for copy in tables:
+        copy.wait()
     contacts(twin_ref, contact_high_ref, contact_low_ref, local_ref, partner_ref, count_ref, total_ref)
     for index in range(patches // 2):
         image_tile = tile(lead_ref if index < lead else image_ref, index)
@@ -303,11 +340,7 @@
     out_ref[...] = value_ref[...]
 
 
-def last_kernel(
-    place_ref, moment_ref, field_ref, image_ref, lead_ref, twice_ref, far_received_ref,
-    solution_ref, residual_ref, step_ref, *, columns, groups,
-):
-    rows = field_ref.shape[0]
+def scale_kernel(moment_ref, scale_ref, step_ref, *, columns, groups):
     devices = moment_ref.shape[0]
 
     def moment(place):
@@ -349,7 +382,7 @@
     counted = jnp.where((lane < columns) & (row < groups), gradient * gradient, 0.0)
     square_total = jnp.sum(jnp.sum(counted, axis=1, keepdims=True), axis=0, keepdims=True)
     scaled = gradient / jnp.sqrt(square_total / (columns * groups) + 1e-06)
-    mine = row == place_ref[0]
+    mine = row == lax.axis_index("col")
 
     def own(value):
         return jnp.sum(jnp.where(mine, value, 0.0), axis=0, keepdims=True)
@@ -357,17 +390,35 @@
     step_ref[...] = own(scaled)[:, :columns]
     pair = jnp.concatenate([own(on_field), own(on_image), jnp.zeros((LANES - 2, LANES), jnp.float32)], axis=0)
     flipped = jnp.transpose(pair)[:columns]
-    field_rows = jnp.concatenate([jnp.broadcast_to(flipped[:, 0:1], (columns, LANES))] * (rows // columns), axis=0)
-    image_rows = jnp.concatenate([jnp.broadcast_to(flipped[:, 1:2], (columns, LANES))] * (rows // columns), axis=0)
-    for index in range(field_ref.shape[1] // LANES):
-        field_tile = tile(field_ref, index)
-        image_tile = tile(lead_ref if index < NB // 2 else image_ref, index)
-        twice_tile = tile(twice_ref, index)
-        if index < NB // 2:
-            twice_tile = twice_tile + tile(far_received_ref, index)
-        where = slice(index * LANES, (index + 1) * LANES)
-        solution_ref[:, where] = field_rows * field_tile + image_rows * image_tile
-        residual_ref[:, where] = field_tile - field_rows * image_tile - image_rows * twice_tile
+    scale_ref[:columns] = jnp.broadcast_to(flipped[:, 0:1], (columns, LANES))
+    scale_ref[columns:] = jnp.broadcast_to(flipped[:, 1:2], (columns, LANES))
+
+
+def last_kernel(
+    scale_ref, field_ref, image_ref, lead_ref, twice_ref, far_received_ref,
+    solution_hbm, residual_hbm, solution_ref, residual_ref, sems,
+):
+    rows = field_ref.shape[0]
+    columns = scale_ref.shape[0] // 2
+    field_rows = jnp.concatenate([scale_ref[:columns]] * (rows // columns), axis=0)
+    image_rows = jnp.concatenate([scale_ref[columns:]] * (rows // columns), axis=0)
+    chunk = field_ref.shape[1] // CHUNKS
+    tiles = chunk // LANES
+    copies = chunked((solution_ref, residual_ref), (solution_hbm, residual_hbm), sems, chunk)
+    for place, group in enumerate(copies):
+        for index in range(place * tiles, (place + 1) * tiles):
+            field_tile = tile(field_ref, index)
+            image_tile = tile(lead_ref if index < NB // 2 else image_ref, index)
+            twice_tile = tile(twice_ref, index)
+            if index < NB // 2:
+                twice_tile = twice_tile + tile(far_received_ref, index)
+            put(solution_ref, index, field_rows * field_tile + image_rows * image_tile)
+            put(residual_ref, index, field_tile - field_rows * image_tile - image_rows * twice_tile)
+        for copy in group:
+            copy.start()
+    for group in copies:
+        for copy in group:
+            copy.wait()
 
 
 def shards(right_side, stiffness, contact, pair_local, pair_partner, pair_count, objective_weight):
@@ -385,33 +436,37 @@
     shape = jax.ShapeDtypeStruct
     wide = shape((rows, nodes), f32)
     narrow = shape((rows, width), f32)
-    scratch = [pltpu.VMEM((patches + NB, rows, LANES), f32)] * 2
+    tables = (shape(pair_local.shape, jnp.int32), shape(pair_partner.shape, jnp.int32))
+    scratch = [pltpu.SMEM(table.shape, jnp.int32) for table in tables]
+    scratch += [pltpu.SemaphoreType.DMA((len(tables),))]
+    scratch += [pltpu.VMEM((patches + NB, rows, LANES), f32)] * 2
     parts = [shape(block.shape, jnp.bfloat16) for block in (stiffness, stiffness, contact, contact)]
 
     field_hbm = right_side.reshape(rows, nodes)
     halo = shifted(right_side[:, :, :width], "dom", -1).reshape(rows, width)
-    chain = jnp.stack([lax.axis_index("dom").astype(jnp.int32), jnp.int32(chain_length)])
-    tables = (pair_local, pair_partner, pair_count, chain)
-    field, elastic, stiff_high, stiff_low, contact_high, contact_low = call(
+    given = (field_hbm, stiffness, contact, pair_local, pair_partner)
+    field, elastic, stiff_high, stiff_low, contact_high, contact_low, *tables = call(
         prepare_kernel,
-        out_shape=(wide, wide, *parts),
-        in_specs=[HBM] * 3,
-        out_specs=(VMEM,) * 6,
+        out_shape=(wide, wide, *parts, *tables),
+        in_specs=[HBM] * 5,
+        out_specs=(VMEM,) * 8,
         scratch_shapes=[
             pltpu.VMEM(stiffness.shape, f32),
             pltpu.VMEM(contact.shape, f32),
-            pltpu.SemaphoreType.DMA((3,)),
+            pltpu.SemaphoreType.DMA((2 * CHUNKS,)),
+            pltpu.SemaphoreType.DMA((CHUNKS,)),
+            pltpu.SemaphoreType.DMA((2,)),
         ],
         name="prepare",
-    )(*(pltpu.with_memory_space_constraint(value, pltpu.HBM) for value in (field_hbm, stiffness, contact)))
+    )(*(pltpu.with_memory_space_constraint(value, pltpu.HBM) for value in given))
     image, spread, even, odd = call(
         couple_kernel,
         out_shape=(wide, narrow, narrow, narrow),
-        in_specs=[SMEM] * 4 + [VMEM] * 5,
+        in_specs=[SMEM] + [VMEM] * 7,
         out_specs=(VMEM,) * 4,
         scratch_shapes=scratch,
         name="couple",
-    )(*tables, field, elastic, halo, contact_high, contact_low)
+    )(pair_count, *tables, field, elastic, halo, contact_high, contact_low)
     even = swapped(even, "dom", False)
     odd = swapped(odd, "dom", True)
     elastic, sums, trial = call(
@@ -428,25 +483,40 @@
     twice, lead, moments, far_spread = call(
         functools.partial(second_kernel, columns=columns),
         out_shape=(wide, narrow, shape((devices, 1, MOMENT_LANES), f32), narrow),
-        in_specs=[SMEM] * 4 + [VMEM] * 14,
+        in_specs=[SMEM] + [VMEM] * 16,
         out_specs=(VMEM,) * 4,
         scratch_shapes=scratch,
         name="second",
     )(
-        *tables, field, halo, image, spread, even, odd, stiff_high, stiff_low, contact_high, contact_low,
+        pair_count, *tables, field, halo, image, spread, even, odd, stiff_high, stiff_low, contact_high, contact_low,
         objective_weight, sums, trial, elastic,
     )
     gathered = lax.all_to_all(moments, ("dom", "col"), 0, 0, tiled=True).reshape(devices, MOMENT_LANES)
-    far_spread = call(relay_kernel, out_shape=narrow, in_specs=[VMEM], out_specs=VMEM, name="relay")(far_spread)
+    far_spread = call(
+        relay_kernel,
+        out_shape=narrow,
+        in_specs=[VMEM],
+        out_specs=VMEM,
+        cost_estimate=pl.CostEstimate(flops=10**9, bytes_accessed=2 * rows * width * 4, transcendentals=0),
+        name="relay",
+    )(far_spread)
     far_received = shifted(far_spread, "dom", 1)
-    place = lax.axis_index("col").astype(jnp.int32).reshape(1)
-    solution_field, residual, step = call(
-        functools.partial(last_kernel, columns=columns, groups=groups),
-        out_shape=(wide, wide, shape((1, columns), f32)),
-        in_specs=[SMEM] + [VMEM] * 6,
-        out_specs=(VMEM,) * 3,
+    scales, step = call(
+        functools.partial(scale_kernel, columns=columns, groups=groups),
+        out_shape=(shape((2 * columns, LANES), f32), shape((1, columns), f32)),
+        in_specs=[VMEM],
+        out_specs=(VMEM,) * 2,
+        cost_estimate=pl.CostEstimate(flops=10**9, bytes_accessed=devices * MOMENT_LANES * 4, transcendentals=0),
+        name="scale",
+    )(gathered)
+    solution_field, residual = call(
+        last_kernel,
+        out_shape=(wide, wide),
+        in_specs=[VMEM] * 6,
+        out_specs=(HBM,) * 2,
+        scratch_shapes=[pltpu.VMEM((rows, nodes), f32)] * 2 + [pltpu.SemaphoreType.DMA((2 * CHUNKS,))],
         name="last",
-    )(place, gathered, field, image, lead, twice, far_received)
+    )(scales, field, image, lead, twice, far_received)
     return (
         solution_field.reshape(right_side.shape),
         residual.reshape(right_side.shape),

time: 41.9 us -> 38.6 us (0.921)
  waiting for transfers between devices: 13.8 us -> 9.81 us
  starting transfers between devices: 13.5 us -> 15 us
  local copies, waits for them, and re-layouts: 1.58 us -> 0.91 us
    all_to_all x1, waiting for transfers between devices: 7.25 us -> 3.55 us  [shards(): lax.all_to_all(moments, ('dom', 'col'), 0, 0, tiled=True)]
    ppermute x2, starting transfers between devices: 2.58 us -> 4.96 us  [shifted(): return lax.ppermute(value, axis, pairs)]
    all_to_all x1, starting transfers between devices: 5.31 us -> 4.27 us  [shards(): lax.all_to_all(moments, ('dom', 'col'), 0, 0, tiled=True)]
    unnamed x7 -> x3, local copies, waits for them, and re-layouts: 0.68 us -> 0.01 us
    pallas_call x3 -> x4, Pallas kernels: 4.39 us -> 4.83 us  [the longest x1 2.83 us: shards(): call(prepare_kernel, out_shape=(wide, wide, *parts, *tables), in_specs=[H...]
  transfers between devices with their start and end apart: 5 -> 5, of which waited for: 3 -> 3; matrix products, arithmetic and copies ran while one was open for 0% -> 0% of each run, Pallas kernels for 9% -> 12%
where the time goes in v3:
time: 38.6 us; the launch traced here: 38.4 us
  starting transfers between devices  15 us (39%)
  Pallas kernels  11.3 us (29%)
  waiting for transfers between devices  9.81 us (25%)
  between operations  1.35 us (3%)
  local copies, waits for them, and re-layouts  0.91 us (2%)
    ppermute x2, starting transfers between devices, swapped(): return lax.ppermute(value, axis, pairs)  5.75 us
    ppermute x2, starting transfers between devices, shifted(): return lax.ppermute(value, axis, pairs)  4.96 us
    all_to_all x1, starting transfers between devices, shards(): lax.all_to_all(moments, ('dom', 'col'), 0, 0, tiled=True)  4.27 us
    all_to_all x1, waiting for transfers between devices, shards(): lax.all_to_all(moments, ('dom', 'col'), 0, 0, tiled=True)  3.55 us
    pallas_call x1, Pallas kernels, shards(): call(functools.partial(second_kernel, columns=columns), out_shape=(wide,...  3.39 us
    ppermute x2, waiting for transfers between devices, swapped(): return lax.ppermute(value, axis, pairs)  3.39 us
    ppermute x2, waiting for transfers between devices, shifted(): return lax.ppermute(value, axis, pairs)  2.87 us
    pallas_call x1, Pallas kernels, shards(): call(prepare_kernel, out_shape=(wide, wide, *parts, *tables), in_specs=[H...  2.83 us
  transfers between devices with their start and end apart: 5, of which 3 were waited for; matrix products, arithmetic and copies ran while one was open for 0% of the time, Pallas kernels for 12%

profile of v3, /device:TPU:0, one launch (start us, length us, event | category | flops | bytes accessed | tf_op | source)
XLA Modules:
  0.0 38.4 jit_solution(1681614976554454532)
XLA Ops:
  0.6 0.9 %slice.3 = f32[3,16,512]{2,1,0:T(8,128)S(1)} slice(f32[3,16,4096]{2,1,0:T(8,128)} %param.7), slice={[0:3], [0:16], [0:512]} | slice | bytes 196608 | tf_op jit(solution)/shard_map/slice | solution.py:446
  1.5 1.3 %collective-permute-start = (f32[3,16,512]{2,1,0:T(8,128)S(1)}, f32[3,16,512]{2,1,0:T(8,128)S(1)}, u32[]{:S(2)}, u32[]{:S(2)}) collective-permute-start(f32[3,16,512]{2,1,0:T(8,128)S(1)} %slice.3), channel_id=1, source_target_pairs={{4,0},{8,4},{12,8},{16,12},{20,16},{24,20},{28,24},{5,1},{9,5},{13... | collective-permute-start | bytes 294920 | tf_op jit(solution)/shard_map/ppermute | solution.py:24
  3.5 2.8 %prepare.1 = (f32[48,4096]{1,0:T(8,128)S(1)}, f32[48,4096]{1,0:T(8,128)S(1)}, bf16[64,4096]{1,0:T(8,128)(2,1)S(1)}, bf16[64,4096]{1,0:T(8,128)(2,1)S(1)}, bf16[6...) custom-call(f32[48,4096]{1,0:T(8,128)} %bitcast.11, ...), custom_call_target="tpu_custom_call" | custom-call | tf_op jit(solution)/shard_map/prepare/pallas_call | solution.py:448
  6.3 2.9 %collective-permute-done = f32[3,16,512]{2,1,0:T(8,128)S(1)} collective-permute-done((f32[3,16,512]{2,1,0:T(8,128)S(1)}, f32[3,16,512]{2,1,0:T(8,128)S(1)}, u32[]{:S(2)}, u32[]{:S(2)}) %collective-permute-start) | collective-permute-done | bytes 98336 | tf_op jit(solution)/shard_map/ppermute | solution.py:24
  9.2 0.0 copy-start
  9.2 2.2 %couple.1 = (f32[48,4096]{1,0:T(8,128)S(1)}, f32[48,512]{1,0:T(8,128)S(1)}, f32[48,512]{1,0:T(8,128)S(1)}, f32[48,512]{1,0:T(8,128)S(1)}) custom-call(s32[1]{0:T(128)S(6)} %copy.14.count_ref, s32[64]{0:T(128)S(1)} %get-tuple-element.26.local_vmem, s32[64]{0:T(128)S(1)} %get-tuple-element.27.partner_vmem, f32[48,4096]{1,0:T(8,128)S(1)} %get-tuple-element.28.field_ref, ...), custom_call_target="tpu_custom_call" | custom-call | tf_op jit(solution)/shard_map/couple/pallas_call | solution.py:462
  11.4 2.8 %collective-permute-start.1 = (f32[48,512]{1,0:T(8,128)S(1)}, f32[48,512]{1,0:T(8,128)S(1)}, u32[]{:S(2)}, u32[]{:S(2)}) collective-permute-start(f32[48,512]{1,0:T(8,128)S(1)} %get-tuple-element.34), channel_id=1, source_target_pairs={{0,4},{4,0},{8,12},{12,8},{16,20},{20,16},{24,28},{28,24},{1,5},{5... | collective-permute-start | bytes 294920 | tf_op jit(solution)/shard_map/ppermute | solution.py:33
  14.1 3.0 %collective-permute-start.2 = (f32[48,512]{1,0:T(8,128)S(1)}, f32[48,512]{1,0:T(8,128)S(1)}, u32[]{:S(2)}, u32[]{:S(2)}) collective-permute-start(f32[48,512]{1,0:T(8,128)S(1)} %get-tuple-element.35), channel_id=1, source_target_pairs={{4,8},{8,4},{12,16},{16,12},{20,24},{24,20},{28,0},{0,28},{5,9},{9... | collective-permute-start | bytes 294920 | tf_op jit(solution)/shard_map/ppermute | solution.py:33
  17.1 0.0 copy-done
  17.1 0.9 %lift.1 = (f32[48,3584]{1,0:T(8,128)S(1)}, f32[192,128]{1,0:T(8,128)S(1)}, f32[16,128]{1,0:T(8,128)S(1)}) custom-call(f32[48,4096]{1,0:T(8,128)S(1)} %get-tuple-element.28.field_ref, f32[48,4096]{1,0:T(8,128)S(1)} %get-tuple-element.32.image_ref, bf16[64,4096]{1,0:T(8,128)(2,1)S(1)} %get-tuple-element.36.stiff_high_ref, ...), custom_call_target="tpu_custom_call" | custom-call | tf_op jit(solution)/shard_map/lift/pallas_call | solution.py:472
  18.1 0.0 collective-permute-done.1.even_ref
  18.1 3.4 %collective-permute-done.2.odd_ref = f32[48,512]{1,0:T(8,128)S(1)} collective-permute-done((f32[48,512]{1,0:T(8,128)S(1)}, f32[48,512]{1,0:T(8,128)S(1)}, u32[]{:S(2)}, u32[]{:S(2)}) %collective-permute-start.2) | collective-permute-done | bytes 98336 | tf_op jit(solution)/shard_map/ppermute | solution.py:33
  21.5 3.4 %second.1 = (f32[48,4096]{1,0:T(8,128)S(1)}, f32[48,512]{1,0:T(8,128)S(1)}, f32[32,1,256]{2,1,0:T(1,128)}, f32[48,512]{1,0:T(8,128)S(1)}) custom-call(s32[1]{0:T(128)S(6)} %copy.14.count_ref, s32[64]{0:T(128)S(1)} %get-tuple-element.26.local_vmem, s32[64]{0:T(128)S(1)} %get-tuple-element.27.partner_vmem, f32[48,4096]{1,0:T(8,128)S(1)} %get-tuple-element.28.field_ref, ...), custom_call_target="tpu_custom_call" | custom-call | tf_op jit(solution)/shard_map/second/pallas_call | solution.py:483
  24.9 4.3 %all-to-all-start = ((f32[32,1,256]{2,1,0:T(1,128)}), f32[32,1,256]{2,1,0:T(1,128)S(1)}, u32[]{:S(2)}, u32[]{:S(2)}) async-start(f32[32,1,256]{2,1,0:T(1,128)} %get-tuple-element.41), calls=%async_computation | async-start | bytes 65536 | tf_op jit(solution)/shard_map/all_to_all | solution.py:494
  29.1 3.7 %collective-permute-start.3 = (f32[48,512]{1,0:T(8,128)S(1)}, f32[48,512]{1,0:T(8,128)S(1)}, u32[]{:S(2)}, u32[]{:S(2)}) collective-permute-start(f32[48,512]{1,0:T(8,128)S(1)} %relay.1), channel_id=1, source_target_pairs={{0,4},{4,8},{8,12},{12,16},{16,20},{20,24},{24,28},{1,5},{5,9},{9,... | collective-permute-start | bytes 294920 | tf_op jit(solution)/shard_map/ppermute | solution.py:24
  32.8 3.5 %all-to-all-done = f32[32,1,256]{2,1,0:T(1,128)S(1)} async-done(((f32[32,1,256]{2,1,0:T(1,128)}), f32[32,1,256]{2,1,0:T(1,128)S(1)}, u32[]{:S(2)}, u32[]{:S(2)}) %all-to-all-start) | async-done | bytes 32800 | tf_op jit(solution)/shard_map/all_to_all | solution.py:494
  36.4 0.7 %scale.1 = (f32[32,128]{1,0:T(8,128)S(1)}, f32[1,16]{1,0:T(1,128)}) custom-call(f32[32,256]{1,0:T(8,128)S(1)} %bitcast.10), custom_call_target="tpu_custom_call" | custom-call | flops 1000000000 | bytes 32768 | tf_op jit(solution)/shard_map/scale/pallas_call | solution.py:504
  37.1 0.0 collective-permute-done.3.far_received_ref
  37.1 1.2 %last.1 = (f32[48,4096]{1,0:T(8,128)}, f32[48,4096]{1,0:T(8,128)}) custom-call(f32[32,128]{1,0:T(8,128)S(1)} %get-tuple-element.42.scale_ref, f32[48,4096]{1,0:T(8,128)S(1)} %get-tuple-element.28.field_ref, f32[48,4096]{1,0:T(8,128)S(1)} %get-tuple-element.32.image_ref, f32[48,512]{1,0:T(8,128)S(1)} %get-tuple-element.43.lead_ref, ...), custom_call_target="tpu_custom_call" | custom-call | tf_op jit(solution)/shard_map/last/pallas_call | solution.py:512
  (2 shorter events, 0.0 us)
Async XLA Ops:
  1.5 7.6 %collective-permute-start = (f32[3,16,512]{2,1,0:T(8,128)S(1)}, f32[3,16,512]{2,1,0:T(8,128)S(1)}, u32[]{:S(2)}, u32[]{:S(2)}) collective-permute-start(f32[3,16,512]{2,1,0:T(8,128)S(1)} %slice.3), channel_id=1, source_target_pairs={{4,0},{8,4},{12,8},{16,12},{20,16},{24,20},{28,24},{5,1},{9,5},{13... | collective-permute-start | bytes 294920 | tf_op jit(solution)/shard_map/ppermute | solution.py:24
  9.2 7.9 %copy-start = (f32[3,4096]{1,0:T(4,128)S(1)}, f32[3,4096]{1,0:T(4,128)}, u32[]{:S(2)}) copy-start(f32[3,4096]{1,0:T(4,128)} %weight_ref.3) | copy-start | bytes 147460
  11.4 6.7 %collective-permute-start.1 = (f32[48,512]{1,0:T(8,128)S(1)}, f32[48,512]{1,0:T(8,128)S(1)}, u32[]{:S(2)}, u32[]{:S(2)}) collective-permute-start(f32[48,512]{1,0:T(8,128)S(1)} %get-tuple-element.34), channel_id=1, source_target_pairs={{0,4},{4,0},{8,12},{12,8},{16,20},{20,16},{24,28},{28,24},{1,5},{5... | collective-permute-start | bytes 294920 | tf_op jit(solution)/shard_map/ppermute | solution.py:33
  14.1 7.3 %collective-permute-start.2 = (f32[48,512]{1,0:T(8,128)S(1)}, f32[48,512]{1,0:T(8,128)S(1)}, u32[]{:S(2)}, u32[]{:S(2)}) collective-permute-start(f32[48,512]{1,0:T(8,128)S(1)} %get-tuple-element.35), channel_id=1, source_target_pairs={{4,8},{8,4},{12,16},{16,12},{20,24},{24,20},{28,0},{0,28},{5,9},{9... | collective-permute-start | bytes 294920 | tf_op jit(solution)/shard_map/ppermute | solution.py:33
  24.9 11.5 %all-to-all-start = ((f32[32,1,256]{2,1,0:T(1,128)}), f32[32,1,256]{2,1,0:T(1,128)S(1)}, u32[]{:S(2)}, u32[]{:S(2)}) async-start(f32[32,1,256]{2,1,0:T(1,128)} %get-tuple-element.41), calls=%async_computation | async-start | bytes 65536 | tf_op jit(solution)/shard_map/all_to_all | solution.py:494
  29.1 8.0 %collective-permute-start.3 = (f32[48,512]{1,0:T(8,128)S(1)}, f32[48,512]{1,0:T(8,128)S(1)}, u32[]{:S(2)}, u32[]{:S(2)}) collective-permute-start(f32[48,512]{1,0:T(8,128)S(1)} %relay.1), channel_id=1, source_target_pairs={{0,4},{4,8},{8,12},{12,16},{16,20},{20,24},{24,28},{1,5},{5,9},{9,... | collective-permute-start | bytes 294920 | tf_op jit(solution)/shard_map/ppermute | solution.py:24

commit v4 on v3

--- a/solution.py
+++ b/solution.py
@@ -14,7 +14,7 @@
 VMEM = pl.BlockSpec(memory_space=pltpu.VMEM)
 HBM = pl.BlockSpec(memory_space=pltpu.HBM)
 SMEM = pl.BlockSpec(memory_space=pltpu.SMEM)
-SUMS = 12
+SUMS = 10
 CHUNKS = 4
 
 
@@ -24,13 +24,18 @@
     return lax.ppermute(value, axis, pairs)
 
 
-def swapped(value, axis, odd):
-    count = lax.axis_size(axis)
+def swapped(value, odd):
+    count, groups = lax.axis_size("dom"), lax.axis_size("col")
     pairs = []
-    for low in range(1 if odd else 0, count, 2):
-        high = (low + 1) % count
-        pairs += [(low, high), (high, low)]
-    return lax.ppermute(value, axis, pairs)
+    for place in range(count):
+        partner = place + 1 if (place % 2 == 1) == odd else place - 1
+        for column in range(groups):
+            if 0 <= partner < count:
+                pairs.append((place * groups + column, partner * groups + column))
+            else:
+                beside = column ^ 1 if column ^ 1 < groups else column
+                pairs.append((place * groups + column, place * groups + beside))
+    return lax.ppermute(value, ("dom", "col"), pairs)
 
 
 def left_half(shape):
@@ -97,27 +102,24 @@
     twin_ref[patch + 1] = jnp.where(left, swapped, field_tile)
 
 
-def contacts(twin_ref, high_ref, low_ref, local_ref, partner_ref, count_ref, total_ref):
-    rows = twin_ref.shape[1]
-    left = left_half((rows, LANES))
+def slot_forces(twin_ref, high_ref, low_ref, local_ref, partner_ref, count_ref, step):
+    slot = 2 * step
     live_count = count_ref[0]
-    for step in range(high_ref.shape[1] // LANES):
-        slot = 2 * step
-        first_a, first_b = local_ref[slot], partner_ref[slot]
-        second_a, second_b = local_ref[slot + 1], partner_ref[slot + 1]
-        first_live = jnp.where(slot < live_count, 1.0, 0.0)
-        second_live = jnp.where(slot + 1 < live_count, 1.0, 0.0)
-        first_gap = (twin_ref[first_a] - twin_ref[first_b]) * first_live
-        second_gap = (twin_ref[second_a] - twin_ref[second_b]) * second_live
-        force = pair_product(
-            jnp.where(left, first_gap, second_gap), tile(high_ref, step), tile(low_ref, step)
-        )
-        first_force = jnp.where(left, force, 0.0)
-        second_force = jnp.where(left, 0.0, force)
-        total_ref[first_a] = total_ref[first_a] + first_force
-        total_ref[first_b] = total_ref[first_b] - first_force
-        total_ref[second_a] = total_ref[second_a] + second_force
-        total_ref[second_b] = total_ref[second_b] - second_force
+    first_live = jnp.where(slot < live_count, 1.0, 0.0)
+    second_live = jnp.where(slot + 1 < live_count, 1.0, 0.0)
+    first_gap = (twin_ref[local_ref[slot]] - twin_ref[partner_ref[slot]]) * first_live
+    second_gap = (twin_ref[local_ref[slot + 1]] - twin_ref[partner_ref[slot + 1]]) * second_live
+    gap = jnp.where(left_half(first_gap.shape), first_gap, second_gap)
+    return gap, pair_product(gap, tile(high_ref, step), tile(low_ref, step))
+
+
+def scatter(force, local_ref, partner_ref, total_ref, step):
+    slot = 2 * step
+    left = left_half(force.shape)
+    for number, half in ((slot, jnp.where(left, force, 0.0)), (slot + 1, jnp.where(left, 0.0, force))):
+        patch, partner = local_ref[number], partner_ref[number]
+        total_ref[patch] = total_ref[patch] + half
+        total_ref[partner] = total_ref[partner] - half
 
 
 def folded(total_ref, patch):
@@ -168,29 +170,31 @@
 
 def couple_kernel(
     count_ref, local_vmem, partner_vmem, field_ref, elastic_ref, halo_ref, high_ref, low_ref,
-    image_ref, spread_ref, even_ref, odd_ref,
-    local_ref, partner_ref, sems, twin_ref, total_ref,
+    total_ref, gap_ref, force_ref, own_ref, spread_ref, even_ref, odd_ref,
+    local_ref, partner_ref, sems, twin_ref,
 ):
     tables = fetch((local_vmem, partner_vmem), (local_ref, partner_ref), sems)
-    patches = image_ref.shape[1] // PN
-    lead = NB // 2
+    patches = field_ref.shape[1] // PN
     clear(total_ref)
     for index in range(patches // 2):
         fill_twins(tile(field_ref, index), twin_ref, 2 * index)
-    for index in range(lead):
+    for index in range(NB // 2):
         fill_twins(tile(halo_ref, index), twin_ref, patches + 2 * index)
     for copy in tables:
         copy.wait()
-    contacts(twin_ref, high_ref, low_ref, local_ref, partner_ref, count_ref, total_ref)
+    for step in range(high_ref.shape[1] // LANES):
+        gap, force = slot_forces(twin_ref, high_ref, low_ref, local_ref, partner_ref, count_ref, step)
+        put(gap_ref, step, gap)
+        put(force_ref, step, force)
+        scatter(force, local_ref, partner_ref, total_ref, step)
     even = lax.axis_index("dom") % 2 == 0
-    for index in range(patches // 2):
+    for index in range(NB // 2):
         value = tile(elastic_ref, index) + folded(total_ref, 2 * index)
-        put(image_ref, index, value)
-        if index < lead:
-            spread = folded(total_ref, patches + 2 * index)
-            put(spread_ref, index, spread)
-            put(even_ref, index, jnp.where(even, spread, value))
-            put(odd_ref, index, jnp.where(even, value, spread))
+        spread = folded(total_ref, patches + 2 * index)
+        put(own_ref, index, value)
+        put(spread_ref, index, spread)
+        put(even_ref, index, jnp.where(even, spread, value))
+        put(odd_ref, index, jnp.where(even, value, spread))
 
 
 def by_column(product, columns):
@@ -230,9 +234,16 @@
     )
 
 
+def add_energy(sums, trial_rows, field_part, field_force, image_part, image_force):
+    rest = field_part - trial_rows * image_part
+    sums.add(5, rest * (field_force - trial_rows * image_force))
+    sums.add(6, rest * image_force)
+    sums.add(7, image_part * image_force)
+
+
 def lift_kernel(
-    field_ref, image_ref, stiff_high_ref, stiff_low_ref, weight_ref,
-    elastic_ref, sums_ref, trial_ref, *, columns,
+    field_ref, total_ref, field_elastic_ref, stiff_high_ref, stiff_low_ref, weight_ref,
+    image_ref, elastic_ref, sums_ref, trial_ref, *, columns,
 ):
     rows = field_ref.shape[0]
     patches = field_ref.shape[1] // PN
@@ -242,15 +253,16 @@
         field_tile = tile(field_ref, index)
         weight_tile = weights_of(weight_ref, index, rows)
         sums.add(0, field_tile * field_tile)
-        sums.add(10, weight_tile * field_tile)
+        sums.add(8, weight_tile * field_tile)
         if index < lead:
             continue
-        image_tile = tile(image_ref, index)
+        image_tile = tile(field_elastic_ref, index) + folded(total_ref, 2 * index)
+        put(image_ref, index - lead, image_tile)
         product = pair_product(image_tile, tile(stiff_high_ref, index), tile(stiff_low_ref, index))
         put(elastic_ref, index - lead, product)
         sums.add(1, field_tile * image_tile)
         sums.add(4, image_tile * image_tile)
-        sums.add(11, weight_tile * image_tile)
+        sums.add(9, weight_tile * image_tile)
     across = jnp.sum(sums.values[1], axis=1, keepdims=True)
     square = jnp.sum(sums.values[4], axis=1, keepdims=True)
     some = square > 0.0
@@ -259,18 +271,22 @@
     trial_ref[...] = trial
     trial_rows = jnp.concatenate([trial] * (rows // columns), axis=0)
     for index in range(lead, patches // 2):
-        image_tile = tile(image_ref, index)
-        rest = tile(field_ref, index) - trial_rows * image_tile
+        field_tile, image_tile = tile(field_ref, index), tile(image_ref, index - lead)
+        rest = field_tile - trial_rows * image_tile
         sums.add(2, rest * rest)
         sums.add(3, rest * image_tile)
+        add_energy(
+            sums, trial_rows, field_tile, tile(field_elastic_ref, index), image_tile, tile(elastic_ref, index - lead)
+        )
     sums.store(sums_ref)
 
 
-def second_kernel(
-    count_ref, local_vmem, partner_vmem, field_ref, halo_ref, image_ref, spread_ref, even_ref, odd_ref,
-    stiff_high_ref, stiff_low_ref, contact_high_ref, contact_low_ref, weight_ref, sums_ref, trial_ref, elastic_ref,
-    twice_ref, lead_ref, moment_ref, far_spread_ref,
-    local_ref, partner_ref, sems, twin_ref, total_ref, *, columns,
+def energy_kernel(
+    count_ref, local_vmem, partner_vmem, field_ref, field_elastic_ref, gap_ref, force_ref, own_ref, spread_ref,
+    even_ref, odd_ref, image_ref, stiff_high_ref, stiff_low_ref, contact_high_ref, contact_low_ref, weight_ref,
+    sums_ref, trial_ref,
+    lead_ref, lead_elastic_ref, image_force_ref, moment_ref,
+    local_ref, partner_ref, sems, twin_ref, *, columns,
 ):
     tables = fetch((local_vmem, partner_vmem), (local_ref, partner_ref), sems)
     rows = field_ref.shape[0]
@@ -282,46 +298,34 @@
     trial_rows = jnp.concatenate([trial] * (rows // columns), axis=0)
     sums = Sums(columns)
     sums.load(sums_ref)
-    far_tiles = []
-    products = []
-    clear(total_ref)
     for index in range(lead, patches // 2):
-        fill_twins(tile(image_ref, index), twin_ref, 2 * index)
+        fill_twins(tile(image_ref, index - lead), twin_ref, 2 * index)
     for index in range(lead):
         first, second = tile(even_ref, index), tile(odd_ref, index)
         received = jnp.where(place > 0, jnp.where(even, second, first), 0.0)
         far_tile = jnp.where(place < last, jnp.where(even, first, second) + tile(spread_ref, index), 0.0)
-        far_tiles.append(far_tile)
         fill_twins(far_tile, twin_ref, patches + 2 * index)
         field_tile = tile(field_ref, index)
-        image_tile = tile(image_ref, index) + received
+        image_tile = tile(own_ref, index) + received
         put(lead_ref, index, image_tile)
         fill_twins(image_tile, twin_ref, 2 * index)
-        products.append(pair_product(image_tile, tile(stiff_high_ref, index), tile(stiff_low_ref, index)))
+        product = pair_product(image_tile, tile(stiff_high_ref, index), tile(stiff_low_ref, index))
+        put(lead_elastic_ref, index, product)
         rest = field_tile - trial_rows * image_tile
         sums.add(1, field_tile * image_tile)
         sums.add(2, rest * rest)
         sums.add(3, rest * image_tile)
         sums.add(4, image_tile * image_tile)
-        sums.add(11, weights_of(weight_ref, index, rows) * image_tile)
+        sums.add(9, weights_of(weight_ref, index, rows) * image_tile)
+        add_energy(sums, trial_rows, field_tile, tile(field_elastic_ref, index), image_tile, product)
     for copy in tables:
         copy.wait()
-    contacts(twin_ref, contact_high_ref, contact_low_ref, local_ref, partner_ref, count_ref, total_ref)
-    for index in range(patches // 2):
-        image_tile = tile(lead_ref if index < lead else image_ref, index)
-        product = products[index] if index < lead else tile(elastic_ref, index - lead)
-        twice_tile = product + folded(total_ref, 2 * index)
-        put(twice_ref, index, twice_tile)
-        rest = tile(field_ref, index) - trial_rows * image_tile
-        image_rest = image_tile - trial_rows * twice_tile
-        sums.add(5, rest * image_rest)
-        sums.add(6, rest * twice_tile + image_tile * image_rest)
-        sums.add(7, image_tile * twice_tile)
-    for index in range(lead):
-        far_spread = folded(total_ref, patches + 2 * index)
-        put(far_spread_ref, index, far_spread)
-        sums.add(8, (tile(halo_ref, index) - trial_rows * far_tiles[index]) * far_spread)
-        sums.add(9, far_tiles[index] * far_spread)
+    for step in range(contact_high_ref.shape[1] // LANES):
+        gap, force = slot_forces(
+            twin_ref, contact_high_ref, contact_low_ref, local_ref, partner_ref, count_ref, step
+        )
+        put(image_force_ref, step, force)
+        add_energy(sums, trial_rows, tile(gap_ref, step), tile(force_ref, step), gap, force)
     lane = lax.broadcasted_iota(jnp.int32, (columns, LANES), 1)
     table = jnp.where(lane == SUMS, trial, 0.0)
     for number in range(SUMS):
@@ -336,8 +340,27 @@
         )
 
 
-def relay_kernel(value_ref, out_ref):
-    out_ref[...] = value_ref[...]
+def settle_kernel(
+    local_vmem, partner_vmem, force_ref,
+    total_ref, far_spread_ref,
+    local_ref, partner_ref, sems,
+):
+    tables = fetch((local_vmem, partner_vmem), (local_ref, partner_ref), sems)
+    patches = total_ref.shape[0] - NB
+    clear(total_ref)
+    for copy in tables:
+        copy.wait()
+    for step in range(force_ref.shape[1] // LANES):
+        scatter(tile(force_ref, step), local_ref, partner_ref, total_ref, step)
+    for index in range(NB // 2):
+        put(far_spread_ref, index, folded(total_ref, patches + 2 * index))
+
+
+def gather_kernel(total_ref, lead_elastic_ref, elastic_ref, twice_ref):
+    lead = NB // 2
+    for index in range(twice_ref.shape[1] // LANES):
+        product = tile(lead_elastic_ref, index) if index < lead else tile(elastic_ref, index - lead)
+        put(twice_ref, index, product + folded(total_ref, 2 * index))
 
 
 def scale_kernel(moment_ref, scale_ref, step_ref, *, columns, groups):
@@ -362,21 +385,18 @@
     norm = total(moment(0))
     bend = total(moment(1))
     first_step = norm / bend
-    change = first_step[None] - moment(12)
+    change = first_step[None] - moment(SUMS)
     square = moment(4)
     mixed = moment(3)
     norm_next = total(moment(2) - 2.0 * change * mixed + change * change * square)
     drift = total(mixed - change * square)
-    curve = total(
-        moment(5) - change * moment(6) + change * change * moment(7)
-        - first_step[None] * (moment(8) - change * moment(9))
-    )
+    curve = total(moment(5) - 2.0 * change * moment(6) + change * change * moment(7))
     ratio = norm_next / norm
     bend_next = curve + 2.0 * ratio * drift + ratio * ratio * bend
     second_step = norm_next / bend_next
     on_field = first_step + second_step * (1.0 + ratio)
     on_image = -second_step * first_step
-    gradient = on_field * total(moment(10)) + on_image * total(moment(11))
+    gradient = on_field * total(moment(8)) + on_image * total(moment(9))
     lane = lax.broadcasted_iota(jnp.int32, (8, LANES), 1)
     row = lax.broadcasted_iota(jnp.int32, (8, LANES), 0)
     counted = jnp.where((lane < columns) & (row < groups), gradient * gradient, 0.0)
@@ -408,7 +428,7 @@
     for place, group in enumerate(copies):
         for index in range(place * tiles, (place + 1) * tiles):
             field_tile = tile(field_ref, index)
-            image_tile = tile(lead_ref if index < NB // 2 else image_ref, index)
+            image_tile = tile(lead_ref, index) if index < NB // 2 else tile(image_ref, index - NB // 2)
             twice_tile = tile(twice_ref, index)
             if index < NB // 2:
                 twice_tile = twice_tile + tile(far_received_ref, index)
@@ -431,7 +451,7 @@
     f32 = jnp.float32
     width = NB * PN
     call = functools.partial(
-        pl.pallas_call, compiler_params=pltpu.CompilerParams(vmem_limit_bytes=16 * 1024 * 1024)
+        pl.pallas_call, compiler_params=pltpu.CompilerParams(vmem_limit_bytes=8 * 1024 * 1024)
     )
     shape = jax.ShapeDtypeStruct
     wide = shape((rows, nodes), f32)
@@ -439,13 +459,14 @@
     tables = (shape(pair_local.shape, jnp.int32), shape(pair_partner.shape, jnp.int32))
     scratch = [pltpu.SMEM(table.shape, jnp.int32) for table in tables]
     scratch += [pltpu.SemaphoreType.DMA((len(tables),))]
-    scratch += [pltpu.VMEM((patches + NB, rows, LANES), f32)] * 2
+    twins = pltpu.VMEM((patches + NB, rows, LANES), f32)
+    slots = shape((rows, contact.shape[1]), f32)
     parts = [shape(block.shape, jnp.bfloat16) for block in (stiffness, stiffness, contact, contact)]
 
     field_hbm = right_side.reshape(rows, nodes)
     halo = shifted(right_side[:, :, :width], "dom", -1).reshape(rows, width)
     given = (field_hbm, stiffness, contact, pair_local, pair_partner)
-    field, elastic, stiff_high, stiff_low, contact_high, contact_low, *tables = call(
+    field, field_elastic, stiff_high, stiff_low, contact_high, contact_low, *tables = call(
         prepare_kernel,
         out_shape=(wide, wide, *parts, *tables),
         in_specs=[HBM] * 5,
@@ -459,48 +480,54 @@
         ],
         name="prepare",
     )(*(pltpu.with_memory_space_constraint(value, pltpu.HBM) for value in given))
-    image, spread, even, odd = call(
+    total, gap, force, own, spread, even, odd = call(
         couple_kernel,
-        out_shape=(wide, narrow, narrow, narrow),
+        out_shape=(shape(twins.shape, f32), slots, slots, narrow, narrow, narrow, narrow),
         in_specs=[SMEM] + [VMEM] * 7,
+        out_specs=(VMEM,) * 7,
+        scratch_shapes=scratch + [twins],
+        name="couple",
+    )(pair_count, *tables, field, field_elastic, halo, contact_high, contact_low)
+    even = swapped(even, False)
+    odd = swapped(odd, True)
+    tail = shape((rows, nodes - width), f32)
+    image, elastic, sums, trial = call(
+        functools.partial(lift_kernel, columns=columns),
+        out_shape=(tail, tail, shape((SUMS * columns, LANES), f32), shape((columns, LANES), f32)),
+        in_specs=[VMEM] * 6,
         out_specs=(VMEM,) * 4,
+        name="lift",
+    )(field, total, field_elastic, stiff_high, stiff_low, objective_weight)
+    lead, lead_elastic, image_force, moments = call(
+        functools.partial(energy_kernel, columns=columns),
+        out_shape=(narrow, narrow, slots, shape((devices, 1, MOMENT_LANES), f32)),
+        in_specs=[SMEM] + [VMEM] * 18,
+        out_specs=(VMEM,) * 4,
+        scratch_shapes=scratch + [twins],
+        name="energy",
+    )(
+        pair_count, *tables, field, field_elastic, gap, force, own, spread, even, odd, image,
+        stiff_high, stiff_low, contact_high, contact_low, objective_weight, sums, trial,
+    )
+    gathered = lax.all_to_all(moments, ("dom", "col"), 0, 0, tiled=True).reshape(devices, MOMENT_LANES)
+    total, far_spread = call(
+        settle_kernel,
+        out_shape=(shape(twins.shape, f32), narrow),
+        in_specs=[VMEM] * 3,
+        out_specs=(VMEM,) * 2,
         scratch_shapes=scratch,
-        name="couple",
-    )(pair_count, *tables, field, elastic, halo, contact_high, contact_low)
-    even = swapped(even, "dom", False)
-    odd = swapped(odd, "dom", True)
-    elastic, sums, trial = call(
-        functools.partial(lift_kernel, columns=columns),
-        out_shape=(
-            shape((rows, nodes - width), f32),
-            shape((SUMS * columns, LANES), f32),
-            shape((columns, LANES), f32),
-        ),
-        in_specs=[VMEM] * 5,
-        out_specs=(VMEM,) * 3,
-        name="lift",
-    )(field, image, stiff_high, stiff_low, objective_weight)
-    twice, lead, moments, far_spread = call(
-        functools.partial(second_kernel, columns=columns),
-        out_shape=(wide, narrow, shape((devices, 1, MOMENT_LANES), f32), narrow),
-        in_specs=[SMEM] + [VMEM] * 16,
-        out_specs=(VMEM,) * 4,
-        scratch_shapes=scratch,
-        name="second",
-    )(
-        pair_count, *tables, field, halo, image, spread, even, odd, stiff_high, stiff_low, contact_high, contact_low,
-        objective_weight, sums, trial, elastic,
-    )
-    gathered = lax.all_to_all(moments, ("dom", "col"), 0, 0, tiled=True).reshape(devices, MOMENT_LANES)
-    far_spread = call(
-        relay_kernel,
-        out_shape=narrow,
-        in_specs=[VMEM],
+        cost_estimate=pl.CostEstimate(flops=10**9, bytes_accessed=4 * rows * nodes * 4, transcendentals=0),
+        name="settle",
+    )(*tables, image_force)
+    far_received = shifted(far_spread, "dom", 1)
+    twice = call(
+        gather_kernel,
+        out_shape=wide,
+        in_specs=[VMEM] * 3,
         out_specs=VMEM,
-        cost_estimate=pl.CostEstimate(flops=10**9, bytes_accessed=2 * rows * width * 4, transcendentals=0),
-        name="relay",
-    )(far_spread)
-    far_received = shifted(far_spread, "dom", 1)
+        cost_estimate=pl.CostEstimate(flops=10**9, bytes_accessed=3 * rows * nodes * 4, transcendentals=0),
+        name="gather",
+    )(total, lead_elastic, elastic)
     scales, step = call(
         functools.partial(scale_kernel, columns=columns, groups=groups),
         out_shape=(shape((2 * columns, LANES), f32), shape((1, columns), f32)),

time: 38.6 us -> 35.4 us (0.917)
  waiting for transfers between devices: 9.81 us -> 5.2 us
  Pallas kernels: 11.3 us -> 12.3 us
  local copies, waits for them, and re-layouts: 0.91 us -> 1.76 us
  starting transfers between devices: 15 us -> 14.5 us
    ppermute x2, starting transfers between devices: 5.75 us -> 2.79 us  [swapped(): return lax.ppermute(value, ('dom', 'col'), pairs)]
    ppermute x2, waiting for transfers between devices: 3.39 us -> 0.51 us  [swapped(): return lax.ppermute(value, ('dom', 'col'), pairs)]
    all_to_all x1, starting transfers between devices: 4.27 us -> 6.79 us  [shards(): lax.all_to_all(moments, ('dom', 'col'), 0, 0, tiled=True)]
    all_to_all x1, waiting for transfers between devices: 3.55 us -> 1.83 us  [shards(): lax.all_to_all(moments, ('dom', 'col'), 0, 0, tiled=True)]
    pallas_call x4 -> x5, Pallas kernels: 6.5 us -> 7.47 us  [the longest x1 2.74 us: shards(): call(functools.partial(energy_kernel, columns=columns), out_shape=(narrow...]
    unnamed x3 -> x7, local copies, waits for them, and re-layouts: 0.01 us -> 0.86 us
  transfers between devices with their start and end apart: 5 -> 5, of which waited for: 3 -> 3; matrix products, arithmetic and copies ran while one was open for 0% -> 0% of each run, Pallas kernels for 12% -> 18%
where the time goes in v4:
time: 35.4 us; the launch traced here: 35.2 us
  starting transfers between devices  14.5 us (41%)
  Pallas kernels  12.3 us (35%)
  waiting for transfers between devices  5.2 us (15%)
  local copies, waits for them, and re-layouts  1.76 us (5%)
  between operations  1.38 us (4%)
    all_to_all x1, starting transfers between devices, shards(): lax.all_to_all(moments, ('dom', 'col'), 0, 0, tiled=True)  6.79 us
    ppermute x2, starting transfers between devices, shifted(): return lax.ppermute(value, axis, pairs)  4.96 us
    ppermute x2, waiting for transfers between devices, shifted(): return lax.ppermute(value, axis, pairs)  2.86 us
    pallas_call x1, Pallas kernels, shards(): call(prepare_kernel, out_shape=(wide, wide, *parts, *tables), in_specs=[H...  2.84 us
    ppermute x2, starting transfers between devices, swapped(): return lax.ppermute(value, ('dom', 'col'), pairs)  2.79 us
    pallas_call x1, Pallas kernels, shards(): call(functools.partial(energy_kernel, columns=columns), out_shape=(narrow...  2.74 us
    all_to_all x1, waiting for transfers between devices, shards(): lax.all_to_all(moments, ('dom', 'col'), 0, 0, tiled=True)  1.83 us
    pallas_call x1, Pallas kernels, shards(): call(couple_kernel, out_shape=(shape(twins.shape, f32), slots, slots, nar...  1.81 us
  transfers between devices with their start and end apart: 5, of which 3 were waited for; matrix products, arithmetic and copies ran while one was open for 0% of the time, Pallas kernels for 18%

profile of v4, /device:TPU:0, one launch (start us, length us, event | category | flops | bytes accessed | tf_op | source)
XLA Modules:
  0.0 35.2 jit_solution(11438702084008917616)
XLA Ops:
  0.6 0.9 %slice.3 = f32[3,16,512]{2,1,0:T(8,128)S(1)} slice(f32[3,16,4096]{2,1,0:T(8,128)} %param.7), slice={[0:3], [0:16], [0:512]} | slice | bytes 196608 | tf_op jit(solution)/shard_map/slice | solution.py:467
  1.5 1.3 %collective-permute-start = (f32[3,16,512]{2,1,0:T(8,128)S(1)}, f32[3,16,512]{2,1,0:T(8,128)S(1)}, u32[]{:S(2)}, u32[]{:S(2)}) collective-permute-start(f32[3,16,512]{2,1,0:T(8,128)S(1)} %slice.3), channel_id=1, source_target_pairs={{4,0},{8,4},{12,8},{16,12},{20,16},{24,20},{28,24},{5,1},{9,5},{13... | collective-permute-start | bytes 294920 | tf_op jit(solution)/shard_map/ppermute | solution.py:24
  3.5 2.8 %prepare.1 = (f32[48,4096]{1,0:T(8,128)S(1)}, f32[48,4096]{1,0:T(8,128)S(1)}, bf16[64,4096]{1,0:T(8,128)(2,1)S(1)}, bf16[64,4096]{1,0:T(8,128)(2,1)S(1)}, bf16[6...) custom-call(f32[48,4096]{1,0:T(8,128)} %bitcast.10, ...), custom_call_target="tpu_custom_call" | custom-call | tf_op jit(solution)/shard_map/prepare/pallas_call | solution.py:469
  6.3 0.0 copy-start
  6.3 2.9 %collective-permute-done = f32[3,16,512]{2,1,0:T(8,128)S(1)} collective-permute-done((f32[3,16,512]{2,1,0:T(8,128)S(1)}, f32[3,16,512]{2,1,0:T(8,128)S(1)}, u32[]{:S(2)}, u32[]{:S(2)}) %collective-permute-start) | collective-permute-done | bytes 98336 | tf_op jit(solution)/shard_map/ppermute | solution.py:24
  9.2 1.8 %couple.1 = (f32[72,48,128]{2,1,0:T(8,128)S(1)}, f32[48,4096]{1,0:T(8,128)S(1)}, f32[48,4096]{1,0:T(8,128)S(1)}, f32[48,512]{1,0:T(8,128)S(1)}, f32[48,512]{1,0:...) custom-call(s32[1]{0:T(128)S(6)} %copy.14.count_ref, s32[64]{0:T(128)S(1)} %get-tuple-element.32.local_vmem, ...), custom_call_target="tpu_custom_call" | custom-call | tf_op jit(solution)/shard_map/couple/pallas_call | solution.py:483
  11.0 2.8 %collective-permute-start.1 = (f32[48,512]{1,0:T(8,128)S(1)}, f32[48,512]{1,0:T(8,128)S(1)}, u32[]{:S(2)}, u32[]{:S(2)}) collective-permute-start(f32[48,512]{1,0:T(8,128)S(1)} %get-tuple-element.42), channel_id=1, source_target_pairs={{0,4},{1,5},{2,6},{3,7},{4,0},{5,1},{6,2},{7,3},{8,12},{9,13},{10,... | collective-permute-start | bytes 294920 | tf_op jit(solution)/shard_map/ppermute | solution.py:38
  13.8 0.0 collective-permute-start.2
  13.8 0.0 copy-done
  13.8 1.2 %lift.1 = (f32[48,3584]{1,0:T(8,128)S(1)}, f32[48,3584]{1,0:T(8,128)S(1)}, f32[160,128]{1,0:T(8,128)S(1)}, f32[16,128]{1,0:T(8,128)S(1)}) custom-call(f32[48,4096]{1,0:T(8,128)S(1)} %get-tuple-element.34.field_ref, f32[72,48,128]{2,1,0:T(8,128)S(1)} %get-tuple-element.44.total_ref, f32[48,4096]{1,0:T(8,128)S(1)} %get-tuple-element.35.elastic_ref.field_elastic_ref, ...), custom_call_target="tpu_custom_call" | custom-call | tf_op jit(solution)/shard_map/lift/pallas_call | solution.py:494
  15.0 0.0 copy-start.1
  15.0 0.8 %copy-done.1 = f32[48,3584]{1,0:T(8,128)} copy-done((f32[48,3584]{1,0:T(8,128)}, f32[48,3584]{1,0:T(8,128)S(1)}, u32[]{:S(2)}) %copy-start.1) | copy-done | bytes 688152
  15.9 0.5 %collective-permute-done.1.even_ref = f32[48,512]{1,0:T(8,128)S(1)} collective-permute-done((f32[48,512]{1,0:T(8,128)S(1)}, f32[48,512]{1,0:T(8,128)S(1)}, u32[]{:S(2)}, u32[]{:S(2)}) %collective-permute-start.1) | collective-permute-done | bytes 98336 | tf_op jit(solution)/shard_map/ppermute | solution.py:38
  16.4 0.0 collective-permute-done.2.odd_ref
  16.4 2.7 %energy.1 = (f32[48,512]{1,0:T(8,128)S(1)}, f32[48,512]{1,0:T(8,128)S(1)}, f32[48,4096]{1,0:T(8,128)S(1)}, f32[32,1,256]{2,1,0:T(1,128)}) custom-call(s32[1]{0:T(128)S(6)} %copy.14.count_ref, s32[64]{0:T(128)S(1)} %get-tuple-element.32.local_vmem, s32[64]{0:T(128)S(1)} %get-tuple-element.33.partner_vmem, f32[48,4096]{1,0:T(8,128)S(1)} %get-tuple-element.34.field_ref, ...), custom_call_target="tpu_custom_call" | custom-call | tf_op jit(solution)/shard_map/energy/pallas_call | solution.py:501
  19.1 6.8 %all-to-all-start = ((f32[32,1,256]{2,1,0:T(1,128)}), f32[32,1,256]{2,1,0:T(1,128)S(1)}, u32[]{:S(2)}, u32[]{:S(2)}) async-start(f32[32,1,256]{2,1,0:T(1,128)} %get-tuple-element.50), calls=%async_computation | async-start | bytes 65536 | tf_op jit(solution)/shard_map/all_to_all | solution.py:512
  25.9 0.0 copy-start.2
  25.9 1.2 %settle.1 = (f32[72,48,128]{2,1,0:T(8,128)S(1)}, f32[48,512]{1,0:T(8,128)S(1)}) custom-call(s32[64]{0:T(128)S(1)} %get-tuple-element.32.local_vmem, s32[64]{0:T(128)S(1)} %get-tuple-element.33.partner_vmem, f32[48,4096]{1,0:T(8,128)S(1)} %get-tuple-element.53.force_ref), custom_call_target="tpu_custom_call" | custom-call | flops 1000000000 | bytes 3145728 | tf_op jit(solution)/shard_map/settle/pallas_call | solution.py:513
  27.2 3.7 %collective-permute-start.3 = (f32[48,512]{1,0:T(8,128)S(1)}, f32[48,512]{1,0:T(8,128)S(1)}, u32[]{:S(2)}, u32[]{:S(2)}) collective-permute-start(f32[48,512]{1,0:T(8,128)S(1)} %get-tuple-element.57), channel_id=1, source_target_pairs={{0,4},{4,8},{8,12},{12,16},{16,20},{20,24},{24,28},{1,5},{5,9},{9,... | collective-permute-start | bytes 294920 | tf_op jit(solution)/shard_map/ppermute | solution.py:24
  30.9 0.0 copy-done.2
  30.9 0.5 %gather.1.twice_ref = f32[48,4096]{1,0:T(8,128)S(1)} custom-call(f32[72,48,128]{2,1,0:T(8,128)S(1)} %get-tuple-element.54.total_ref, f32[48,512]{1,0:T(8,128)S(1)} %get-tuple-element.55.lead_elastic_ref, f32[48,3584]{1,0:T(8,128)S(1)} %copy-done.2), custom_call_target="tpu_custom_call" | custom-call | flops 1000000000 | bytes 2359296 | tf_op jit(solution)/shard_map/gather/pallas_call | solution.py:523
  31.4 1.8 %all-to-all-done = f32[32,1,256]{2,1,0:T(1,128)S(1)} async-done(((f32[32,1,256]{2,1,0:T(1,128)}), f32[32,1,256]{2,1,0:T(1,128)S(1)}, u32[]{:S(2)}, u32[]{:S(2)}) %all-to-all-start) | async-done | bytes 32800 | tf_op jit(solution)/shard_map/all_to_all | solution.py:512
  33.2 0.7 %scale.1 = (f32[32,128]{1,0:T(8,128)S(1)}, f32[1,16]{1,0:T(1,128)}) custom-call(f32[32,256]{1,0:T(8,128)S(1)} %bitcast.9), custom_call_target="tpu_custom_call" | custom-call | flops 1000000000 | bytes 32768 | tf_op jit(solution)/shard_map/scale/pallas_call | solution.py:531
  33.9 0.0 collective-permute-done.3.far_received_ref
  33.9 1.2 %last.1 = (f32[48,4096]{1,0:T(8,128)}, f32[48,4096]{1,0:T(8,128)}) custom-call(f32[32,128]{1,0:T(8,128)S(1)} %get-tuple-element.51.scale_ref, f32[48,4096]{1,0:T(8,128)S(1)} %get-tuple-element.34.field_ref, f32[48,3584]{1,0:T(8,128)S(1)} %get-tuple-element.47.image_ref, f32[48,512]{1,0:T(8,128)S(1)} %get-tuple-element.52.lead_ref, ...), custom_call_target="tpu_custom_call" | custom-call | tf_op jit(solution)/shard_map/last/pallas_call | solution.py:539
  (1 shorter events, 0.0 us)
Async XLA Ops:
  1.5 7.6 %collective-permute-start = (f32[3,16,512]{2,1,0:T(8,128)S(1)}, f32[3,16,512]{2,1,0:T(8,128)S(1)}, u32[]{:S(2)}, u32[]{:S(2)}) collective-permute-start(f32[3,16,512]{2,1,0:T(8,128)S(1)} %slice.3), channel_id=1, source_target_pairs={{4,0},{8,4},{12,8},{16,12},{20,16},{24,20},{28,24},{5,1},{9,5},{13... | collective-permute-start | bytes 294920 | tf_op jit(solution)/shard_map/ppermute | solution.py:24
  6.3 7.5 %copy-start = (f32[3,4096]{1,0:T(4,128)S(1)}, f32[3,4096]{1,0:T(4,128)}, u32[]{:S(2)}) copy-start(f32[3,4096]{1,0:T(4,128)} %weight_ref.3) | copy-start | bytes 147460
  11.0 5.4 %collective-permute-start.1 = (f32[48,512]{1,0:T(8,128)S(1)}, f32[48,512]{1,0:T(8,128)S(1)}, u32[]{:S(2)}, u32[]{:S(2)}) collective-permute-start(f32[48,512]{1,0:T(8,128)S(1)} %get-tuple-element.42), channel_id=1, source_target_pairs={{0,4},{1,5},{2,6},{3,7},{4,0},{5,1},{6,2},{7,3},{8,12},{9,13},{10,... | collective-permute-start | bytes 294920 | tf_op jit(solution)/shard_map/ppermute | solution.py:38
  13.8 2.6 %collective-permute-start.2 = (f32[48,512]{1,0:T(8,128)S(1)}, f32[48,512]{1,0:T(8,128)S(1)}, u32[]{:S(2)}, u32[]{:S(2)}) collective-permute-start(f32[48,512]{1,0:T(8,128)S(1)} %get-tuple-element.43), channel_id=1, source_target_pairs={{0,1},{1,0},{2,3},{3,2},{4,8},{5,9},{6,10},{7,11},{8,4},{9,5},{10,... | collective-permute-start | bytes 294920 | tf_op jit(solution)/shard_map/ppermute | solution.py:38
  15.0 0.8 %copy-start.1 = (f32[48,3584]{1,0:T(8,128)}, f32[48,3584]{1,0:T(8,128)S(1)}, u32[]{:S(2)}) copy-start(f32[48,3584]{1,0:T(8,128)S(1)} %get-tuple-element.56.elastic_ref) | copy-start | bytes 2064388
  19.1 14.1 %all-to-all-start = ((f32[32,1,256]{2,1,0:T(1,128)}), f32[32,1,256]{2,1,0:T(1,128)S(1)}, u32[]{:S(2)}, u32[]{:S(2)}) async-start(f32[32,1,256]{2,1,0:T(1,128)} %get-tuple-element.50), calls=%async_computation | async-start | bytes 65536 | tf_op jit(solution)/shard_map/all_to_all | solution.py:512
  25.9 4.9 %copy-start.2 = (f32[48,3584]{1,0:T(8,128)S(1)}, f32[48,3584]{1,0:T(8,128)}, u32[]{:S(2)}) copy-start(f32[48,3584]{1,0:T(8,128)} %copy-done.1) | copy-start | bytes 2064388
  27.2 6.7 %collective-permute-start.3 = (f32[48,512]{1,0:T(8,128)S(1)}, f32[48,512]{1,0:T(8,128)S(1)}, u32[]{:S(2)}, u32[]{:S(2)}) collective-permute-start(f32[48,512]{1,0:T(8,128)S(1)} %get-tuple-element.57), channel_id=1, source_target_pairs={{0,4},{4,8},{8,12},{12,16},{16,20},{20,24},{24,28},{1,5},{5,9},{9,... | collective-permute-start | bytes 294920 | tf_op jit(solution)/shard_map/ppermute | solution.py:24

commit v5 on v4

--- a/solution.py
+++ b/solution.py
@@ -10,12 +10,13 @@
 PN = 64
 NB = 8
 LANES = 128
+SMEM = pl.BlockSpec(memory_space=pltpu.SMEM)
 MOMENT_LANES = 256
 VMEM = pl.BlockSpec(memory_space=pltpu.VMEM)
 HBM = pl.BlockSpec(memory_space=pltpu.HBM)
-SMEM = pl.BlockSpec(memory_space=pltpu.SMEM)
 SUMS = 10
 CHUNKS = 4
+LAST_CHUNKS = 4
 
 
 def shifted(value, axis, by):
@@ -56,14 +57,23 @@
     ref[:, index * LANES : (index + 1) * LANES] = value
 
 
-def fetch(sources, targets, sems):
-    copies = [
-        pltpu.make_async_copy(source, target, sems.at[place])
-        for place, (source, target) in enumerate(zip(sources, targets))
-    ]
-    for copy in copies:
-        copy.start()
-    return copies
+class Slots:
+    def __init__(self, sources, targets, sems):
+        self.local, self.partner = targets
+        self.copies = [
+            pltpu.make_async_copy(source, target, sems.at[place])
+            for place, (source, target) in enumerate(zip(sources, targets))
+        ]
+        for copy in self.copies:
+            copy.start()
+
+    def wait(self):
+        for copy in self.copies:
+            copy.wait()
+
+
+def live(count_ref, slot):
+    return jnp.where(slot < count_ref[0], 1.0, 0.0)
 
 
 def chunked(sources, targets, sems, chunk):
@@ -102,24 +112,15 @@
     twin_ref[patch + 1] = jnp.where(left, swapped, field_tile)
 
 
-def slot_forces(twin_ref, high_ref, low_ref, local_ref, partner_ref, count_ref, step):
-    slot = 2 * step
-    live_count = count_ref[0]
-    first_live = jnp.where(slot < live_count, 1.0, 0.0)
-    second_live = jnp.where(slot + 1 < live_count, 1.0, 0.0)
-    first_gap = (twin_ref[local_ref[slot]] - twin_ref[partner_ref[slot]]) * first_live
-    second_gap = (twin_ref[local_ref[slot + 1]] - twin_ref[partner_ref[slot + 1]]) * second_live
-    gap = jnp.where(left_half(first_gap.shape), first_gap, second_gap)
-    return gap, pair_product(gap, tile(high_ref, step), tile(low_ref, step))
-
-
-def scatter(force, local_ref, partner_ref, total_ref, step):
-    slot = 2 * step
+def side_by_side(first, second):
+    return jnp.where(left_half(first.shape), first, second)
+
+
+def scatter(force, step, targets):
     left = left_half(force.shape)
-    for number, half in ((slot, jnp.where(left, force, 0.0)), (slot + 1, jnp.where(left, 0.0, force))):
-        patch, partner = local_ref[number], partner_ref[number]
-        total_ref[patch] = total_ref[patch] + half
-        total_ref[partner] = total_ref[partner] - half
+    for slot, half in ((2 * step, jnp.where(left, force, 0.0)), (2 * step + 1, jnp.where(left, 0.0, force))):
+        for ref, patch, sign in targets(slot):
+            ref[patch] = ref[patch] + half if sign > 0 else ref[patch] - half
 
 
 def folded(total_ref, patch):
@@ -137,8 +138,7 @@
 
 def prepare_kernel(
     field_hbm, stiff_hbm, contact_hbm, local_hbm, partner_hbm,
-    field_ref, elastic_ref, stiff_high_ref, stiff_low_ref, contact_high_ref, contact_low_ref,
-    local_ref, partner_ref,
+    field_ref, elastic_ref, stiff_high_ref, stiff_low_ref, contact_high_ref, contact_low_ref, local_ref, partner_ref,
     stiff_ref, contact_ref, sems, contact_sems, table_sems,
 ):
     chunk = stiff_ref.shape[1] // CHUNKS
@@ -148,7 +148,7 @@
     for group in copies + contact_copies:
         for copy in group:
             copy.start()
-    tables = fetch((local_hbm, partner_hbm), (local_ref, partner_ref), table_sems)
+    slots = Slots((local_hbm, partner_hbm), (local_ref, partner_ref), table_sems)
     for place, group in enumerate(copies):
         for copy in group:
             copy.wait()
@@ -164,29 +164,35 @@
             high, low = split(tile(contact_ref, index))
             put(contact_high_ref, index, high)
             put(contact_low_ref, index, low)
-    for copy in tables:
-        copy.wait()
+    slots.wait()
 
 
 def couple_kernel(
     count_ref, local_vmem, partner_vmem, field_ref, elastic_ref, halo_ref, high_ref, low_ref,
     total_ref, gap_ref, force_ref, own_ref, spread_ref, even_ref, odd_ref,
-    local_ref, partner_ref, sems, twin_ref,
+    local_ref, partner_ref, table_sems, twin_ref,
 ):
-    tables = fetch((local_vmem, partner_vmem), (local_ref, partner_ref), sems)
+    slots = Slots((local_vmem, partner_vmem), (local_ref, partner_ref), table_sems)
     patches = field_ref.shape[1] // PN
     clear(total_ref)
     for index in range(patches // 2):
         fill_twins(tile(field_ref, index), twin_ref, 2 * index)
     for index in range(NB // 2):
         fill_twins(tile(halo_ref, index), twin_ref, patches + 2 * index)
-    for copy in tables:
-        copy.wait()
+    slots.wait()
+
+    def slot_gap(slot):
+        return (twin_ref[slots.local[slot]] - twin_ref[slots.partner[slot]]) * live(count_ref, slot)
+
+    def targets(slot):
+        return (total_ref, slots.local[slot], 1), (total_ref, slots.partner[slot], -1)
+
     for step in range(high_ref.shape[1] // LANES):
-        gap, force = slot_forces(twin_ref, high_ref, low_ref, local_ref, partner_ref, count_ref, step)
+        gap = side_by_side(slot_gap(2 * step), slot_gap(2 * step + 1))
+        force = pair_product(gap, tile(high_ref, step), tile(low_ref, step))
         put(gap_ref, step, gap)
         put(force_ref, step, force)
-        scatter(force, local_ref, partner_ref, total_ref, step)
+        scatter(force, step, targets)
     even = lax.axis_index("dom") % 2 == 0
     for index in range(NB // 2):
         value = tile(elastic_ref, index) + folded(total_ref, 2 * index)
@@ -242,9 +248,11 @@
 
 
 def lift_kernel(
-    field_ref, total_ref, field_elastic_ref, stiff_high_ref, stiff_low_ref, weight_ref,
-    image_ref, elastic_ref, sums_ref, trial_ref, *, columns,
+    local_vmem, partner_vmem, field_ref, total_ref, field_elastic_ref, stiff_high_ref, stiff_low_ref, weight_ref,
+    image_ref, elastic_ref, near_ref, sums_ref, trial_ref,
+    local_ref, partner_ref, table_sems, twin_ref, *, columns,
 ):
+    slots = Slots((local_vmem, partner_vmem), (local_ref, partner_ref), table_sems)
     rows = field_ref.shape[0]
     patches = field_ref.shape[1] // PN
     lead = NB // 2
@@ -258,6 +266,7 @@
             continue
         image_tile = tile(field_elastic_ref, index) + folded(total_ref, 2 * index)
         put(image_ref, index - lead, image_tile)
+        fill_twins(image_tile, twin_ref, 2 * index)
         product = pair_product(image_tile, tile(stiff_high_ref, index), tile(stiff_low_ref, index))
         put(elastic_ref, index - lead, product)
         sums.add(1, field_tile * image_tile)
@@ -279,16 +288,27 @@
             sums, trial_rows, field_tile, tile(field_elastic_ref, index), image_tile, tile(elastic_ref, index - lead)
         )
     sums.store(sums_ref)
+    twin_ref[patches] = jnp.zeros(twin_ref.shape[1:], jnp.float32)
+    slots.wait()
+
+    def inner(patch):
+        return twin_ref[jnp.where((patch >= NB) & (patch < patches), patch, patches)]
+
+    def inner_gap(slot):
+        return inner(slots.local[slot]) - inner(slots.partner[slot])
+
+    for step in range(near_ref.shape[1] // LANES):
+        put(near_ref, step, side_by_side(inner_gap(2 * step), inner_gap(2 * step + 1)))
 
 
 def energy_kernel(
     count_ref, local_vmem, partner_vmem, field_ref, field_elastic_ref, gap_ref, force_ref, own_ref, spread_ref,
-    even_ref, odd_ref, image_ref, stiff_high_ref, stiff_low_ref, contact_high_ref, contact_low_ref, weight_ref,
+    even_ref, odd_ref, near_ref, stiff_high_ref, stiff_low_ref, contact_high_ref, contact_low_ref, weight_ref,
     sums_ref, trial_ref,
     lead_ref, lead_elastic_ref, image_force_ref, moment_ref,
-    local_ref, partner_ref, sems, twin_ref, *, columns,
+    local_ref, partner_ref, table_sems, twin_ref, *, columns,
 ):
-    tables = fetch((local_vmem, partner_vmem), (local_ref, partner_ref), sems)
+    slots = Slots((local_vmem, partner_vmem), (local_ref, partner_ref), table_sems)
     rows = field_ref.shape[0]
     patches = field_ref.shape[1] // PN
     lead = NB // 2
@@ -298,13 +318,11 @@
     trial_rows = jnp.concatenate([trial] * (rows // columns), axis=0)
     sums = Sums(columns)
     sums.load(sums_ref)
-    for index in range(lead, patches // 2):
-        fill_twins(tile(image_ref, index - lead), twin_ref, 2 * index)
     for index in range(lead):
         first, second = tile(even_ref, index), tile(odd_ref, index)
         received = jnp.where(place > 0, jnp.where(even, second, first), 0.0)
         far_tile = jnp.where(place < last, jnp.where(even, first, second) + tile(spread_ref, index), 0.0)
-        fill_twins(far_tile, twin_ref, patches + 2 * index)
+        fill_twins(far_tile, twin_ref, NB + 2 * index)
         field_tile = tile(field_ref, index)
         image_tile = tile(own_ref, index) + received
         put(lead_ref, index, image_tile)
@@ -318,52 +336,75 @@
         sums.add(4, image_tile * image_tile)
         sums.add(9, weights_of(weight_ref, index, rows) * image_tile)
         add_energy(sums, trial_rows, field_tile, tile(field_elastic_ref, index), image_tile, product)
-    for copy in tables:
-        copy.wait()
+    twin_ref[2 * NB] = jnp.zeros(twin_ref.shape[1:], jnp.float32)
+    slots.wait()
+
+    def outer(patch):
+        far = patch >= patches
+        return twin_ref[jnp.where(far, patch - patches + NB, jnp.where(patch < NB, patch, 2 * NB))]
+
+    def outer_gap(slot):
+        return outer(slots.local[slot]) - outer(slots.partner[slot])
+
     for step in range(contact_high_ref.shape[1] // LANES):
-        gap, force = slot_forces(
-            twin_ref, contact_high_ref, contact_low_ref, local_ref, partner_ref, count_ref, step
-        )
+        gap = tile(near_ref, step) + side_by_side(outer_gap(2 * step), outer_gap(2 * step + 1))
+        lives = [jnp.full(gap.shape, live(count_ref, 2 * step + side), jnp.float32) for side in range(2)]
+        gap = gap * side_by_side(*lives)
+        force = pair_product(gap, tile(contact_high_ref, step), tile(contact_low_ref, step))
         put(image_force_ref, step, force)
         add_energy(sums, trial_rows, tile(gap_ref, step), tile(force_ref, step), gap, force)
     lane = lax.broadcasted_iota(jnp.int32, (columns, LANES), 1)
-    table = jnp.where(lane == SUMS, trial, 0.0)
-    for number in range(SUMS):
-        table = jnp.where(lane == number, jnp.sum(sums.values[number], axis=1, keepdims=True), table)
-    table = jnp.concatenate([table, jnp.zeros((LANES - columns, LANES), jnp.float32)], axis=0)
-    flipped = jnp.transpose(table)
+    column = lax.broadcasted_iota(jnp.int32, (columns, LANES), 0)
     for half in range(2):
-        row = pltpu.roll(flipped[half * 8 : half * 8 + 8], 0, 1, stride=columns, stride_axis=0)
-        row = jnp.sum(row, axis=0, keepdims=True)
+        spread_out = jnp.zeros((columns, LANES), jnp.float32)
+        for number in range(half * 8, min(half * 8 + 8, SUMS + 1)):
+            value = trial if number == SUMS else jnp.sum(sums.values[number], axis=1, keepdims=True)
+            spread_out = jnp.where(lane == column + columns * (number % 8), value, spread_out)
+        row = jnp.sum(spread_out, axis=0, keepdims=True)
         moment_ref[:, :, half * LANES : (half + 1) * LANES] = jnp.broadcast_to(
             row[None], (moment_ref.shape[0], 1, LANES)
         )
 
 
 def settle_kernel(
-    local_vmem, partner_vmem, force_ref,
-    total_ref, far_spread_ref,
-    local_ref, partner_ref, sems,
+    local_vmem, partner_vmem, force_ref, far_spread_ref, local_ref, partner_ref, table_sems, total_ref, *, patches
 ):
-    tables = fetch((local_vmem, partner_vmem), (local_ref, partner_ref), sems)
-    patches = total_ref.shape[0] - NB
+    slots = Slots((local_vmem, partner_vmem), (local_ref, partner_ref), table_sems)
     clear(total_ref)
-    for copy in tables:
-        copy.wait()
+    slots.wait()
+
+    def targets(slot):
+        partner = slots.partner[slot]
+        return ((total_ref, jnp.where(partner < patches, NB, partner - patches), -1),)
+
     for step in range(force_ref.shape[1] // LANES):
-        scatter(tile(force_ref, step), local_ref, partner_ref, total_ref, step)
+        scatter(tile(force_ref, step), step, targets)
     for index in range(NB // 2):
-        put(far_spread_ref, index, folded(total_ref, patches + 2 * index))
-
-
-def gather_kernel(total_ref, lead_elastic_ref, elastic_ref, twice_ref):
+        put(far_spread_ref, index, folded(total_ref, 2 * index))
+
+
+def gather_kernel(
+    local_vmem, partner_vmem, force_ref, lead_elastic_ref, elastic_ref, twice_ref,
+    local_ref, partner_ref, table_sems, total_ref,
+):
+    slots = Slots((local_vmem, partner_vmem), (local_ref, partner_ref), table_sems)
+    patches = twice_ref.shape[1] // PN
     lead = NB // 2
-    for index in range(twice_ref.shape[1] // LANES):
+    clear(total_ref)
+    slots.wait()
+
+    def targets(slot):
+        partner = slots.partner[slot]
+        return (total_ref, slots.local[slot], 1), (total_ref, jnp.where(partner < patches, partner, patches), -1)
+
+    for step in range(force_ref.shape[1] // LANES):
+        scatter(tile(force_ref, step), step, targets)
+    for index in range(patches // 2):
         product = tile(lead_elastic_ref, index) if index < lead else tile(elastic_ref, index - lead)
         put(twice_ref, index, product + folded(total_ref, 2 * index))
 
 
-def scale_kernel(moment_ref, scale_ref, step_ref, *, columns, groups):
+def scale_kernel(moment_ref, scale_ref, gradient_ref, *, columns, groups):
     devices = moment_ref.shape[0]
 
     def moment(place):
@@ -397,34 +438,43 @@
     on_field = first_step + second_step * (1.0 + ratio)
     on_image = -second_step * first_step
     gradient = on_field * total(moment(8)) + on_image * total(moment(9))
+    gradient_ref[...] = gradient
+    mine = lax.broadcasted_iota(jnp.int32, (8, LANES), 0) == lax.axis_index("col")
+    diagonal = lax.broadcasted_iota(jnp.int32, (columns, LANES), 0) == lax.broadcasted_iota(
+        jnp.int32, (columns, LANES), 1
+    )
+    for place, value in enumerate((on_field, on_image)):
+        own = jnp.sum(jnp.where(mine, value, 0.0), axis=0, keepdims=True)
+        own = jnp.sum(jnp.where(diagonal, own, 0.0), axis=1, keepdims=True)
+        scale_ref[place * columns : (place + 1) * columns] = jnp.broadcast_to(own, (columns, LANES))
+
+
+def own_step(gradient, columns, groups):
     lane = lax.broadcasted_iota(jnp.int32, (8, LANES), 1)
     row = lax.broadcasted_iota(jnp.int32, (8, LANES), 0)
     counted = jnp.where((lane < columns) & (row < groups), gradient * gradient, 0.0)
     square_total = jnp.sum(jnp.sum(counted, axis=1, keepdims=True), axis=0, keepdims=True)
     scaled = gradient / jnp.sqrt(square_total / (columns * groups) + 1e-06)
-    mine = row == lax.axis_index("col")
-
-    def own(value):
-        return jnp.sum(jnp.where(mine, value, 0.0), axis=0, keepdims=True)
-
-    step_ref[...] = own(scaled)[:, :columns]
-    pair = jnp.concatenate([own(on_field), own(on_image), jnp.zeros((LANES - 2, LANES), jnp.float32)], axis=0)
-    flipped = jnp.transpose(pair)[:columns]
-    scale_ref[:columns] = jnp.broadcast_to(flipped[:, 0:1], (columns, LANES))
-    scale_ref[columns:] = jnp.broadcast_to(flipped[:, 1:2], (columns, LANES))
+    return jnp.sum(jnp.where(row == lax.axis_index("col"), scaled, 0.0), axis=0, keepdims=True)[:, :columns]
+
+
+def scale_rows(scale_ref, rows):
+    columns = scale_ref.shape[0] // 2
+    return (
+        jnp.concatenate([scale_ref[:columns]] * (rows // columns), axis=0),
+        jnp.concatenate([scale_ref[columns:]] * (rows // columns), axis=0),
+    )
 
 
 def last_kernel(
-    scale_ref, field_ref, image_ref, lead_ref, twice_ref, far_received_ref,
-    solution_hbm, residual_hbm, solution_ref, residual_ref, sems,
+    scale_ref, gradient_ref, field_ref, image_ref, lead_ref, twice_ref, far_received_ref,
+    solution_hbm, residual_hbm, step_hbm, solution_ref, residual_ref, step_ref, sems, step_sem, *, groups,
 ):
-    rows = field_ref.shape[0]
-    columns = scale_ref.shape[0] // 2
-    field_rows = jnp.concatenate([scale_ref[:columns]] * (rows // columns), axis=0)
-    image_rows = jnp.concatenate([scale_ref[columns:]] * (rows // columns), axis=0)
-    chunk = field_ref.shape[1] // CHUNKS
+    field_rows, image_rows = scale_rows(scale_ref, field_ref.shape[0])
+    chunk = field_ref.shape[1] // LAST_CHUNKS
     tiles = chunk // LANES
     copies = chunked((solution_ref, residual_ref), (solution_hbm, residual_hbm), sems, chunk)
+    step_copy = pltpu.make_async_copy(step_ref, step_hbm, step_sem.at[0])
     for place, group in enumerate(copies):
         for index in range(place * tiles, (place + 1) * tiles):
             field_tile = tile(field_ref, index)
@@ -436,6 +486,10 @@
             put(residual_ref, index, field_tile - field_rows * image_tile - image_rows * twice_tile)
         for copy in group:
             copy.start()
+        if place == 0:
+            step_ref[...] = own_step(gradient_ref[...], scale_ref.shape[0] // 2, groups)
+            step_copy.start()
+    step_copy.wait()
     for group in copies:
         for copy in group:
             copy.wait()
@@ -456,19 +510,27 @@
     shape = jax.ShapeDtypeStruct
     wide = shape((rows, nodes), f32)
     narrow = shape((rows, width), f32)
-    tables = (shape(pair_local.shape, jnp.int32), shape(pair_partner.shape, jnp.int32))
-    scratch = [pltpu.SMEM(table.shape, jnp.int32) for table in tables]
-    scratch += [pltpu.SemaphoreType.DMA((len(tables),))]
-    twins = pltpu.VMEM((patches + NB, rows, LANES), f32)
+    parts = [shape(block.shape, jnp.bfloat16) for block in (stiffness, stiffness, contact, contact)]
+
+    def in_hbm(value):
+        return pltpu.with_memory_space_constraint(value, pltpu.HBM)
+
+    field_hbm = in_hbm(right_side.reshape(rows, nodes))
+    pairs = (in_hbm(pair_local), in_hbm(pair_partner))
     slots = shape((rows, contact.shape[1]), f32)
-    parts = [shape(block.shape, jnp.bfloat16) for block in (stiffness, stiffness, contact, contact)]
-
-    field_hbm = right_side.reshape(rows, nodes)
+
+    def scratch(count):
+        return [
+            pltpu.SMEM(pair_local.shape, jnp.int32),
+            pltpu.SMEM(pair_partner.shape, jnp.int32),
+            pltpu.SemaphoreType.DMA((2,)),
+            pltpu.VMEM((count, rows, LANES), f32),
+        ]
+
     halo = shifted(right_side[:, :, :width], "dom", -1).reshape(rows, width)
-    given = (field_hbm, stiffness, contact, pair_local, pair_partner)
     field, field_elastic, stiff_high, stiff_low, contact_high, contact_low, *tables = call(
         prepare_kernel,
-        out_shape=(wide, wide, *parts, *tables),
+        out_shape=(wide, wide, *parts, *(shape(pair.shape, jnp.int32) for pair in pairs)),
         in_specs=[HBM] * 5,
         out_specs=(VMEM,) * 8,
         scratch_shapes=[
@@ -479,71 +541,78 @@
             pltpu.SemaphoreType.DMA((2,)),
         ],
         name="prepare",
-    )(*(pltpu.with_memory_space_constraint(value, pltpu.HBM) for value in given))
+    )(field_hbm, in_hbm(stiffness), in_hbm(contact), *pairs)
     total, gap, force, own, spread, even, odd = call(
         couple_kernel,
-        out_shape=(shape(twins.shape, f32), slots, slots, narrow, narrow, narrow, narrow),
+        out_shape=(shape((patches + NB, rows, LANES), f32), slots, slots, narrow, narrow, narrow, narrow),
         in_specs=[SMEM] + [VMEM] * 7,
         out_specs=(VMEM,) * 7,
-        scratch_shapes=scratch + [twins],
+        scratch_shapes=scratch(patches + NB),
         name="couple",
     )(pair_count, *tables, field, field_elastic, halo, contact_high, contact_low)
     even = swapped(even, False)
     odd = swapped(odd, True)
     tail = shape((rows, nodes - width), f32)
-    image, elastic, sums, trial = call(
+    image, elastic, near, sums, trial = call(
         functools.partial(lift_kernel, columns=columns),
-        out_shape=(tail, tail, shape((SUMS * columns, LANES), f32), shape((columns, LANES), f32)),
-        in_specs=[VMEM] * 6,
-        out_specs=(VMEM,) * 4,
+        out_shape=(tail, tail, slots, shape((SUMS * columns, LANES), f32), shape((columns, LANES), f32)),
+        in_specs=[VMEM] * 8,
+        out_specs=(VMEM,) * 5,
+        scratch_shapes=scratch(patches + 1),
         name="lift",
-    )(field, total, field_elastic, stiff_high, stiff_low, objective_weight)
+    )(*tables, field, total, field_elastic, stiff_high, stiff_low, objective_weight)
     lead, lead_elastic, image_force, moments = call(
         functools.partial(energy_kernel, columns=columns),
         out_shape=(narrow, narrow, slots, shape((devices, 1, MOMENT_LANES), f32)),
         in_specs=[SMEM] + [VMEM] * 18,
         out_specs=(VMEM,) * 4,
-        scratch_shapes=scratch + [twins],
+        scratch_shapes=scratch(2 * NB + 1),
         name="energy",
     )(
-        pair_count, *tables, field, field_elastic, gap, force, own, spread, even, odd, image,
+        pair_count, *tables, field, field_elastic, gap, force, own, spread, even, odd, near,
         stiff_high, stiff_low, contact_high, contact_low, objective_weight, sums, trial,
     )
     gathered = lax.all_to_all(moments, ("dom", "col"), 0, 0, tiled=True).reshape(devices, MOMENT_LANES)
-    total, far_spread = call(
-        settle_kernel,
-        out_shape=(shape(twins.shape, f32), narrow),
+    far_spread = call(
+        functools.partial(settle_kernel, patches=patches),
+        out_shape=narrow,
         in_specs=[VMEM] * 3,
-        out_specs=(VMEM,) * 2,
-        scratch_shapes=scratch,
-        cost_estimate=pl.CostEstimate(flops=10**9, bytes_accessed=4 * rows * nodes * 4, transcendentals=0),
+        out_specs=VMEM,
+        scratch_shapes=scratch(NB + 1),
+        cost_estimate=pl.CostEstimate(flops=10**9, bytes_accessed=rows * nodes * 4, transcendentals=0),
         name="settle",
     )(*tables, image_force)
     far_received = shifted(far_spread, "dom", 1)
     twice = call(
         gather_kernel,
         out_shape=wide,
-        in_specs=[VMEM] * 3,
+        in_specs=[VMEM] * 5,
         out_specs=VMEM,
+        scratch_shapes=scratch(patches + 1),
         cost_estimate=pl.CostEstimate(flops=10**9, bytes_accessed=3 * rows * nodes * 4, transcendentals=0),
         name="gather",
-    )(total, lead_elastic, elastic)
-    scales, step = call(
+    )(*tables, image_force, lead_elastic, elastic)
+    scales, gradient = call(
         functools.partial(scale_kernel, columns=columns, groups=groups),
-        out_shape=(shape((2 * columns, LANES), f32), shape((1, columns), f32)),
+        out_shape=(shape((2 * columns, LANES), f32), shape((8, LANES), f32)),
         in_specs=[VMEM],
         out_specs=(VMEM,) * 2,
         cost_estimate=pl.CostEstimate(flops=10**9, bytes_accessed=devices * MOMENT_LANES * 4, transcendentals=0),
         name="scale",
     )(gathered)
-    solution_field, residual = call(
-        last_kernel,
-        out_shape=(wide, wide),
-        in_specs=[VMEM] * 6,
-        out_specs=(HBM,) * 2,
-        scratch_shapes=[pltpu.VMEM((rows, nodes), f32)] * 2 + [pltpu.SemaphoreType.DMA((2 * CHUNKS,))],
+    solution_field, residual, step = call(
+        functools.partial(last_kernel, groups=groups),
+        out_shape=(wide, wide, shape((1, columns), f32)),
+        in_specs=[VMEM] * 7,
+        out_specs=(HBM,) * 3,
+        scratch_shapes=[pltpu.VMEM((rows, nodes), f32)] * 2
+        + [
+            pltpu.VMEM((1, columns), f32),
+            pltpu.SemaphoreType.DMA((2 * LAST_CHUNKS,)),
+            pltpu.SemaphoreType.DMA((1,)),
+        ],
         name="last",
-    )(scales, field, image, lead, twice, far_received)
+    )(scales, gradient, field, image, lead, twice, far_received)
     return (
         solution_field.reshape(right_side.shape),
         residual.reshape(right_side.shape),

time: 35.4 us -> 34.7 us (0.980)
  Pallas kernels: 12.3 us -> 13.4 us
  waiting for transfers between devices: 5.2 us -> 4.17 us
  local copies, waits for them, and re-layouts: 1.76 us -> 0.92 us
    pallas_call x5, Pallas kernels: 7.59 us -> 8.75 us  [the longest x1 2.84 us: shards(): call(prepare_kernel, out_shape=(wide, wide, *parts, *(shape(pair.shape, j...]
    all_to_all x1, waiting for transfers between devices: 1.83 us -> 0.71 us  [shards(): lax.all_to_all(moments, ('dom', 'col'), 0, 0, tiled=True)]
    unnamed x7, local copies, waits for them, and re-layouts: 0.86 us -> 0.02 us
    pallas_call x1, Pallas kernels: 1.22 us -> 1.98 us  [shards(): call(functools.partial(lift_kernel, columns=columns), out_shape=(tail, ta...]
    pallas_call x1, Pallas kernels: 0.74 us -> 0.19 us  [shards(): call(functools.partial(scale_kernel, columns=columns, groups=groups), out...]
  transfers between devices with their start and end apart: 5 -> 5, of which waited for: 3 -> 3; matrix products, arithmetic and copies ran while one was open for 0% -> 0% of each run, Pallas kernels for 18% -> 23%
where the time goes in v5:
time: 34.7 us; the launch traced here: 34.5 us
  starting transfers between devices  14.5 us (42%)
  Pallas kernels  13.4 us (39%)
  waiting for transfers between devices  4.17 us (12%)
  between operations  1.39 us (4%)
  local copies, waits for them, and re-layouts  0.92 us (3%)
    all_to_all x1, starting transfers between devices, shards(): lax.all_to_all(moments, ('dom', 'col'), 0, 0, tiled=True)  6.81 us
    ppermute x2, starting transfers between devices, shifted(): return lax.ppermute(value, axis, pairs)  4.95 us
    ppermute x2, waiting for transfers between devices, shifted(): return lax.ppermute(value, axis, pairs)  2.86 us
    pallas_call x1, Pallas kernels, shards(): call(prepare_kernel, out_shape=(wide, wide, *parts, *(shape(pair.shape, j...  2.84 us
    ppermute x2, starting transfers between devices, swapped(): return lax.ppermute(value, ('dom', 'col'), pairs)  2.78 us
    pallas_call x1, Pallas kernels, shards(): call(functools.partial(energy_kernel, columns=columns), out_shape=(narrow...  2.5 us
    pallas_call x1, Pallas kernels, shards(): call(functools.partial(lift_kernel, columns=columns), out_shape=(tail, ta...  1.98 us
    pallas_call x1, Pallas kernels, shards(): call(couple_kernel, out_shape=(shape((patches + NB, rows, LANES), f32), s...  1.81 us
  transfers between devices with their start and end apart: 5, of which 3 were waited for; matrix products, arithmetic and copies ran while one was open for 0% of the time, Pallas kernels for 23%

profile of v5, /device:TPU:0, one launch (start us, length us, event | category | flops | bytes accessed | tf_op | source)
XLA Modules:
  0.0 34.5 jit_solution(7560000659454998562)
XLA Ops:
  0.6 0.9 %slice.3 = f32[3,16,512]{2,1,0:T(8,128)S(1)} slice(f32[3,16,4096]{2,1,0:T(8,128)} %param.7), slice={[0:3], [0:16], [0:512]} | slice | bytes 196608 | tf_op jit(solution)/shard_map/slice | solution.py:530
  1.5 1.3 %collective-permute-start = (f32[3,16,512]{2,1,0:T(8,128)S(1)}, f32[3,16,512]{2,1,0:T(8,128)S(1)}, u32[]{:S(2)}, u32[]{:S(2)}) collective-permute-start(f32[3,16,512]{2,1,0:T(8,128)S(1)} %slice.3), channel_id=1, source_target_pairs={{4,0},{8,4},{12,8},{16,12},{20,16},{24,20},{28,24},{5,1},{9,5},{13... | collective-permute-start | bytes 294920 | tf_op jit(solution)/shard_map/ppermute | solution.py:25
  3.5 2.8 %prepare.1 = (f32[48,4096]{1,0:T(8,128)S(1)}, f32[48,4096]{1,0:T(8,128)S(1)}, bf16[64,4096]{1,0:T(8,128)(2,1)S(1)}, bf16[64,4096]{1,0:T(8,128)(2,1)S(1)}, bf16[6...) custom-call(f32[48,4096]{1,0:T(8,128)} %bitcast.10, ...), custom_call_target="tpu_custom_call" | custom-call | tf_op jit(solution)/shard_map/prepare/pallas_call | solution.py:531
  6.3 0.0 copy-start
  6.3 2.9 %collective-permute-done = f32[3,16,512]{2,1,0:T(8,128)S(1)} collective-permute-done((f32[3,16,512]{2,1,0:T(8,128)S(1)}, f32[3,16,512]{2,1,0:T(8,128)S(1)}, u32[]{:S(2)}, u32[]{:S(2)}) %collective-permute-start) | collective-permute-done | bytes 98336 | tf_op jit(solution)/shard_map/ppermute | solution.py:25
  9.2 1.8 %couple.1 = (f32[72,48,128]{2,1,0:T(8,128)S(1)}, f32[48,4096]{1,0:T(8,128)S(1)}, f32[48,4096]{1,0:T(8,128)S(1)}, f32[48,512]{1,0:T(8,128)S(1)}, f32[48,512]{1,0:...) custom-call(s32[1]{0:T(128)S(6)} %copy.14.count_ref, s32[64]{0:T(128)S(1)} %get-tuple-element.32.local_vmem, ...), custom_call_target="tpu_custom_call" | custom-call | tf_op jit(solution)/shard_map/couple/pallas_call | solution.py:545
  11.0 2.8 %collective-permute-start.1 = (f32[48,512]{1,0:T(8,128)S(1)}, f32[48,512]{1,0:T(8,128)S(1)}, u32[]{:S(2)}, u32[]{:S(2)}) collective-permute-start(f32[48,512]{1,0:T(8,128)S(1)} %get-tuple-element.42), channel_id=1, source_target_pairs={{0,4},{1,5},{2,6},{3,7},{4,0},{5,1},{6,2},{7,3},{8,12},{9,13},{10,... | collective-permute-start | bytes 294920 | tf_op jit(solution)/shard_map/ppermute | solution.py:39
  13.8 0.0 collective-permute-start.2
  13.8 0.0 copy-done
  13.8 2.0 %lift.1 = (f32[48,3584]{1,0:T(8,128)S(1)}, f32[48,3584]{1,0:T(8,128)S(1)}, f32[48,4096]{1,0:T(8,128)S(1)}, f32[160,128]{1,0:T(8,128)S(1)}, f32[16,128]{1,0:T(8,128)S(1)}) custom-call(s32[64]{0:T(128)S(1)} %get-tuple-element.32.local_vmem, s32[64]{0:T(128)S(1)} %get-tuple-element.33.partner_vmem, f32[48,4096]{1,0:T(8,128)S(1)} %get-tuple-element.34.field_ref, ...), custom_call_target="tpu_custom_call" | custom-call | tf_op jit(solution)/shard_map/lift/pallas_call | solution.py:556
  15.8 0.0 copy-start.1
  15.8 0.6 %collective-permute-done.1.even_ref = f32[48,512]{1,0:T(8,128)S(1)} collective-permute-done((f32[48,512]{1,0:T(8,128)S(1)}, f32[48,512]{1,0:T(8,128)S(1)}, u32[]{:S(2)}, u32[]{:S(2)}) %collective-permute-start.1) | collective-permute-done | bytes 98336 | tf_op jit(solution)/shard_map/ppermute | solution.py:39
  16.4 0.0 collective-permute-done.2.odd_ref
  16.4 2.5 %energy.1 = (f32[48,512]{1,0:T(8,128)S(1)}, f32[48,512]{1,0:T(8,128)S(1)}, f32[48,4096]{1,0:T(8,128)S(1)}, f32[32,1,256]{2,1,0:T(1,128)}) custom-call(s32[1]{0:T(128)S(6)} %copy.14.count_ref, s32[64]{0:T(128)S(1)} %get-tuple-element.32.local_vmem, s32[64]{0:T(128)S(1)} %get-tuple-element.33.partner_vmem, f32[48,4096]{1,0:T(8,128)S(1)} %get-tuple-element.34.field_ref, ...), custom_call_target="tpu_custom_call" | custom-call | tf_op jit(solution)/shard_map/energy/pallas_call | solution.py:564
  18.9 0.0 copy-done.1
  18.9 6.8 %all-to-all-start = ((f32[32,1,256]{2,1,0:T(1,128)}), f32[32,1,256]{2,1,0:T(1,128)S(1)}, u32[]{:S(2)}, u32[]{:S(2)}) async-start(f32[32,1,256]{2,1,0:T(1,128)} %get-tuple-element.50), calls=%async_computation | async-start | bytes 65536 | tf_op jit(solution)/shard_map/all_to_all | solution.py:575
  25.7 0.0 copy-start.2
  25.7 1.1 %settle.1 = f32[48,512]{1,0:T(8,128)S(1)} custom-call(s32[64]{0:T(128)S(1)} %get-tuple-element.32.local_vmem, s32[64]{0:T(128)S(1)} %get-tuple-element.33.partner_vmem, f32[48,4096]{1,0:T(8,128)S(1)} %get-tuple-element.55.force_ref), custom_call_target="tpu_custom_call" | custom-call | flops 1000000000 | bytes 786432 | tf_op jit(solution)/shard_map/settle/pallas_call | solution.py:576
  26.8 3.7 %collective-permute-start.3 = (f32[48,512]{1,0:T(8,128)S(1)}, f32[48,512]{1,0:T(8,128)S(1)}, u32[]{:S(2)}, u32[]{:S(2)}) collective-permute-start(f32[48,512]{1,0:T(8,128)S(1)} %settle.1), channel_id=1, source_target_pairs={{0,4},{4,8},{8,12},{12,16},{16,20},{20,24},{24,28},{1,5},{5,9},{9,... | collective-permute-start | bytes 294920 | tf_op jit(solution)/shard_map/ppermute | solution.py:25
  30.5 0.0 copy-done.2
  30.5 1.7 %gather.1.twice_ref = f32[48,4096]{1,0:T(8,128)S(1)} custom-call(s32[64]{0:T(128)S(1)} %get-tuple-element.32.local_vmem, s32[64]{0:T(128)S(1)} %get-tuple-element.33.partner_vmem, f32[48,4096]{1,0:T(8,128)S(1)} %get-tuple-element.55.force_ref, f32[48,512]{1,0:T(8,128)S(1)} %get-tuple-element.56.lead_elastic_ref, f32[48,3584]{1,0:T(8,128)S(1)} %copy-done.2), custom_call_target="tpu_custom_call" | custom-call | flops 1000000000 | bytes 2359296 | tf_op jit(solution)/shard_map/gather/pallas_call | solution.py:586
  32.3 0.7 %all-to-all-done = f32[32,1,256]{2,1,0:T(1,128)S(1)} async-done(((f32[32,1,256]{2,1,0:T(1,128)}), f32[32,1,256]{2,1,0:T(1,128)S(1)}, u32[]{:S(2)}, u32[]{:S(2)}) %all-to-all-start) | async-done | bytes 32800 | tf_op jit(solution)/shard_map/all_to_all | solution.py:575
  33.0 0.2 scale.1
  33.2 0.0 collective-permute-done.3.far_received_ref
  33.2 1.3 %last.1 = (f32[48,4096]{1,0:T(8,128)}, f32[48,4096]{1,0:T(8,128)}, f32[1,16]{1,0:T(1,128)}) custom-call(f32[32,128]{1,0:T(8,128)S(1)} %get-tuple-element.51.scale_ref, f32[8,128]{1,0:T(8,128)S(1)} %get-tuple-element.52.gradient_ref, f32[48,4096]{1,0:T(8,128)S(1)} %get-tuple-element.34.field_ref, f32[48,3584]{1,0:T(8,128)S(1)} %get-tuple-element.53.image_ref, ...), custom_call_target="tpu_custom_call" | custom-call | tf_op jit(solution)/shard_map/last/pallas_call | solution.py:603
  (1 shorter events, 0.0 us)
Async XLA Ops:
  1.5 7.6 %collective-permute-start = (f32[3,16,512]{2,1,0:T(8,128)S(1)}, f32[3,16,512]{2,1,0:T(8,128)S(1)}, u32[]{:S(2)}, u32[]{:S(2)}) collective-permute-start(f32[3,16,512]{2,1,0:T(8,128)S(1)} %slice.3), channel_id=1, source_target_pairs={{4,0},{8,4},{12,8},{16,12},{20,16},{24,20},{28,24},{5,1},{9,5},{13... | collective-permute-start | bytes 294920 | tf_op jit(solution)/shard_map/ppermute | solution.py:25
  6.3 7.5 %copy-start = (f32[3,4096]{1,0:T(4,128)S(1)}, f32[3,4096]{1,0:T(4,128)}, u32[]{:S(2)}) copy-start(f32[3,4096]{1,0:T(4,128)} %weight_ref.3) | copy-start | bytes 147460
  11.0 5.4 %collective-permute-start.1 = (f32[48,512]{1,0:T(8,128)S(1)}, f32[48,512]{1,0:T(8,128)S(1)}, u32[]{:S(2)}, u32[]{:S(2)}) collective-permute-start(f32[48,512]{1,0:T(8,128)S(1)} %get-tuple-element.42), channel_id=1, source_target_pairs={{0,4},{1,5},{2,6},{3,7},{4,0},{5,1},{6,2},{7,3},{8,12},{9,13},{10,... | collective-permute-start | bytes 294920 | tf_op jit(solution)/shard_map/ppermute | solution.py:39
  13.8 2.6 %collective-permute-start.2 = (f32[48,512]{1,0:T(8,128)S(1)}, f32[48,512]{1,0:T(8,128)S(1)}, u32[]{:S(2)}, u32[]{:S(2)}) collective-permute-start(f32[48,512]{1,0:T(8,128)S(1)} %get-tuple-element.43), channel_id=1, source_target_pairs={{0,1},{1,0},{2,3},{3,2},{4,8},{5,9},{6,10},{7,11},{8,4},{9,5},{10,... | collective-permute-start | bytes 294920 | tf_op jit(solution)/shard_map/ppermute | solution.py:39
  15.8 3.1 %copy-start.1 = (f32[48,3584]{1,0:T(8,128)}, f32[48,3584]{1,0:T(8,128)S(1)}, u32[]{:S(2)}) copy-start(f32[48,3584]{1,0:T(8,128)S(1)} %get-tuple-element.57.elastic_ref) | copy-start | bytes 2064388
  18.9 14.1 %all-to-all-start = ((f32[32,1,256]{2,1,0:T(1,128)}), f32[32,1,256]{2,1,0:T(1,128)S(1)}, u32[]{:S(2)}, u32[]{:S(2)}) async-start(f32[32,1,256]{2,1,0:T(1,128)} %get-tuple-element.50), calls=%async_computation | async-start | bytes 65536 | tf_op jit(solution)/shard_map/all_to_all | solution.py:575
  25.7 4.8 %copy-start.2 = (f32[48,3584]{1,0:T(8,128)S(1)}, f32[48,3584]{1,0:T(8,128)}, u32[]{:S(2)}) copy-start(f32[48,3584]{1,0:T(8,128)} %copy-done.1) | copy-start | bytes 2064388
  26.8 6.3 %collective-permute-start.3 = (f32[48,512]{1,0:T(8,128)S(1)}, f32[48,512]{1,0:T(8,128)S(1)}, u32[]{:S(2)}, u32[]{:S(2)}) collective-permute-start(f32[48,512]{1,0:T(8,128)S(1)} %settle.1), channel_id=1, source_target_pairs={{0,4},{4,8},{8,12},{12,16},{16,20},{20,24},{24,28},{1,5},{5,9},{9,... | collective-permute-start | bytes 294920 | tf_op jit(solution)/shard_map/ppermute | solution.py:25

commit v6 on v5

--- a/solution.py
+++ b/solution.py
@@ -105,6 +105,17 @@
     return dot(row_high, right_high) + (dot(row_low, right_high) + dot(row_high, right_low))
 
 
+def stacked_product(rows, high, low):
+    row_high, row_low = split(rows)
+    product = jnp.dot(
+        jnp.concatenate([row_high, row_low], axis=0),
+        jnp.concatenate(block_diagonal(high, low), axis=1),
+        preferred_element_type=jnp.float32,
+    )
+    count = rows.shape[0]
+    return product[:count, :LANES] + (product[count:, :LANES] + product[:count, LANES:])
+
+
 def fill_twins(field_tile, twin_ref, patch):
     swapped = pltpu.roll(field_tile, PN, 1)
     left = left_half(field_tile.shape)
@@ -117,14 +128,14 @@
 
 
 def scatter(force, step, targets):
-    left = left_half(force.shape)
-    for slot, half in ((2 * step, jnp.where(left, force, 0.0)), (2 * step + 1, jnp.where(left, 0.0, force))):
+    for slot in (2 * step, 2 * step + 1):
         for ref, patch, sign in targets(slot):
-            ref[patch] = ref[patch] + half if sign > 0 else ref[patch] - half
-
-
-def folded(total_ref, patch):
-    first, second = total_ref[patch], total_ref[patch + 1]
+            ref[patch] = ref[patch] + force if sign > 0 else ref[patch] - force
+
+
+def folded(total_ref, patch, other_ref):
+    first = side_by_side(total_ref[patch], other_ref[patch])
+    second = side_by_side(total_ref[patch + 1], other_ref[patch + 1])
     first = first + pltpu.roll(first, PN, 1)
     second = second + pltpu.roll(second, PN, 1)
     return jnp.where(left_half(first.shape), first, second)
@@ -169,12 +180,13 @@
 
 def couple_kernel(
     count_ref, local_vmem, partner_vmem, field_ref, elastic_ref, halo_ref, high_ref, low_ref,
-    total_ref, gap_ref, force_ref, own_ref, spread_ref, even_ref, odd_ref,
+    total_ref, other_ref, gap_ref, force_ref, own_ref, spread_ref, even_ref, odd_ref,
     local_ref, partner_ref, table_sems, twin_ref,
 ):
     slots = Slots((local_vmem, partner_vmem), (local_ref, partner_ref), table_sems)
     patches = field_ref.shape[1] // PN
     clear(total_ref)
+    clear(other_ref)
     for index in range(patches // 2):
         fill_twins(tile(field_ref, index), twin_ref, 2 * index)
     for index in range(NB // 2):
@@ -185,18 +197,19 @@
         return (twin_ref[slots.local[slot]] - twin_ref[slots.partner[slot]]) * live(count_ref, slot)
 
     def targets(slot):
-        return (total_ref, slots.local[slot], 1), (total_ref, slots.partner[slot], -1)
+        ref = (total_ref, other_ref)[slot % 2]
+        return (ref, slots.local[slot], 1), (ref, slots.partner[slot], -1)
 
     for step in range(high_ref.shape[1] // LANES):
         gap = side_by_side(slot_gap(2 * step), slot_gap(2 * step + 1))
-        force = pair_product(gap, tile(high_ref, step), tile(low_ref, step))
+        force = stacked_product(gap, tile(high_ref, step), tile(low_ref, step))
         put(gap_ref, step, gap)
         put(force_ref, step, force)
         scatter(force, step, targets)
     even = lax.axis_index("dom") % 2 == 0
     for index in range(NB // 2):
-        value = tile(elastic_ref, index) + folded(total_ref, 2 * index)
-        spread = folded(total_ref, patches + 2 * index)
+        value = tile(elastic_ref, index) + folded(total_ref, 2 * index, other_ref)
+        spread = folded(total_ref, patches + 2 * index, other_ref)
         put(own_ref, index, value)
         put(spread_ref, index, spread)
         put(even_ref, index, jnp.where(even, spread, value))
@@ -248,7 +261,7 @@
 
 
 def lift_kernel(
-    local_vmem, partner_vmem, field_ref, total_ref, field_elastic_ref, stiff_high_ref, stiff_low_ref, weight_ref,
+    local_vmem, partner_vmem, field_ref, total_ref, other_ref, field_elastic_ref, stiff_high_ref, stiff_low_ref, weight_ref,
     image_ref, elastic_ref, near_ref, sums_ref, trial_ref,
     local_ref, partner_ref, table_sems, twin_ref, *, columns,
 ):
@@ -264,7 +277,7 @@
         sums.add(8, weight_tile * field_tile)
         if index < lead:
             continue
-        image_tile = tile(field_elastic_ref, index) + folded(total_ref, 2 * index)
+        image_tile = tile(field_elastic_ref, index) + folded(total_ref, 2 * index, other_ref)
         put(image_ref, index - lead, image_tile)
         fill_twins(image_tile, twin_ref, 2 * index)
         product = pair_product(image_tile, tile(stiff_high_ref, index), tile(stiff_low_ref, index))
@@ -350,7 +363,7 @@
         gap = tile(near_ref, step) + side_by_side(outer_gap(2 * step), outer_gap(2 * step + 1))
         lives = [jnp.full(gap.shape, live(count_ref, 2 * step + side), jnp.float32) for side in range(2)]
         gap = gap * side_by_side(*lives)
-        force = pair_product(gap, tile(contact_high_ref, step), tile(contact_low_ref, step))
+        force = stacked_product(gap, tile(contact_high_ref, step), tile(contact_low_ref, step))
         put(image_force_ref, step, force)
         add_energy(sums, trial_rows, tile(gap_ref, step), tile(force_ref, step), gap, force)
     lane = lax.broadcasted_iota(jnp.int32, (columns, LANES), 1)
@@ -367,41 +380,44 @@
 
 
 def settle_kernel(
-    local_vmem, partner_vmem, force_ref, far_spread_ref, local_ref, partner_ref, table_sems, total_ref, *, patches
+    local_vmem, partner_vmem, force_ref, far_spread_ref, local_ref, partner_ref, table_sems, total_ref, other_ref, *, patches
 ):
     slots = Slots((local_vmem, partner_vmem), (local_ref, partner_ref), table_sems)
     clear(total_ref)
+    clear(other_ref)
     slots.wait()
 
     def targets(slot):
         partner = slots.partner[slot]
-        return ((total_ref, jnp.where(partner < patches, NB, partner - patches), -1),)
+        return (((total_ref, other_ref)[slot % 2], jnp.where(partner < patches, NB, partner - patches), -1),)
 
     for step in range(force_ref.shape[1] // LANES):
         scatter(tile(force_ref, step), step, targets)
     for index in range(NB // 2):
-        put(far_spread_ref, index, folded(total_ref, 2 * index))
+        put(far_spread_ref, index, folded(total_ref, 2 * index, other_ref))
 
 
 def gather_kernel(
     local_vmem, partner_vmem, force_ref, lead_elastic_ref, elastic_ref, twice_ref,
-    local_ref, partner_ref, table_sems, total_ref,
+    local_ref, partner_ref, table_sems, total_ref, other_ref,
 ):
     slots = Slots((local_vmem, partner_vmem), (local_ref, partner_ref), table_sems)
     patches = twice_ref.shape[1] // PN
     lead = NB // 2
     clear(total_ref)
+    clear(other_ref)
     slots.wait()
 
     def targets(slot):
         partner = slots.partner[slot]
-        return (total_ref, slots.local[slot], 1), (total_ref, jnp.where(partner < patches, partner, patches), -1)
+        ref = (total_ref, other_ref)[slot % 2]
+        return (ref, slots.local[slot], 1), (ref, jnp.where(partner < patches, partner, patches), -1)
 
     for step in range(force_ref.shape[1] // LANES):
         scatter(tile(force_ref, step), step, targets)
     for index in range(patches // 2):
         product = tile(lead_elastic_ref, index) if index < lead else tile(elastic_ref, index - lead)
-        put(twice_ref, index, product + folded(total_ref, 2 * index))
+        put(twice_ref, index, product + folded(total_ref, 2 * index, other_ref))
 
 
 def scale_kernel(moment_ref, scale_ref, gradient_ref, *, columns, groups):
@@ -519,13 +535,12 @@
     pairs = (in_hbm(pair_local), in_hbm(pair_partner))
     slots = shape((rows, contact.shape[1]), f32)
 
-    def scratch(count):
+    def scratch(count, copies=1):
         return [
             pltpu.SMEM(pair_local.shape, jnp.int32),
             pltpu.SMEM(pair_partner.shape, jnp.int32),
             pltpu.SemaphoreType.DMA((2,)),
-            pltpu.VMEM((count, rows, LANES), f32),
-        ]
+        ] + [pltpu.VMEM((count, rows, LANES), f32)] * copies
 
     halo = shifted(right_side[:, :, :width], "dom", -1).reshape(rows, width)
     field, field_elastic, stiff_high, stiff_low, contact_high, contact_low, *tables = call(
@@ -542,11 +557,11 @@
         ],
         name="prepare",
     )(field_hbm, in_hbm(stiffness), in_hbm(contact), *pairs)
-    total, gap, force, own, spread, even, odd = call(
+    total, other, gap, force, own, spread, even, odd = call(
         couple_kernel,
-        out_shape=(shape((patches + NB, rows, LANES), f32), slots, slots, narrow, narrow, narrow, narrow),
+        out_shape=(*[shape((patches + NB, rows, LANES), f32)] * 2, slots, slots, narrow, narrow, narrow, narrow),
         in_specs=[SMEM] + [VMEM] * 7,
-        out_specs=(VMEM,) * 7,
+        out_specs=(VMEM,) * 8,
         scratch_shapes=scratch(patches + NB),
         name="couple",
     )(pair_count, *tables, field, field_elastic, halo, contact_high, contact_low)
@@ -556,11 +571,11 @@
     image, elastic, near, sums, trial = call(
         functools.partial(lift_kernel, columns=columns),
         out_shape=(tail, tail, slots, shape((SUMS * columns, LANES), f32), shape((columns, LANES), f32)),
-        in_specs=[VMEM] * 8,
+        in_specs=[VMEM] * 9,
         out_specs=(VMEM,) * 5,
         scratch_shapes=scratch(patches + 1),
         name="lift",
-    )(*tables, field, total, field_elastic, stiff_high, stiff_low, objective_weight)
+    )(*tables, field, total, other, field_elastic, stiff_high, stiff_low, objective_weight)
     lead, lead_elastic, image_force, moments = call(
         functools.partial(energy_kernel, columns=columns),
         out_shape=(narrow, narrow, slots, shape((devices, 1, MOMENT_LANES), f32)),
@@ -578,7 +593,7 @@
         out_shape=narrow,
         in_specs=[VMEM] * 3,
         out_specs=VMEM,
-        scratch_shapes=scratch(NB + 1),
+        scratch_shapes=scratch(NB + 1, 2),
         cost_estimate=pl.CostEstimate(flops=10**9, bytes_accessed=rows * nodes * 4, transcendentals=0),
         name="settle",
     )(*tables, image_force)
@@ -588,7 +603,7 @@
         out_shape=wide,
         in_specs=[VMEM] * 5,
         out_specs=VMEM,
-        scratch_shapes=scratch(patches + 1),
+        scratch_shapes=scratch(patches + 1, 2),
         cost_estimate=pl.CostEstimate(flops=10**9, bytes_accessed=3 * rows * nodes * 4, transcendentals=0),
         name="gather",
     )(*tables, image_force, lead_elastic, elastic)

time: 34.7 us -> 34.5 us (level)
  Pallas kernels: 13.4 us -> 12.7 us
  waiting for transfers between devices: 4.17 us -> 4.64 us
    all_to_all x1, waiting for transfers between devices: 0.71 us -> 1.17 us  [shards(): lax.all_to_all(moments, ('dom', 'col'), 0, 0, tiled=True)]
  transfers between devices with their start and end apart: 5 -> 5, of which waited for: 3 -> 3; matrix products, arithmetic and copies ran while one was open for 0% -> 0% of each run, Pallas kernels for 23% -> 22%
where the time goes in v6:
time: 34.5 us; the launch traced here: 34.2 us
  starting transfers between devices  14.5 us (42%)
  Pallas kernels  12.7 us (37%)
  waiting for transfers between devices  4.64 us (13%)
  between operations  1.39 us (4%)
  local copies, waits for them, and re-layouts  0.92 us (3%)
    all_to_all x1, starting transfers between devices, shards(): lax.all_to_all(moments, ('dom', 'col'), 0, 0, tiled=True)  6.81 us
    ppermute x2, starting transfers between devices, shifted(): return lax.ppermute(value, axis, pairs)  4.96 us
    ppermute x2, waiting for transfers between devices, shifted(): return lax.ppermute(value, axis, pairs)  2.86 us
    pallas_call x1, Pallas kernels, shards(): call(prepare_kernel, out_shape=(wide, wide, *parts, *(shape(pair.shape, j...  2.84 us
    ppermute x2, starting transfers between devices, swapped(): return lax.ppermute(value, ('dom', 'col'), pairs)  2.79 us
    pallas_call x1, Pallas kernels, shards(): call(functools.partial(energy_kernel, columns=columns), out_shape=(narrow...  2.45 us
    pallas_call x1, Pallas kernels, shards(): call(functools.partial(lift_kernel, columns=columns), out_shape=(tail, ta...  1.96 us
    pallas_call x1, Pallas kernels, shards(): call(couple_kernel, out_shape=(*[shape((patches + NB, rows, LANES), f32)]...  1.63 us
  transfers between devices with their start and end apart: 5, of which 3 were waited for; matrix products, arithmetic and copies ran while one was open for 0% of the time, Pallas kernels for 22%

profile of v6, /device:TPU:0, one launch (start us, length us, event | category | flops | bytes accessed | tf_op | source)
XLA Modules:
  0.0 34.2 jit_solution(2608046406261253072)
XLA Ops:
  0.6 0.9 %slice.3 = f32[3,16,512]{2,1,0:T(8,128)S(1)} slice(f32[3,16,4096]{2,1,0:T(8,128)} %param.7), slice={[0:3], [0:16], [0:512]} | slice | bytes 196608 | tf_op jit(solution)/shard_map/slice | solution.py:545
  1.5 1.3 %collective-permute-start = (f32[3,16,512]{2,1,0:T(8,128)S(1)}, f32[3,16,512]{2,1,0:T(8,128)S(1)}, u32[]{:S(2)}, u32[]{:S(2)}) collective-permute-start(f32[3,16,512]{2,1,0:T(8,128)S(1)} %slice.3), channel_id=1, source_target_pairs={{4,0},{8,4},{12,8},{16,12},{20,16},{24,20},{28,24},{5,1},{9,5},{13... | collective-permute-start | bytes 294920 | tf_op jit(solution)/shard_map/ppermute | solution.py:25
  3.5 2.8 %prepare.1 = (f32[48,4096]{1,0:T(8,128)S(1)}, f32[48,4096]{1,0:T(8,128)S(1)}, bf16[64,4096]{1,0:T(8,128)(2,1)S(1)}, bf16[64,4096]{1,0:T(8,128)(2,1)S(1)}, bf16[6...) custom-call(f32[48,4096]{1,0:T(8,128)} %bitcast.10, ...), custom_call_target="tpu_custom_call" | custom-call | tf_op jit(solution)/shard_map/prepare/pallas_call | solution.py:546
  6.3 0.0 copy-start
  6.3 2.9 %collective-permute-done = f32[3,16,512]{2,1,0:T(8,128)S(1)} collective-permute-done((f32[3,16,512]{2,1,0:T(8,128)S(1)}, f32[3,16,512]{2,1,0:T(8,128)S(1)}, u32[]{:S(2)}, u32[]{:S(2)}) %collective-permute-start) | collective-permute-done | bytes 98336 | tf_op jit(solution)/shard_map/ppermute | solution.py:25
  9.2 1.6 %couple.1 = (f32[72,48,128]{2,1,0:T(8,128)S(1)}, f32[72,48,128]{2,1,0:T(8,128)S(1)}, f32[48,4096]{1,0:T(8,128)S(1)}, f32[48,4096]{1,0:T(8,128)S(1)}, f32[48,512]...) custom-call(s32[1]{0:T(128)S(6)} %copy.14.count_ref, ...), custom_call_target="tpu_custom_call" | custom-call | tf_op jit(solution)/shard_map/couple/pallas_call | solution.py:560
  10.8 2.8 %collective-permute-start.1 = (f32[48,512]{1,0:T(8,128)S(1)}, f32[48,512]{1,0:T(8,128)S(1)}, u32[]{:S(2)}, u32[]{:S(2)}) collective-permute-start(f32[48,512]{1,0:T(8,128)S(1)} %get-tuple-element.43), channel_id=1, source_target_pairs={{0,4},{1,5},{2,6},{3,7},{4,0},{5,1},{6,2},{7,3},{8,12},{9,13},{10,... | collective-permute-start | bytes 294920 | tf_op jit(solution)/shard_map/ppermute | solution.py:39
  13.6 0.0 collective-permute-start.2
  13.6 0.0 copy-done
  13.6 2.0 %lift.1 = (f32[48,3584]{1,0:T(8,128)S(1)}, f32[48,3584]{1,0:T(8,128)S(1)}, f32[48,4096]{1,0:T(8,128)S(1)}, f32[160,128]{1,0:T(8,128)S(1)}, f32[16,128]{1,0:T(8,128)S(1)}) custom-call(s32[64]{0:T(128)S(1)} %get-tuple-element.33.local_vmem, s32[64]{0:T(128)S(1)} %get-tuple-element.34.partner_vmem, f32[48,4096]{1,0:T(8,128)S(1)} %get-tuple-element.35.field_ref, ...), custom_call_target="tpu_custom_call" | custom-call | tf_op jit(solution)/shard_map/lift/pallas_call | solution.py:571
  15.6 0.0 copy-start.1
  15.6 0.6 %collective-permute-done.1.even_ref = f32[48,512]{1,0:T(8,128)S(1)} collective-permute-done((f32[48,512]{1,0:T(8,128)S(1)}, f32[48,512]{1,0:T(8,128)S(1)}, u32[]{:S(2)}, u32[]{:S(2)}) %collective-permute-start.1) | collective-permute-done | bytes 98336 | tf_op jit(solution)/shard_map/ppermute | solution.py:39
  16.2 0.0 collective-permute-done.2.odd_ref
  16.2 2.4 %energy.1 = (f32[48,512]{1,0:T(8,128)S(1)}, f32[48,512]{1,0:T(8,128)S(1)}, f32[48,4096]{1,0:T(8,128)S(1)}, f32[32,1,256]{2,1,0:T(1,128)}) custom-call(s32[1]{0:T(128)S(6)} %copy.14.count_ref, s32[64]{0:T(128)S(1)} %get-tuple-element.33.local_vmem, s32[64]{0:T(128)S(1)} %get-tuple-element.34.partner_vmem, f32[48,4096]{1,0:T(8,128)S(1)} %get-tuple-element.35.field_ref, ...), custom_call_target="tpu_custom_call" | custom-call | tf_op jit(solution)/shard_map/energy/pallas_call | solution.py:579
  18.7 0.0 copy-done.1
  18.7 6.8 %all-to-all-start = ((f32[32,1,256]{2,1,0:T(1,128)}), f32[32,1,256]{2,1,0:T(1,128)S(1)}, u32[]{:S(2)}, u32[]{:S(2)}) async-start(f32[32,1,256]{2,1,0:T(1,128)} %get-tuple-element.52), calls=%async_computation | async-start | bytes 65536 | tf_op jit(solution)/shard_map/all_to_all | solution.py:590
  25.5 0.0 copy-start.2
  25.5 0.9 %settle.1 = f32[48,512]{1,0:T(8,128)S(1)} custom-call(s32[64]{0:T(128)S(1)} %get-tuple-element.33.local_vmem, s32[64]{0:T(128)S(1)} %get-tuple-element.34.partner_vmem, f32[48,4096]{1,0:T(8,128)S(1)} %get-tuple-element.57.force_ref), custom_call_target="tpu_custom_call" | custom-call | flops 1000000000 | bytes 786432 | tf_op jit(solution)/shard_map/settle/pallas_call | solution.py:591
  26.4 3.7 %collective-permute-start.3 = (f32[48,512]{1,0:T(8,128)S(1)}, f32[48,512]{1,0:T(8,128)S(1)}, u32[]{:S(2)}, u32[]{:S(2)}) collective-permute-start(f32[48,512]{1,0:T(8,128)S(1)} %settle.1), channel_id=1, source_target_pairs={{0,4},{4,8},{8,12},{12,16},{16,20},{20,24},{24,28},{1,5},{5,9},{9,... | collective-permute-start | bytes 294920 | tf_op jit(solution)/shard_map/ppermute | solution.py:25
  30.1 0.0 copy-done.2
  30.1 1.5 %gather.1.twice_ref = f32[48,4096]{1,0:T(8,128)S(1)} custom-call(s32[64]{0:T(128)S(1)} %get-tuple-element.33.local_vmem, s32[64]{0:T(128)S(1)} %get-tuple-element.34.partner_vmem, f32[48,4096]{1,0:T(8,128)S(1)} %get-tuple-element.57.force_ref, f32[48,512]{1,0:T(8,128)S(1)} %get-tuple-element.58.lead_elastic_ref, f32[48,3584]{1,0:T(8,128)S(1)} %copy-done.2), custom_call_target="tpu_custom_call" | custom-call | flops 1000000000 | bytes 2359296 | tf_op jit(solution)/shard_map/gather/pallas_call | solution.py:601
  31.6 1.2 %all-to-all-done = f32[32,1,256]{2,1,0:T(1,128)S(1)} async-done(((f32[32,1,256]{2,1,0:T(1,128)}), f32[32,1,256]{2,1,0:T(1,128)S(1)}, u32[]{:S(2)}, u32[]{:S(2)}) %all-to-all-start) | async-done | bytes 32800 | tf_op jit(solution)/shard_map/all_to_all | solution.py:590
  32.7 0.2 scale.1
  32.9 0.0 collective-permute-done.3.far_received_ref
  32.9 1.3 %last.1 = (f32[48,4096]{1,0:T(8,128)}, f32[48,4096]{1,0:T(8,128)}, f32[1,16]{1,0:T(1,128)}) custom-call(f32[32,128]{1,0:T(8,128)S(1)} %get-tuple-element.53.scale_ref, f32[8,128]{1,0:T(8,128)S(1)} %get-tuple-element.54.gradient_ref, f32[48,4096]{1,0:T(8,128)S(1)} %get-tuple-element.35.field_ref, f32[48,3584]{1,0:T(8,128)S(1)} %get-tuple-element.55.image_ref, ...), custom_call_target="tpu_custom_call" | custom-call | tf_op jit(solution)/shard_map/last/pallas_call | solution.py:618
  (1 shorter events, 0.0 us)
Async XLA Ops:
  1.5 7.6 %collective-permute-start = (f32[3,16,512]{2,1,0:T(8,128)S(1)}, f32[3,16,512]{2,1,0:T(8,128)S(1)}, u32[]{:S(2)}, u32[]{:S(2)}) collective-permute-start(f32[3,16,512]{2,1,0:T(8,128)S(1)} %slice.3), channel_id=1, source_target_pairs={{4,0},{8,4},{12,8},{16,12},{20,16},{24,20},{28,24},{5,1},{9,5},{13... | collective-permute-start | bytes 294920 | tf_op jit(solution)/shard_map/ppermute | solution.py:25
  6.3 7.3 %copy-start = (f32[3,4096]{1,0:T(4,128)S(1)}, f32[3,4096]{1,0:T(4,128)}, u32[]{:S(2)}) copy-start(f32[3,4096]{1,0:T(4,128)} %weight_ref.3) | copy-start | bytes 147460
  10.8 5.4 %collective-permute-start.1 = (f32[48,512]{1,0:T(8,128)S(1)}, f32[48,512]{1,0:T(8,128)S(1)}, u32[]{:S(2)}, u32[]{:S(2)}) collective-permute-start(f32[48,512]{1,0:T(8,128)S(1)} %get-tuple-element.43), channel_id=1, source_target_pairs={{0,4},{1,5},{2,6},{3,7},{4,0},{5,1},{6,2},{7,3},{8,12},{9,13},{10,... | collective-permute-start | bytes 294920 | tf_op jit(solution)/shard_map/ppermute | solution.py:39
  13.6 2.6 %collective-permute-start.2 = (f32[48,512]{1,0:T(8,128)S(1)}, f32[48,512]{1,0:T(8,128)S(1)}, u32[]{:S(2)}, u32[]{:S(2)}) collective-permute-start(f32[48,512]{1,0:T(8,128)S(1)} %get-tuple-element.44), channel_id=1, source_target_pairs={{0,1},{1,0},{2,3},{3,2},{4,8},{5,9},{6,10},{7,11},{8,4},{9,5},{10,... | collective-permute-start | bytes 294920 | tf_op jit(solution)/shard_map/ppermute | solution.py:39
  15.6 3.1 %copy-start.1 = (f32[48,3584]{1,0:T(8,128)}, f32[48,3584]{1,0:T(8,128)S(1)}, u32[]{:S(2)}) copy-start(f32[48,3584]{1,0:T(8,128)S(1)} %get-tuple-element.59.elastic_ref) | copy-start | bytes 2064388
  18.7 14.1 %all-to-all-start = ((f32[32,1,256]{2,1,0:T(1,128)}), f32[32,1,256]{2,1,0:T(1,128)S(1)}, u32[]{:S(2)}, u32[]{:S(2)}) async-start(f32[32,1,256]{2,1,0:T(1,128)} %get-tuple-element.52), calls=%async_computation | async-start | bytes 65536 | tf_op jit(solution)/shard_map/all_to_all | solution.py:590
  25.5 4.6 %copy-start.2 = (f32[48,3584]{1,0:T(8,128)S(1)}, f32[48,3584]{1,0:T(8,128)}, u32[]{:S(2)}) copy-start(f32[48,3584]{1,0:T(8,128)} %copy-done.1) | copy-start | bytes 2064388
  26.4 6.5 %collective-permute-start.3 = (f32[48,512]{1,0:T(8,128)S(1)}, f32[48,512]{1,0:T(8,128)S(1)}, u32[]{:S(2)}, u32[]{:S(2)}) collective-permute-start(f32[48,512]{1,0:T(8,128)S(1)} %settle.1), channel_id=1, source_target_pairs={{0,4},{4,8},{8,12},{12,16},{16,20},{20,24},{24,28},{1,5},{5,9},{9,... | collective-permute-start | bytes 294920 | tf_op jit(solution)/shard_map/ppermute | solution.py:25

commit v7 on v6

--- a/solution.py
+++ b/solution.py
@@ -70,10 +70,6 @@
     def wait(self):
         for copy in self.copies:
             copy.wait()
-
-
-def live(count_ref, slot):
-    return jnp.where(slot < count_ref[0], 1.0, 0.0)
 
 
 def chunked(sources, targets, sems, chunk):
@@ -194,7 +190,9 @@
     slots.wait()
 
     def slot_gap(slot):
-        return (twin_ref[slots.local[slot]] - twin_ref[slots.partner[slot]]) * live(count_ref, slot)
+        patch = slots.local[slot]
+        partner = jnp.where(slot < count_ref[0], slots.partner[slot], patch)
+        return twin_ref[patch] - twin_ref[partner]
 
     def targets(slot):
         ref = (total_ref, other_ref)[slot % 2]
@@ -261,7 +259,7 @@
 
 
 def lift_kernel(
-    local_vmem, partner_vmem, field_ref, total_ref, other_ref, field_elastic_ref, stiff_high_ref, stiff_low_ref, weight_ref,
+    count_ref, local_vmem, partner_vmem, field_ref, total_ref, other_ref, field_elastic_ref, stiff_high_ref, stiff_low_ref, weight_ref,
     image_ref, elastic_ref, near_ref, sums_ref, trial_ref,
     local_ref, partner_ref, table_sems, twin_ref, *, columns,
 ):
@@ -304,11 +302,11 @@
     twin_ref[patches] = jnp.zeros(twin_ref.shape[1:], jnp.float32)
     slots.wait()
 
-    def inner(patch):
-        return twin_ref[jnp.where((patch >= NB) & (patch < patches), patch, patches)]
+    def inner(slot, patch):
+        return twin_ref[jnp.where((slot < count_ref[0]) & (patch >= NB) & (patch < patches), patch, patches)]
 
     def inner_gap(slot):
-        return inner(slots.local[slot]) - inner(slots.partner[slot])
+        return inner(slot, slots.local[slot]) - inner(slot, slots.partner[slot])
 
     for step in range(near_ref.shape[1] // LANES):
         put(near_ref, step, side_by_side(inner_gap(2 * step), inner_gap(2 * step + 1)))
@@ -352,17 +350,15 @@
     twin_ref[2 * NB] = jnp.zeros(twin_ref.shape[1:], jnp.float32)
     slots.wait()
 
-    def outer(patch):
-        far = patch >= patches
-        return twin_ref[jnp.where(far, patch - patches + NB, jnp.where(patch < NB, patch, 2 * NB))]
+    def outer(slot, patch):
+        here = jnp.where(patch >= patches, patch - patches + NB, jnp.where(patch < NB, patch, 2 * NB))
+        return twin_ref[jnp.where(slot < count_ref[0], here, 2 * NB)]
 
     def outer_gap(slot):
-        return outer(slots.local[slot]) - outer(slots.partner[slot])
+        return outer(slot, slots.local[slot]) - outer(slot, slots.partner[slot])
 
     for step in range(contact_high_ref.shape[1] // LANES):
         gap = tile(near_ref, step) + side_by_side(outer_gap(2 * step), outer_gap(2 * step + 1))
-        lives = [jnp.full(gap.shape, live(count_ref, 2 * step + side), jnp.float32) for side in range(2)]
-        gap = gap * side_by_side(*lives)
         force = stacked_product(gap, tile(contact_high_ref, step), tile(contact_low_ref, step))
         put(image_force_ref, step, force)
         add_energy(sums, trial_rows, tile(gap_ref, step), tile(force_ref, step), gap, force)
@@ -571,11 +567,11 @@
     image, elastic, near, sums, trial = call(
         functools.partial(lift_kernel, columns=columns),
         out_shape=(tail, tail, slots, shape((SUMS * columns, LANES), f32), shape((columns, LANES), f32)),
-        in_specs=[VMEM] * 9,
+        in_specs=[SMEM] + [VMEM] * 9,
         out_specs=(VMEM,) * 5,
         scratch_shapes=scratch(patches + 1),
         name="lift",
-    )(*tables, field, total, other, field_elastic, stiff_high, stiff_low, objective_weight)
+    )(pair_count, *tables, field, total, other, field_elastic, stiff_high, stiff_low, objective_weight)
     lead, lead_elastic, image_force, moments = call(
         functools.partial(energy_kernel, columns=columns),
         out_shape=(narrow, narrow, slots, shape((devices, 1, MOMENT_LANES), f32)),

time: 34.5 us -> 34.4 us (level)
  no operation moved by 1% of the time
where the time goes in v7:
time: 34.4 us; the launch traced here: 34.2 us
  starting transfers between devices  14.5 us (42%)
  Pallas kernels  12.9 us (38%)
  waiting for transfers between devices  4.46 us (13%)
  between operations  1.39 us (4%)
  local copies, waits for them, and re-layouts  0.92 us (3%)
    all_to_all x1, starting transfers between devices, shards(): lax.all_to_all(moments, ('dom', 'col'), 0, 0, tiled=True)  6.77 us
    ppermute x2, starting transfers between devices, shifted(): return lax.ppermute(value, axis, pairs)  4.96 us
    ppermute x2, waiting for transfers between devices, shifted(): return lax.ppermute(value, axis, pairs)  2.86 us
    pallas_call x1, Pallas kernels, shards(): call(prepare_kernel, out_shape=(wide, wide, *parts, *(shape(pair.shape, j...  2.84 us
    ppermute x2, starting transfers between devices, swapped(): return lax.ppermute(value, ('dom', 'col'), pairs)  2.79 us
    pallas_call x1, Pallas kernels, shards(): call(functools.partial(energy_kernel, columns=columns), out_shape=(narrow...  2.41 us
    pallas_call x1, Pallas kernels, shards(): call(functools.partial(lift_kernel, columns=columns), out_shape=(tail, ta...  2.13 us
    pallas_call x1, Pallas kernels, shards(): call(couple_kernel, out_shape=(*[shape((patches + NB, rows, LANES), f32)]...  1.63 us
  transfers between devices with their start and end apart: 5, of which 3 were waited for; matrix products, arithmetic and copies ran while one was open for 0% of the time, Pallas kernels for 22%

profile of v7, /device:TPU:0, one launch (start us, length us, event | category | flops | bytes accessed | tf_op | source)
XLA Modules:
  0.0 34.2 jit_solution(12019101613959451539)
XLA Ops:
  0.6 0.9 %slice.3 = f32[3,16,512]{2,1,0:T(8,128)S(1)} slice(f32[3,16,4096]{2,1,0:T(8,128)} %param.7), slice={[0:3], [0:16], [0:512]} | slice | bytes 196608 | tf_op jit(solution)/shard_map/slice | solution.py:541
  1.5 1.3 %collective-permute-start = (f32[3,16,512]{2,1,0:T(8,128)S(1)}, f32[3,16,512]{2,1,0:T(8,128)S(1)}, u32[]{:S(2)}, u32[]{:S(2)}) collective-permute-start(f32[3,16,512]{2,1,0:T(8,128)S(1)} %slice.3), channel_id=1, source_target_pairs={{4,0},{8,4},{12,8},{16,12},{20,16},{24,20},{28,24},{5,1},{9,5},{13... | collective-permute-start | bytes 294920 | tf_op jit(solution)/shard_map/ppermute | solution.py:25
  3.5 2.8 %prepare.1 = (f32[48,4096]{1,0:T(8,128)S(1)}, f32[48,4096]{1,0:T(8,128)S(1)}, bf16[64,4096]{1,0:T(8,128)(2,1)S(1)}, bf16[64,4096]{1,0:T(8,128)(2,1)S(1)}, bf16[6...) custom-call(f32[48,4096]{1,0:T(8,128)} %bitcast.10, ...), custom_call_target="tpu_custom_call" | custom-call | tf_op jit(solution)/shard_map/prepare/pallas_call | solution.py:542
  6.3 0.0 copy-start
  6.3 2.9 %collective-permute-done = f32[3,16,512]{2,1,0:T(8,128)S(1)} collective-permute-done((f32[3,16,512]{2,1,0:T(8,128)S(1)}, f32[3,16,512]{2,1,0:T(8,128)S(1)}, u32[]{:S(2)}, u32[]{:S(2)}) %collective-permute-start) | collective-permute-done | bytes 98336 | tf_op jit(solution)/shard_map/ppermute | solution.py:25
  9.2 1.6 %couple.1 = (f32[72,48,128]{2,1,0:T(8,128)S(1)}, f32[72,48,128]{2,1,0:T(8,128)S(1)}, f32[48,4096]{1,0:T(8,128)S(1)}, f32[48,4096]{1,0:T(8,128)S(1)}, f32[48,512]...) custom-call(s32[1]{0:T(128)S(6)} %copy.14.count_ref, ...), custom_call_target="tpu_custom_call" | custom-call | tf_op jit(solution)/shard_map/couple/pallas_call | solution.py:556
  10.8 2.8 %collective-permute-start.1 = (f32[48,512]{1,0:T(8,128)S(1)}, f32[48,512]{1,0:T(8,128)S(1)}, u32[]{:S(2)}, u32[]{:S(2)}) collective-permute-start(f32[48,512]{1,0:T(8,128)S(1)} %get-tuple-element.43), channel_id=1, source_target_pairs={{0,4},{1,5},{2,6},{3,7},{4,0},{5,1},{6,2},{7,3},{8,12},{9,13},{10,... | collective-permute-start | bytes 294920 | tf_op jit(solution)/shard_map/ppermute | solution.py:39
  13.6 0.0 collective-permute-start.2
  13.6 0.0 copy-done
  13.6 2.1 %lift.1 = (f32[48,3584]{1,0:T(8,128)S(1)}, f32[48,3584]{1,0:T(8,128)S(1)}, f32[48,4096]{1,0:T(8,128)S(1)}, f32[160,128]{1,0:T(8,128)S(1)}, f32[16,128]{1,0:T(8,128)S(1)}) custom-call(s32[1]{0:T(128)S(6)} %copy.14.count_ref, s32[64]{0:T(128)S(1)} %get-tuple-element.33.local_vmem, s32[64]{0:T(128)S(1)} %get-tuple-element.34.partner_vmem, ...), custom_call_target="tpu_custom_call" | custom-call | tf_op jit(solution)/shard_map/lift/pallas_call | solution.py:567
  15.8 0.0 copy-start.1
  15.8 0.4 %collective-permute-done.1.even_ref = f32[48,512]{1,0:T(8,128)S(1)} collective-permute-done((f32[48,512]{1,0:T(8,128)S(1)}, f32[48,512]{1,0:T(8,128)S(1)}, u32[]{:S(2)}, u32[]{:S(2)}) %collective-permute-start.1) | collective-permute-done | bytes 98336 | tf_op jit(solution)/shard_map/ppermute | solution.py:39
  16.2 0.0 collective-permute-done.2.odd_ref
  16.2 2.4 %energy.1 = (f32[48,512]{1,0:T(8,128)S(1)}, f32[48,512]{1,0:T(8,128)S(1)}, f32[48,4096]{1,0:T(8,128)S(1)}, f32[32,1,256]{2,1,0:T(1,128)}) custom-call(s32[1]{0:T(128)S(6)} %copy.14.count_ref, s32[64]{0:T(128)S(1)} %get-tuple-element.33.local_vmem, s32[64]{0:T(128)S(1)} %get-tuple-element.34.partner_vmem, f32[48,4096]{1,0:T(8,128)S(1)} %get-tuple-element.35.field_ref, ...), custom_call_target="tpu_custom_call" | custom-call | tf_op jit(solution)/shard_map/energy/pallas_call | solution.py:575
  18.6 0.0 copy-done.1
  18.6 6.8 %all-to-all-start = ((f32[32,1,256]{2,1,0:T(1,128)}), f32[32,1,256]{2,1,0:T(1,128)S(1)}, u32[]{:S(2)}, u32[]{:S(2)}) async-start(f32[32,1,256]{2,1,0:T(1,128)} %get-tuple-element.52), calls=%async_computation | async-start | bytes 65536 | tf_op jit(solution)/shard_map/all_to_all | solution.py:586
  25.4 0.0 copy-start.2
  25.4 0.9 %settle.1 = f32[48,512]{1,0:T(8,128)S(1)} custom-call(s32[64]{0:T(128)S(1)} %get-tuple-element.33.local_vmem, s32[64]{0:T(128)S(1)} %get-tuple-element.34.partner_vmem, f32[48,4096]{1,0:T(8,128)S(1)} %get-tuple-element.57.force_ref), custom_call_target="tpu_custom_call" | custom-call | flops 1000000000 | bytes 786432 | tf_op jit(solution)/shard_map/settle/pallas_call | solution.py:587
  26.4 3.7 %collective-permute-start.3 = (f32[48,512]{1,0:T(8,128)S(1)}, f32[48,512]{1,0:T(8,128)S(1)}, u32[]{:S(2)}, u32[]{:S(2)}) collective-permute-start(f32[48,512]{1,0:T(8,128)S(1)} %settle.1), channel_id=1, source_target_pairs={{0,4},{4,8},{8,12},{12,16},{16,20},{20,24},{24,28},{1,5},{5,9},{9,... | collective-permute-start | bytes 294920 | tf_op jit(solution)/shard_map/ppermute | solution.py:25
  30.0 0.0 copy-done.2
  30.0 1.5 %gather.1.twice_ref = f32[48,4096]{1,0:T(8,128)S(1)} custom-call(s32[64]{0:T(128)S(1)} %get-tuple-element.33.local_vmem, s32[64]{0:T(128)S(1)} %get-tuple-element.34.partner_vmem, f32[48,4096]{1,0:T(8,128)S(1)} %get-tuple-element.57.force_ref, f32[48,512]{1,0:T(8,128)S(1)} %get-tuple-element.58.lead_elastic_ref, f32[48,3584]{1,0:T(8,128)S(1)} %copy-done.2), custom_call_target="tpu_custom_call" | custom-call | flops 1000000000 | bytes 2359296 | tf_op jit(solution)/shard_map/gather/pallas_call | solution.py:597
  31.5 1.2 %all-to-all-done = f32[32,1,256]{2,1,0:T(1,128)S(1)} async-done(((f32[32,1,256]{2,1,0:T(1,128)}), f32[32,1,256]{2,1,0:T(1,128)S(1)}, u32[]{:S(2)}, u32[]{:S(2)}) %all-to-all-start) | async-done | bytes 32800 | tf_op jit(solution)/shard_map/all_to_all | solution.py:586
  32.7 0.2 scale.1
  32.9 0.0 collective-permute-done.3.far_received_ref
  32.9 1.3 %last.1 = (f32[48,4096]{1,0:T(8,128)}, f32[48,4096]{1,0:T(8,128)}, f32[1,16]{1,0:T(1,128)}) custom-call(f32[32,128]{1,0:T(8,128)S(1)} %get-tuple-element.53.scale_ref, f32[8,128]{1,0:T(8,128)S(1)} %get-tuple-element.54.gradient_ref, f32[48,4096]{1,0:T(8,128)S(1)} %get-tuple-element.35.field_ref, f32[48,3584]{1,0:T(8,128)S(1)} %get-tuple-element.55.image_ref, ...), custom_call_target="tpu_custom_call" | custom-call | tf_op jit(solution)/shard_map/last/pallas_call | solution.py:614
  (1 shorter events, 0.0 us)
Async XLA Ops:
  1.5 7.6 %collective-permute-start = (f32[3,16,512]{2,1,0:T(8,128)S(1)}, f32[3,16,512]{2,1,0:T(8,128)S(1)}, u32[]{:S(2)}, u32[]{:S(2)}) collective-permute-start(f32[3,16,512]{2,1,0:T(8,128)S(1)} %slice.3), channel_id=1, source_target_pairs={{4,0},{8,4},{12,8},{16,12},{20,16},{24,20},{28,24},{5,1},{9,5},{13... | collective-permute-start | bytes 294920 | tf_op jit(solution)/shard_map/ppermute | solution.py:25
  6.3 7.3 %copy-start = (f32[3,4096]{1,0:T(4,128)S(1)}, f32[3,4096]{1,0:T(4,128)}, u32[]{:S(2)}) copy-start(f32[3,4096]{1,0:T(4,128)} %weight_ref.3) | copy-start | bytes 147460
  10.8 5.4 %collective-permute-start.1 = (f32[48,512]{1,0:T(8,128)S(1)}, f32[48,512]{1,0:T(8,128)S(1)}, u32[]{:S(2)}, u32[]{:S(2)}) collective-permute-start(f32[48,512]{1,0:T(8,128)S(1)} %get-tuple-element.43), channel_id=1, source_target_pairs={{0,4},{1,5},{2,6},{3,7},{4,0},{5,1},{6,2},{7,3},{8,12},{9,13},{10,... | collective-permute-start | bytes 294920 | tf_op jit(solution)/shard_map/ppermute | solution.py:39
  13.6 2.6 %collective-permute-start.2 = (f32[48,512]{1,0:T(8,128)S(1)}, f32[48,512]{1,0:T(8,128)S(1)}, u32[]{:S(2)}, u32[]{:S(2)}) collective-permute-start(f32[48,512]{1,0:T(8,128)S(1)} %get-tuple-element.44), channel_id=1, source_target_pairs={{0,1},{1,0},{2,3},{3,2},{4,8},{5,9},{6,10},{7,11},{8,4},{9,5},{10,... | collective-permute-start | bytes 294920 | tf_op jit(solution)/shard_map/ppermute | solution.py:39
  15.8 2.9 %copy-start.1 = (f32[48,3584]{1,0:T(8,128)}, f32[48,3584]{1,0:T(8,128)S(1)}, u32[]{:S(2)}) copy-start(f32[48,3584]{1,0:T(8,128)S(1)} %get-tuple-element.59.elastic_ref) | copy-start | bytes 2064388
  18.6 14.0 %all-to-all-start = ((f32[32,1,256]{2,1,0:T(1,128)}), f32[32,1,256]{2,1,0:T(1,128)S(1)}, u32[]{:S(2)}, u32[]{:S(2)}) async-start(f32[32,1,256]{2,1,0:T(1,128)} %get-tuple-element.52), calls=%async_computation | async-start | bytes 65536 | tf_op jit(solution)/shard_map/all_to_all | solution.py:586
  25.4 4.6 %copy-start.2 = (f32[48,3584]{1,0:T(8,128)S(1)}, f32[48,3584]{1,0:T(8,128)}, u32[]{:S(2)}) copy-start(f32[48,3584]{1,0:T(8,128)} %copy-done.1) | copy-start | bytes 2064388
  26.4 6.5 %collective-permute-start.3 = (f32[48,512]{1,0:T(8,128)S(1)}, f32[48,512]{1,0:T(8,128)S(1)}, u32[]{:S(2)}, u32[]{:S(2)}) collective-permute-start(f32[48,512]{1,0:T(8,128)S(1)} %settle.1), channel_id=1, source_target_pairs={{0,4},{4,8},{8,12},{12,16},{16,20},{20,24},{24,28},{1,5},{5,9},{9,... | collective-permute-start | bytes 294920 | tf_op jit(solution)/shard_map/ppermute | solution.py:25

commit v8 on v6

--- a/solution.py
+++ b/solution.py
@@ -99,13 +99,6 @@
 
 
 def pair_product(rows, high, low):
-    right_high, right_low = block_diagonal(high, low)
-    row_high, row_low = split(rows)
-    dot = functools.partial(jnp.dot, preferred_element_type=jnp.float32)
-    return dot(row_high, right_high) + (dot(row_low, right_high) + dot(row_high, right_low))
-
-
-def stacked_product(rows, high, low):
     row_high, row_low = split(rows)
     product = jnp.dot(
         jnp.concatenate([row_high, row_low], axis=0),
@@ -202,7 +195,7 @@
 
     for step in range(high_ref.shape[1] // LANES):
         gap = side_by_side(slot_gap(2 * step), slot_gap(2 * step + 1))
-        force = stacked_product(gap, tile(high_ref, step), tile(low_ref, step))
+        force = pair_product(gap, tile(high_ref, step), tile(low_ref, step))
         put(gap_ref, step, gap)
         put(force_ref, step, force)
         scatter(force, step, targets)
@@ -363,7 +356,7 @@
         gap = tile(near_ref, step) + side_by_side(outer_gap(2 * step), outer_gap(2 * step + 1))
         lives = [jnp.full(gap.shape, live(count_ref, 2 * step + side), jnp.float32) for side in range(2)]
         gap = gap * side_by_side(*lives)
-        force = stacked_product(gap, tile(contact_high_ref, step), tile(contact_low_ref, step))
+        force = pair_product(gap, tile(contact_high_ref, step), tile(contact_low_ref, step))
         put(image_force_ref, step, force)
         add_energy(sums, trial_rows, tile(gap_ref, step), tile(force_ref, step), gap, force)
     lane = lax.broadcasted_iota(jnp.int32, (columns, LANES), 1)

time: 34.5 us -> 34.4 us (level)
  Pallas kernels: 12.7 us -> 12 us
  waiting for transfers between devices: 4.64 us -> 5.31 us
  transfers between devices with their start and end apart: 5 -> 5, of which waited for: 3 -> 3; matrix products, arithmetic and copies ran while one was open for 0% -> 0% of each run, Pallas kernels for 22% -> 20%
where the time goes in v8:
time: 34.4 us; the launch traced here: 34.2 us
  starting transfers between devices  14.5 us (42%)
  Pallas kernels  12 us (35%)
  waiting for transfers between devices  5.31 us (15%)
  between operations  1.39 us (4%)
  local copies, waits for them, and re-layouts  0.92 us (3%)
    all_to_all x1, starting transfers between devices, shards(): lax.all_to_all(moments, ('dom', 'col'), 0, 0, tiled=True)  6.79 us
    ppermute x2, starting transfers between devices, shifted(): return lax.ppermute(value, axis, pairs)  4.96 us
    ppermute x2, waiting for transfers between devices, shifted(): return lax.ppermute(value, axis, pairs)  3.19 us
    ppermute x2, starting transfers between devices, swapped(): return lax.ppermute(value, ('dom', 'col'), pairs)  2.78 us
    pallas_call x1, Pallas kernels, shards(): call(prepare_kernel, out_shape=(wide, wide, *parts, *(shape(pair.shape, j...  2.5 us
    pallas_call x1, Pallas kernels, shards(): call(functools.partial(energy_kernel, columns=columns), out_shape=(narrow...  2.4 us
    pallas_call x1, Pallas kernels, shards(): call(couple_kernel, out_shape=(*[shape((patches + NB, rows, LANES), f32)]...  1.65 us
    pallas_call x1, Pallas kernels, shards(): call(functools.partial(lift_kernel, columns=columns), out_shape=(tail, ta...  1.62 us
  transfers between devices with their start and end apart: 5, of which 3 were waited for; matrix products, arithmetic and copies ran while one was open for 0% of the time, Pallas kernels for 20%

profile of v8, /device:TPU:0, one launch (start us, length us, event | category | flops | bytes accessed | tf_op | source)
XLA Modules:
  0.0 34.2 jit_solution(16907266011358509561)
XLA Ops:
  0.6 0.9 %slice.3 = f32[3,16,512]{2,1,0:T(8,128)S(1)} slice(f32[3,16,4096]{2,1,0:T(8,128)} %param.7), slice={[0:3], [0:16], [0:512]} | slice | bytes 196608 | tf_op jit(solution)/shard_map/slice | solution.py:538
  1.5 1.3 %collective-permute-start = (f32[3,16,512]{2,1,0:T(8,128)S(1)}, f32[3,16,512]{2,1,0:T(8,128)S(1)}, u32[]{:S(2)}, u32[]{:S(2)}) collective-permute-start(f32[3,16,512]{2,1,0:T(8,128)S(1)} %slice.3), channel_id=1, source_target_pairs={{4,0},{8,4},{12,8},{16,12},{20,16},{24,20},{28,24},{5,1},{9,5},{13... | collective-permute-start | bytes 294920 | tf_op jit(solution)/shard_map/ppermute | solution.py:25
  3.5 2.5 %prepare.1 = (f32[48,4096]{1,0:T(8,128)S(1)}, f32[48,4096]{1,0:T(8,128)S(1)}, bf16[64,4096]{1,0:T(8,128)(2,1)S(1)}, bf16[64,4096]{1,0:T(8,128)(2,1)S(1)}, bf16[6...) custom-call(f32[48,4096]{1,0:T(8,128)} %bitcast.10, ...), custom_call_target="tpu_custom_call" | custom-call | tf_op jit(solution)/shard_map/prepare/pallas_call | solution.py:539
  6.0 0.0 copy-start
  6.0 3.2 %collective-permute-done = f32[3,16,512]{2,1,0:T(8,128)S(1)} collective-permute-done((f32[3,16,512]{2,1,0:T(8,128)S(1)}, f32[3,16,512]{2,1,0:T(8,128)S(1)}, u32[]{:S(2)}, u32[]{:S(2)}) %collective-permute-start) | collective-permute-done | bytes 98336 | tf_op jit(solution)/shard_map/ppermute | solution.py:25
  9.2 1.6 %couple.1 = (f32[72,48,128]{2,1,0:T(8,128)S(1)}, f32[72,48,128]{2,1,0:T(8,128)S(1)}, f32[48,4096]{1,0:T(8,128)S(1)}, f32[48,4096]{1,0:T(8,128)S(1)}, f32[48,512]...) custom-call(s32[1]{0:T(128)S(6)} %copy.14.count_ref, ...), custom_call_target="tpu_custom_call" | custom-call | tf_op jit(solution)/shard_map/couple/pallas_call | solution.py:553
  10.8 2.8 %collective-permute-start.1 = (f32[48,512]{1,0:T(8,128)S(1)}, f32[48,512]{1,0:T(8,128)S(1)}, u32[]{:S(2)}, u32[]{:S(2)}) collective-permute-start(f32[48,512]{1,0:T(8,128)S(1)} %get-tuple-element.43), channel_id=1, source_target_pairs={{0,4},{1,5},{2,6},{3,7},{4,0},{5,1},{6,2},{7,3},{8,12},{9,13},{10,... | collective-permute-start | bytes 294920 | tf_op jit(solution)/shard_map/ppermute | solution.py:39
  13.6 0.0 collective-permute-start.2
  13.6 0.0 copy-done
  13.6 1.6 %lift.1 = (f32[48,3584]{1,0:T(8,128)S(1)}, f32[48,3584]{1,0:T(8,128)S(1)}, f32[48,4096]{1,0:T(8,128)S(1)}, f32[160,128]{1,0:T(8,128)S(1)}, f32[16,128]{1,0:T(8,128)S(1)}) custom-call(s32[64]{0:T(128)S(1)} %get-tuple-element.33.local_vmem, s32[64]{0:T(128)S(1)} %get-tuple-element.34.partner_vmem, f32[48,4096]{1,0:T(8,128)S(1)} %get-tuple-element.35.field_ref, ...), custom_call_target="tpu_custom_call" | custom-call | tf_op jit(solution)/shard_map/lift/pallas_call | solution.py:564
  15.2 0.0 copy-start.1
  15.3 1.0 %collective-permute-done.1.even_ref = f32[48,512]{1,0:T(8,128)S(1)} collective-permute-done((f32[48,512]{1,0:T(8,128)S(1)}, f32[48,512]{1,0:T(8,128)S(1)}, u32[]{:S(2)}, u32[]{:S(2)}) %collective-permute-start.1) | collective-permute-done | bytes 98336 | tf_op jit(solution)/shard_map/ppermute | solution.py:39
  16.2 0.0 collective-permute-done.2.odd_ref
  16.2 2.4 %energy.1 = (f32[48,512]{1,0:T(8,128)S(1)}, f32[48,512]{1,0:T(8,128)S(1)}, f32[48,4096]{1,0:T(8,128)S(1)}, f32[32,1,256]{2,1,0:T(1,128)}) custom-call(s32[1]{0:T(128)S(6)} %copy.14.count_ref, s32[64]{0:T(128)S(1)} %get-tuple-element.33.local_vmem, s32[64]{0:T(128)S(1)} %get-tuple-element.34.partner_vmem, f32[48,4096]{1,0:T(8,128)S(1)} %get-tuple-element.35.field_ref, ...), custom_call_target="tpu_custom_call" | custom-call | tf_op jit(solution)/shard_map/energy/pallas_call | solution.py:572
  18.6 0.0 copy-done.1
  18.6 6.8 %all-to-all-start = ((f32[32,1,256]{2,1,0:T(1,128)}), f32[32,1,256]{2,1,0:T(1,128)S(1)}, u32[]{:S(2)}, u32[]{:S(2)}) async-start(f32[32,1,256]{2,1,0:T(1,128)} %get-tuple-element.52), calls=%async_computation | async-start | bytes 65536 | tf_op jit(solution)/shard_map/all_to_all | solution.py:583
  25.4 0.0 copy-start.2
  25.4 0.9 %settle.1 = f32[48,512]{1,0:T(8,128)S(1)} custom-call(s32[64]{0:T(128)S(1)} %get-tuple-element.33.local_vmem, s32[64]{0:T(128)S(1)} %get-tuple-element.34.partner_vmem, f32[48,4096]{1,0:T(8,128)S(1)} %get-tuple-element.57.force_ref), custom_call_target="tpu_custom_call" | custom-call | flops 1000000000 | bytes 786432 | tf_op jit(solution)/shard_map/settle/pallas_call | solution.py:584
  26.4 3.7 %collective-permute-start.3 = (f32[48,512]{1,0:T(8,128)S(1)}, f32[48,512]{1,0:T(8,128)S(1)}, u32[]{:S(2)}, u32[]{:S(2)}) collective-permute-start(f32[48,512]{1,0:T(8,128)S(1)} %settle.1), channel_id=1, source_target_pairs={{0,4},{4,8},{8,12},{12,16},{16,20},{20,24},{24,28},{1,5},{5,9},{9,... | collective-permute-start | bytes 294920 | tf_op jit(solution)/shard_map/ppermute | solution.py:25
  30.1 0.0 copy-done.2
  30.1 1.5 %gather.1.twice_ref = f32[48,4096]{1,0:T(8,128)S(1)} custom-call(s32[64]{0:T(128)S(1)} %get-tuple-element.33.local_vmem, s32[64]{0:T(128)S(1)} %get-tuple-element.34.partner_vmem, f32[48,4096]{1,0:T(8,128)S(1)} %get-tuple-element.57.force_ref, f32[48,512]{1,0:T(8,128)S(1)} %get-tuple-element.58.lead_elastic_ref, f32[48,3584]{1,0:T(8,128)S(1)} %copy-done.2), custom_call_target="tpu_custom_call" | custom-call | flops 1000000000 | bytes 2359296 | tf_op jit(solution)/shard_map/gather/pallas_call | solution.py:594
  31.5 1.2 %all-to-all-done = f32[32,1,256]{2,1,0:T(1,128)S(1)} async-done(((f32[32,1,256]{2,1,0:T(1,128)}), f32[32,1,256]{2,1,0:T(1,128)S(1)}, u32[]{:S(2)}, u32[]{:S(2)}) %all-to-all-start) | async-done | bytes 32800 | tf_op jit(solution)/shard_map/all_to_all | solution.py:583
  32.7 0.2 scale.1
  32.9 0.0 collective-permute-done.3.far_received_ref
  32.9 1.3 %last.1 = (f32[48,4096]{1,0:T(8,128)}, f32[48,4096]{1,0:T(8,128)}, f32[1,16]{1,0:T(1,128)}) custom-call(f32[32,128]{1,0:T(8,128)S(1)} %get-tuple-element.53.scale_ref, f32[8,128]{1,0:T(8,128)S(1)} %get-tuple-element.54.gradient_ref, f32[48,4096]{1,0:T(8,128)S(1)} %get-tuple-element.35.field_ref, f32[48,3584]{1,0:T(8,128)S(1)} %get-tuple-element.55.image_ref, ...), custom_call_target="tpu_custom_call" | custom-call | tf_op jit(solution)/shard_map/last/pallas_call | solution.py:611
  (1 shorter events, 0.0 us)
Async XLA Ops:
  1.5 7.6 %collective-permute-start = (f32[3,16,512]{2,1,0:T(8,128)S(1)}, f32[3,16,512]{2,1,0:T(8,128)S(1)}, u32[]{:S(2)}, u32[]{:S(2)}) collective-permute-start(f32[3,16,512]{2,1,0:T(8,128)S(1)} %slice.3), channel_id=1, source_target_pairs={{4,0},{8,4},{12,8},{16,12},{20,16},{24,20},{28,24},{5,1},{9,5},{13... | collective-permute-start | bytes 294920 | tf_op jit(solution)/shard_map/ppermute | solution.py:25
  6.0 7.6 %copy-start = (f32[3,4096]{1,0:T(4,128)S(1)}, f32[3,4096]{1,0:T(4,128)}, u32[]{:S(2)}) copy-start(f32[3,4096]{1,0:T(4,128)} %weight_ref.3) | copy-start | bytes 147460
  10.8 5.4 %collective-permute-start.1 = (f32[48,512]{1,0:T(8,128)S(1)}, f32[48,512]{1,0:T(8,128)S(1)}, u32[]{:S(2)}, u32[]{:S(2)}) collective-permute-start(f32[48,512]{1,0:T(8,128)S(1)} %get-tuple-element.43), channel_id=1, source_target_pairs={{0,4},{1,5},{2,6},{3,7},{4,0},{5,1},{6,2},{7,3},{8,12},{9,13},{10,... | collective-permute-start | bytes 294920 | tf_op jit(solution)/shard_map/ppermute | solution.py:39
  13.6 2.6 %collective-permute-start.2 = (f32[48,512]{1,0:T(8,128)S(1)}, f32[48,512]{1,0:T(8,128)S(1)}, u32[]{:S(2)}, u32[]{:S(2)}) collective-permute-start(f32[48,512]{1,0:T(8,128)S(1)} %get-tuple-element.44), channel_id=1, source_target_pairs={{0,1},{1,0},{2,3},{3,2},{4,8},{5,9},{6,10},{7,11},{8,4},{9,5},{10,... | collective-permute-start | bytes 294920 | tf_op jit(solution)/shard_map/ppermute | solution.py:39
  15.2 3.4 %copy-start.1 = (f32[48,3584]{1,0:T(8,128)}, f32[48,3584]{1,0:T(8,128)S(1)}, u32[]{:S(2)}) copy-start(f32[48,3584]{1,0:T(8,128)S(1)} %get-tuple-element.59.elastic_ref) | copy-start | bytes 2064388
  18.6 14.1 %all-to-all-start = ((f32[32,1,256]{2,1,0:T(1,128)}), f32[32,1,256]{2,1,0:T(1,128)S(1)}, u32[]{:S(2)}, u32[]{:S(2)}) async-start(f32[32,1,256]{2,1,0:T(1,128)} %get-tuple-element.52), calls=%async_computation | async-start | bytes 65536 | tf_op jit(solution)/shard_map/all_to_all | solution.py:583
  25.4 4.6 %copy-start.2 = (f32[48,3584]{1,0:T(8,128)S(1)}, f32[48,3584]{1,0:T(8,128)}, u32[]{:S(2)}) copy-start(f32[48,3584]{1,0:T(8,128)} %copy-done.1) | copy-start | bytes 2064388
  26.4 6.5 %collective-permute-start.3 = (f32[48,512]{1,0:T(8,128)S(1)}, f32[48,512]{1,0:T(8,128)S(1)}, u32[]{:S(2)}, u32[]{:S(2)}) collective-permute-start(f32[48,512]{1,0:T(8,128)S(1)} %settle.1), channel_id=1, source_target_pairs={{0,4},{4,8},{8,12},{12,16},{16,20},{20,24},{24,28},{1,5},{5,9},{9,... | collective-permute-start | bytes 294920 | tf_op jit(solution)/shard_map/ppermute | solution.py:25
